TPU v7x, 32 devices: a whole 2x2x4 slice. The times are simulated.
32 devices in a mesh: tile: 8 (over z, x), row: 4 (over y, core).
Axes of the slice: x: 2, y: 2, z: 4, core: 2. Of those that a mesh axis runs over, the one named last changes fastest.
Arguments:
- point_feats: bfloat16 [11, 262144], P(None, ('tile', 'row')), may hold values from -6 to 6
- point_tile: int32 [262144, 1], P(('tile', 'row')), may hold values from 0 to 7; in each aligned block of 8192 rows (0 to 8191, 8192 to 16383, ...) at most 2048 rows name the same one
- point_cell: int32 [262144], P(('tile', 'row')), may hold values from 0 to 4607
- point_valid: int32 [262144], P(('tile', 'row')), may hold values 0 or 1
- pillar_frame: int32 [192, 768], P('tile', 'row'), may hold values from 0 to 2
- cotangent: bfloat16 [192, 768, 128], P('tile', 'row'), may hold values from -6 to 6
- params: float32 [273792], replicated, as said below
- first_moment: float32 [273792], replicated, as said below
- second_moment: float32 [273792], replicated, as said below
Outputs:
- grad_norm: float32 [], replicated
- new_params: float32 [273792], replicated
- new_first_moment: float32 [273792], replicated
- new_second_moment: float32 [273792], replicated
- params_bf16: bfloat16 [273792], replicated
- sublayer_rms: float32 [6], replicated
Inputs may be any that keep to these rules, and one draw needn't show every extreme that they name: `point_tile`: in the 8192 rows of one device no tile is named by more than 2048 rows, a bound that some block reaches. `params`: matrices of order one over the square root of their fan-in, norm gains near 1, other vectors of order a few tenths. `first_moment`: entries of both signs. `second_moment`: every entry is positive.
All inputs are finite; a program needn't handle non-finite values. No bound on the sum of `point_valid` on one device may be relied on, other than what follows from the above.
Results may differ from a plain program's by a relative error of at most 0.0075.
The roundings to bfloat16 on the way count: a program that leaves them out, or rounds other values in their place, can miss the bound.
Values may be sent and summed in bfloat16 or wider, within the bound.
No kernel may reach another device: no remote copies, remote signals or barrier semaphores. Data moves between devices by JAX's collectives and lax.ppermute only.
A program may use at most 320 MiB of HBM per device.

v0:
```python
import math

import jax
import jax.numpy as jnp
from jax import lax
from jax.sharding import PartitionSpec as P

D = 128
HEADS = 8
HD = 16
FF = 256
H1 = 64
WIN = 12
C_IN = 11
LAYERS = 2


clip_norm = 0.01
beta_one = 0.9
beta_two = 0.999
step_count = 10
learn_rate = 0.1
decay_rate = 0.05
adam_eps = 1e-08


def passed_along(x, axis, by):
    count = lax.axis_size(axis)
    return lax.ppermute(x, axis, [(i, (i + by) % count) for i in range(count)])


def shortened(x):
    return jax.tree.map(lambda a: a.astype(jnp.bfloat16) if a.dtype == jnp.float32 else a, x)


def layout():
    entries = [
        ("point_in_weight", (C_IN, H1)),
        ("point_in_bias", (H1,)),
        ("point_out_weight", (H1, D)),
        ("point_out_bias", (D,)),
    ]
    for layer_idx in range(LAYERS):
        entries = entries + [
            ("qkv_weight", (D, 3 * D)),
            ("out_weight", (D, D)),
            ("ffn_in_weight", (D, FF)),
            ("ffn_out_weight", (FF, D)),
            ("query_bias", (D,)),
            ("value_bias", (D,)),
            ("out_bias", (D,)),
            ("norm1_gain", (D,)),
            ("norm1_bias", (D,)),
            ("ffn_in_bias", (FF,)),
            ("ffn_out_bias", (D,)),
            ("norm2_gain", (D,)),
            ("norm2_bias", (D,)),
        ]
    return entries


def unpack(flat_vec):
    pieces = []
    offset = 0
    for entry_name, extents in layout():
        length = math.prod(extents)
        pieces.append(flat_vec[offset : offset + length].reshape(extents))
        offset = offset + length
    return pieces


def flatten(arrays):
    return jnp.concatenate([piece.reshape(-1) for piece in arrays])


def layer_norm(values, gain, shift_bias):
    center = values - jnp.mean(values, axis=-1, keepdims=True)
    spread = jnp.mean(center * center, axis=-1, keepdims=True)
    return center * lax.rsqrt(spread + 1e-05) * gain + shift_bias


def to_windows(grid):
    across = grid.shape[0] // WIN
    along = grid.shape[1] // WIN
    trailing = grid.shape[2:]
    parted = grid.reshape((across, WIN, along, WIN) + trailing)
    parted = jnp.swapaxes(parted, 1, 2)
    return parted.reshape((across * along, WIN * WIN) + trailing)


def from_windows(parted, extent_x, extent_y):
    across = extent_x // WIN
    along = extent_y // WIN
    trailing = parted.shape[2:]
    grid = parted.reshape((across, along, WIN, WIN) + trailing)
    grid = jnp.swapaxes(grid, 1, 2)
    return grid.reshape((extent_x, extent_y) + trailing)


def attention_mask(win_tags, win_regions):
    slot_count = win_tags.shape[1]
    same_group = (
        (win_tags[:, :, None] == win_tags[:, None, :])
        & (win_tags[:, None, :] > 0)
        & (win_regions[:, :, None] == win_regions[:, None, :])
    )
    return same_group | jnp.eye(slot_count, dtype=bool)[None]


def attention_scores(packed, allowed):
    scores = jnp.einsum(
        "wqhd,wkhd->whqk", packed[:, :, 0], packed[:, :, 1], preferred_element_type=jnp.float32
    ) * HD ** (-0.5)
    return jnp.where(allowed[:, None], scores, -1000000000.0)


def layer_forward(grid_field, cell_tags, regions, weights):
    (
        qkv_weight,
        out_weight,
        ffn_in_weight,
        ffn_out_weight,
        query_bias,
        value_bias,
        out_bias,
        norm1_gain,
        norm1_bias,
        ffn_in_bias,
        ffn_out_bias,
        norm2_gain,
        norm2_bias,
    ) = weights
    windows = to_windows(grid_field)
    win_tags = to_windows(cell_tags)
    win_count = windows.shape[0]
    slot_count = windows.shape[1]
    live_mask = (win_tags > 0).astype(jnp.float32)[..., None]
    allowed = attention_mask(win_tags, to_windows(regions))
    inputs = windows.astype(jnp.bfloat16)
    qkv_bias = jnp.concatenate([query_bias, jnp.zeros_like(query_bias), value_bias])
    packed = (
        jnp.einsum("wsd,de->wse", inputs, qkv_weight, preferred_element_type=jnp.float32) + qkv_bias
    )
    packed = packed.astype(jnp.bfloat16).reshape(win_count, slot_count, 3, HEADS, HD)
    scores = attention_scores(packed, allowed)
    top_score = jnp.max(scores, axis=-1, keepdims=True)
    exponent = jnp.exp(scores - top_score)
    row_total = jnp.sum(exponent, axis=-1, keepdims=True)
    log_total = top_score + jnp.log(row_total)
    attn_low = (exponent / row_total).astype(jnp.bfloat16)
    mixture = jnp.einsum(
        "whqk,wkhd->wqhd", attn_low, packed[:, :, 2], preferred_element_type=jnp.float32
    )
    mixture = mixture.reshape(win_count, slot_count, D).astype(jnp.bfloat16)
    attn_out = (
        jnp.einsum("wsd,de->wse", mixture, out_weight, preferred_element_type=jnp.float32)
        + out_bias
    )
    first_sum = windows + attn_out
    normed = layer_norm(first_sum, norm1_gain, norm1_bias) * live_mask
    normed_low = normed.astype(jnp.bfloat16)
    pre_act = (
        jnp.einsum("wsd,df->wsf", normed_low, ffn_in_weight, preferred_element_type=jnp.float32)
        + ffn_in_bias
    )
    hidden = jax.nn.gelu(pre_act).astype(jnp.bfloat16)
    ffn_result = (
        jnp.einsum("wsf,fd->wsd", hidden, ffn_out_weight, preferred_element_type=jnp.float32)
        + ffn_out_bias
    )
    second_sum = normed + ffn_result
    layer_out = layer_norm(second_sum, norm2_gain, norm2_bias) * live_mask
    square_sums = jnp.stack(
        [
            jnp.sum(attn_out * attn_out * live_mask),
            jnp.sum(ffn_result * ffn_result * live_mask),
            jnp.sum(layer_out * layer_out),
        ]
    )
    kept = (
        inputs,
        packed,
        allowed,
        log_total,
        mixture,
        first_sum,
        normed_low,
        pre_act,
        hidden,
        second_sum,
        live_mask,
    )
    return (from_windows(layer_out, grid_field.shape[0], grid_field.shape[1]), kept, square_sums)


def layer_backward(grad_grid, kept, weights):
    (
        qkv_weight,
        out_weight,
        ffn_in_weight,
        ffn_out_weight,
        query_bias,
        value_bias,
        out_bias,
        norm1_gain,
        norm1_bias,
        ffn_in_bias,
        ffn_out_bias,
        norm2_gain,
        norm2_bias,
    ) = weights
    (
        inputs,
        packed,
        allowed,
        log_total,
        mixture,
        first_sum,
        normed_low,
        pre_act,
        hidden,
        second_sum,
        live_mask,
    ) = kept
    win_count = inputs.shape[0]
    slot_count = inputs.shape[1]
    grad_layer = to_windows(grad_grid) * live_mask
    norm_pull = jax.vjp(layer_norm, second_sum, norm2_gain, norm2_bias)[1]
    grad_second, grad_gain2, grad_bias2 = norm_pull(grad_layer)
    grad_ffn = grad_second.astype(jnp.bfloat16)
    grad_ffn_out = jnp.einsum("wsf,wsd->fd", hidden, grad_ffn, preferred_element_type=jnp.float32)
    grad_ffn_bias2 = jnp.sum(grad_ffn.astype(jnp.float32), axis=(0, 1))
    grad_hidden = jnp.einsum(
        "wsd,fd->wsf", grad_ffn, ffn_out_weight, preferred_element_type=jnp.float32
    )
    gelu_pull = jax.vjp(jax.nn.gelu, pre_act)[1]
    grad_pre = gelu_pull(grad_hidden)[0].astype(jnp.bfloat16)
    grad_ffn_in = jnp.einsum(
        "wsd,wsf->df", normed_low, grad_pre, preferred_element_type=jnp.float32
    )
    grad_ffn_bias1 = jnp.sum(grad_pre.astype(jnp.float32), axis=(0, 1))
    grad_normed = (
        grad_second
        + jnp.einsum("wsf,df->wsd", grad_pre, ffn_in_weight, preferred_element_type=jnp.float32)
    ) * live_mask
    norm_pull = jax.vjp(layer_norm, first_sum, norm1_gain, norm1_bias)[1]
    grad_first, grad_gain1, grad_bias1 = norm_pull(grad_normed)
    grad_attn = grad_first.astype(jnp.bfloat16)
    grad_out_weight = jnp.einsum(
        "wsd,wse->de", mixture, grad_attn, preferred_element_type=jnp.float32
    )
    grad_out_bias = jnp.sum(grad_attn.astype(jnp.float32), axis=(0, 1))
    grad_mix = jnp.einsum("wse,de->wsd", grad_attn, out_weight, preferred_element_type=jnp.float32)
    grad_mix = grad_mix.astype(jnp.bfloat16).reshape(win_count, slot_count, HEADS, HD)
    attn_probs = jnp.exp(attention_scores(packed, allowed) - log_total)
    grad_vals = jnp.einsum(
        "whqk,wqhd->wkhd",
        attn_probs.astype(jnp.bfloat16),
        grad_mix,
        preferred_element_type=jnp.float32,
    )
    grad_probs = jnp.einsum(
        "wqhd,wkhd->whqk", grad_mix, packed[:, :, 2], preferred_element_type=jnp.float32
    )
    grad_scores = attn_probs * (
        grad_probs - jnp.sum(grad_probs * attn_probs, axis=-1, keepdims=True)
    )
    grad_scores = grad_scores.astype(jnp.bfloat16)
    grad_query = jnp.einsum(
        "whqk,wkhd->wqhd", grad_scores, packed[:, :, 1], preferred_element_type=jnp.float32
    ) * HD ** (-0.5)
    grad_keys = jnp.einsum(
        "whqk,wqhd->wkhd", grad_scores, packed[:, :, 0], preferred_element_type=jnp.float32
    ) * HD ** (-0.5)
    grad_packed = (
        jnp.stack([grad_query, grad_keys, grad_vals], axis=2)
        .reshape(win_count, slot_count, 3 * D)
        .astype(jnp.bfloat16)
    )
    grad_qkv = jnp.einsum("wsd,wse->de", inputs, grad_packed, preferred_element_type=jnp.float32)
    packed_sums = jnp.sum(grad_packed.astype(jnp.float32), axis=(0, 1))
    grad_inputs = grad_first + jnp.einsum(
        "wse,de->wsd", grad_packed, qkv_weight, preferred_element_type=jnp.float32
    )
    layer_grads = [
        grad_qkv,
        grad_out_weight,
        grad_ffn_in,
        grad_ffn_out,
        packed_sums[:D],
        packed_sums[2 * D :],
        grad_out_bias,
        grad_gain1,
        grad_bias1,
        grad_ffn_bias1,
        grad_ffn_bias2,
        grad_gain2,
        grad_bias2,
    ]
    return (from_windows(grad_inputs, grad_grid.shape[0], grad_grid.shape[1]), layer_grads)


def point_forward(feature_cols, point_in_weight, point_in_bias, point_out_weight, point_out_bias):
    pre_act = (
        jnp.einsum("cp,ch->ph", feature_cols, point_in_weight, preferred_element_type=jnp.float32)
        + point_in_bias
    )
    activity = jax.nn.gelu(pre_act).astype(jnp.bfloat16)
    point_out = (
        jnp.einsum("ph,hd->pd", activity, point_out_weight, preferred_element_type=jnp.float32)
        + point_out_bias
    )
    return (pre_act, activity, point_out.astype(jnp.bfloat16))


def point_backward(feature_cols, pre_act, activity, grad_point, point_out_weight):
    grad_out_weight = jnp.einsum(
        "ph,pd->hd", activity, grad_point, preferred_element_type=jnp.float32
    )
    grad_out_bias = jnp.sum(grad_point.astype(jnp.float32), axis=0)
    grad_activity = jnp.einsum(
        "pd,hd->ph", grad_point, point_out_weight, preferred_element_type=jnp.float32
    )
    gelu_pull = jax.vjp(jax.nn.gelu, pre_act)[1]
    grad_pre = gelu_pull(grad_activity)[0].astype(jnp.bfloat16)
    grad_in_weight = jnp.einsum(
        "cp,ph->ch", feature_cols, grad_pre, preferred_element_type=jnp.float32
    )
    grad_in_bias = jnp.sum(grad_pre.astype(jnp.float32), axis=0)
    return [grad_in_weight, grad_in_bias, grad_out_weight, grad_out_bias]


def roll_forward(grid_field, cell_tags, cotan_field, half_win):
    moved = passed_along(
        (grid_field[:half_win], cell_tags[:half_win], cotan_field[:half_win]), "tile", -1
    )
    grid_field = jnp.concatenate([grid_field[half_win:], moved[0]], axis=0)
    cell_tags = jnp.concatenate([cell_tags[half_win:], moved[1]], axis=0)
    cotan_field = jnp.concatenate([cotan_field[half_win:], moved[2]], axis=0)
    moved = (
        passed_along(grid_field[:, :half_win].astype(jnp.bfloat16), "row", -1).astype(jnp.float32),
        passed_along(cell_tags[:, :half_win].astype(jnp.bfloat16), "row", -1).astype(jnp.float32),
        passed_along(cotan_field[:, :half_win].astype(jnp.bfloat16), "row", -1).astype(jnp.float32),
    )
    grid_field = jnp.concatenate([grid_field[:, half_win:], moved[0]], axis=1)
    cell_tags = jnp.concatenate([cell_tags[:, half_win:], moved[1]], axis=1)
    cotan_field = jnp.concatenate([cotan_field[:, half_win:], moved[2]], axis=1)
    return (grid_field, cell_tags, cotan_field)


def roll_back(grad_field, half_win):
    moved = passed_along(shortened(grad_field[-half_win:]), "tile", 1)
    grad_field = jnp.concatenate([moved, grad_field[:-half_win]], axis=0)
    moved = passed_along(shortened(grad_field[:, -half_win:]), "row", 1)
    return jnp.concatenate([moved, grad_field[:, :-half_win]], axis=1)


def local(
    point_feats,
    point_tile,
    point_cell,
    point_valid,
    pillar_frame,
    cotangent,
    params,
    first_moment,
    second_moment,
):
    tile_count = lax.axis_size("tile")
    device_count = tile_count * lax.axis_size("row")
    extent_x, extent_y = pillar_frame.shape
    cell_count = extent_x * extent_y
    half_win = WIN // 2
    capacity = 2 * point_cell.shape[0] // tile_count
    pieces = unpack(params)
    lowered = [piece.astype(jnp.bfloat16) if piece.ndim == 2 else piece for piece in pieces]
    point_in_weight, point_in_bias, point_out_weight, point_out_bias = lowered[:4]
    first_layer = lowered[4:17]
    second_layer = lowered[17:30]
    target = point_tile[:, 0]
    choose = (target[:, None] == jnp.arange(tile_count, dtype=jnp.int32)[None, :]).astype(jnp.int32)
    position = jnp.sum((jnp.cumsum(choose, axis=0) - choose) * choose, axis=1)
    slot_index = target * capacity + position
    live_point = point_valid > 0
    send_cells = (
        jnp.full((tile_count * capacity,), -1, jnp.int32)
        .at[slot_index]
        .set(jnp.where(live_point, point_cell, -1))
    )
    recv_cells = lax.all_to_all(
        send_cells.reshape(tile_count, capacity), "tile", split_axis=0, concat_axis=0, tiled=True
    ).reshape(-1)
    slot_live = recv_cells >= 0
    safe_cells = jnp.where(slot_live, recv_cells, cell_count)
    counts = jax.ops.segment_sum(
        slot_live.astype(jnp.float32), safe_cells, num_segments=cell_count + 1
    )[:cell_count]
    divisor = jnp.maximum(counts, 1.0)[:, None]
    live_cells = (counts > 0).reshape(extent_x, extent_y)
    cell_tags = jnp.where(live_cells, pillar_frame + 1, 0).astype(jnp.float32)
    pre_act, activity, point_out = point_forward(
        point_feats, point_in_weight, point_in_bias, point_out_weight, point_out_bias
    )
    send_out = jnp.zeros((tile_count * capacity, D), jnp.bfloat16).at[slot_index].set(point_out)
    slot_out = lax.all_to_all(
        send_out.reshape(tile_count, capacity, D), "tile", split_axis=0, concat_axis=0, tiled=True
    ).reshape(-1, D)
    pillar_sum = jax.ops.segment_sum(
        slot_out.astype(jnp.float32), safe_cells, num_segments=cell_count + 1
    )[:cell_count]
    field_zero = (pillar_sum / divisor).reshape(extent_x, extent_y, D)
    zero_regions = jnp.zeros((extent_x, extent_y), jnp.int32)
    field_one, kept_one, sums_one = layer_forward(field_zero, cell_tags, zero_regions, first_layer)
    rolled_field, rolled_tags, rolled_cot = roll_forward(
        field_one, cell_tags, cotangent.astype(jnp.float32), half_win
    )
    last_x = (lax.axis_index("tile") == tile_count - 1) & (
        jnp.arange(extent_x) >= extent_x - half_win
    )
    last_y = (lax.axis_index("row") == lax.axis_size("row") - 1) & (
        jnp.arange(extent_y) >= extent_y - half_win
    )
    regions = last_x.astype(jnp.int32)[:, None] * 2 + last_y.astype(jnp.int32)[None, :]
    field_two, kept_two, sums_two = layer_forward(rolled_field, rolled_tags, regions, second_layer)
    grad_mid, grads_two = layer_backward(
        rolled_cot / (cell_count * device_count), kept_two, second_layer
    )
    flat_two = flatten(grads_two)
    grad_one_grid = roll_back(grad_mid, half_win)
    grad_zero, grads_one = layer_backward(grad_one_grid, kept_one, first_layer)
    grad_pillar = (grad_zero.reshape(cell_count, D) / divisor).astype(jnp.bfloat16)
    grad_table = jnp.concatenate([grad_pillar, jnp.zeros((1, D), jnp.bfloat16)], axis=0)
    slot_grads = grad_table[safe_cells]
    returned = lax.all_to_all(
        slot_grads.reshape(tile_count, capacity, D), "tile", split_axis=0, concat_axis=0, tiled=True
    ).reshape(-1, D)
    grad_point = jnp.where(live_point[:, None], returned[slot_index], jnp.zeros((), jnp.bfloat16))
    point_grads = point_backward(point_feats, pre_act, activity, grad_point, point_out_weight)
    flat_rest = flatten(point_grads + grads_one)
    square_sums = jnp.concatenate([sums_one, sums_two])
    live_total = jnp.sum(live_cells.astype(jnp.float32))
    flat_rest, flat_two, square_sums, live_total = lax.psum(
        (flat_rest, flat_two, square_sums, live_total), ("tile", "row")
    )
    gradient = jnp.concatenate([flat_rest, flat_two])
    grad_norm = jnp.sqrt(jnp.sum(gradient * gradient))
    clipped = gradient * jnp.minimum(1.0, clip_norm / (grad_norm + 1e-06))
    new_first = beta_one * first_moment + (1.0 - beta_one) * clipped
    new_second = beta_two * second_moment + (1.0 - beta_two) * clipped * clipped
    first_hat = new_first / (1.0 - beta_one**step_count)
    second_hat = new_second / (1.0 - beta_two**step_count)
    new_params = params - learn_rate * (
        first_hat / (jnp.sqrt(second_hat) + adam_eps) + decay_rate * params
    )
    sublayer_rms = jnp.sqrt(square_sums / (jnp.maximum(live_total, 1.0) * D))
    return (
        grad_norm,
        new_params,
        new_first,
        new_second,
        new_params.astype(jnp.bfloat16),
        sublayer_rms,
    )


def solution(mesh):
    return jax.shard_map(
        local,
        mesh=mesh,
        in_specs=(
            P(None, ("tile", "row")),
            P(("tile", "row"), None),
            P(("tile", "row")),
            P(("tile", "row")),
            P("tile", "row"),
            P("tile", "row", None),
            P(),
            P(),
            P(),
        ),
        out_specs=(P(), P(), P(), P(), P(), P()),
        check_vma=False,
    )
```

profile of v0, /device:TPU:0, one launch (start us, length us, event | category | flops | bytes accessed | tf_op | source)
XLA Modules:
  0.0 1179.0 jit_solution(17677191722824290081)
XLA Ops:
  14.4 31.0 %scatter_custom_fusion = s32[16384]{0:T(1024)} fusion(s32[8192]{0:T(1024)S(1)} %bitcast.342, s32[8192]{0:T(1024)S(1)} %get-tuple-element.70, s32[]{:T(128)} %constant.45.clone.1), kind=kCustom, calls=%fused_computation.224 | custom fusion | bytes 65540 | tf_op jit(solution)/shard_map/scatter | solution.py:388
  45.5 7.3 all-to-all-start
  64.4 23.9 %scatter_custom_fusion.2 = bf16[16384,128]{1,0:T(8,128)(2,1)} fusion(s32[8192]{0:T(1024)S(1)} %bitcast.343, bf16[8192,128]{1,0:T(8,128)(2,1)} %fusion.12, bf16[]{:T(256)} %constant.50.clone.1), kind=kCustom, calls=%fused_computation.151 | custom fusion | bytes 4194816 | tf_op jit(solution)/shard_map/scatter | solution.py:404
  95.1 101.6 %scatter_custom_fusion.1 = f32[4609]{0:T(1024)S(1)} fusion(s32[16384]{0:T(1024)S(1)} %bitcast.345, f32[16384]{0:T(1024)S(1)} %bitcast.347, f32[]{:T(128)} %constant.44.clone.1), kind=kCustom, calls=%fused_computation.251 | custom fusion | flops 16384 | bytes 18440 | tf_op jit(solution)/shard_map/scatter-add | solution.py:395
  210.9 103.5 %scatter_custom_fusion.3 = f32[4609,128]{1,0:T(8,128)S(1)} fusion(s32[16384]{0:T(1024)S(1)} %bitcast.346, bf16[16384,128]{1,0:T(8,128)(2,1)} %bitcast.97, f32[]{:T(128)} %constant.44.clone.1), kind=kCustom, calls=%fused_computation.35 | custom fusion | flops 4194304 | bytes 6554116 | tf_op jit(solution)/shard_map/scatter-add | solution.py:408
  326.1 7.3 copy.112
  333.4 17.3 %fusion.116 = (f32[32,8,144]{2,1,0:T(8,128)S(1)}, f32[32,8,144,144]{2,3,1,0:T(8,128)}) fusion(bf16[32,144,3,8,16]{1,4,3,2,0:T(8,128)(2,1)} %bitcast.286, pred[32,144,144]{1,2,0:T(8,128)(4,1)S(1)} %copy-done.26), kind=kOutput, calls=%fused_computation.296 | convolution fusion | flops 185757696 | bytes 26238976 | tf_op jit(solution)/shard_map/wqhd,wkhd->whqk/dot_general | solution.py:111
  350.7 19.0 %fusion = f32[32,8,144]{2,1,0:T(8,128)S(1)} fusion(f32[32,8,144,144]{2,3,1,0:T(8,128)} %get-tuple-element.107, f32[32,8,144]{2,1,0:T(8,128)S(1)} %get-tuple-element.106), kind=kLoop, calls=%fused_computation.18 | loop fusion | flops 10579968 | bytes 21528576 | tf_op jit(solution)/shard_map/reduce_sum | solution.py:148
  369.7 17.5 %fusion.48 = bf16[32,8,16,144]{3,2,1,0:T(8,128)(2,1)} fusion(f32[32,8,144,144]{2,3,1,0:T(8,128)} %get-tuple-element.107, f32[32,8,144]{2,1,0:T(8,128)S(1)} %fusion, f32[32,8,144]{2,1,0:T(8,128)S(1)} %get-tuple-element.106, bf16[32,144,3,8,16]{1,4,3,2,0:T(8,128)(2,1)} %bitcast.287), kind=kOutput, calls=%fused_computation.155 | convolution fusion | flops 186384384 | bytes 41320448 | tf_op jit(solution)/shard_map/whqk,wkhd->wqhd/dot_general | solution.py:151
  446.4 7.2 copy.129
  453.6 17.4 %fusion.117 = (f32[32,8,144]{2,1,0:T(8,128)S(1)}, f32[32,8,144,144]{2,3,1,0:T(8,128)}) fusion(bf16[32,144,3,8,16]{1,4,3,2,0:T(8,128)(2,1)} %bitcast.293, pred[32,144,144]{1,2,0:T(8,128)(4,1)} %get-tuple-element.97), kind=kOutput, calls=%fused_computation.297 | convolution fusion | flops 185757696 | bytes 26755072 | tf_op jit(solution)/shard_map/wqhd,wkhd->whqk/dot_general | solution.py:111
  471.0 19.4 %fusion.1 = f32[32,8,144]{2,1,0:T(8,128)S(1)} fusion(f32[32,8,144,144]{2,3,1,0:T(8,128)} %get-tuple-element.113, f32[32,8,144]{2,1,0:T(8,128)S(1)} %get-tuple-element.112), kind=kLoop, calls=%fused_computation.19 | loop fusion | flops 10579968 | bytes 21528576 | tf_op jit(solution)/shard_map/reduce_sum | solution.py:148
  491.9 17.2 %fusion.47 = bf16[32,8,16,144]{3,2,1,0:T(8,128)(2,1)} fusion(f32[32,8,144,144]{2,3,1,0:T(8,128)} %get-tuple-element.113, f32[32,8,144]{2,1,0:T(8,128)} %copy-done.67, f32[32,8,144]{2,1,0:T(8,128)} %copy-done.45, bf16[32,144,3,8,16]{1,4,3,2,0:T(8,128)(2,1)} %bitcast.294), kind=kOutput, calls=%fused_computation.154 | convolution fusion | flops 186384384 | bytes 41549824 | tf_op jit(solution)/shard_map/whqk,wkhd->wqhd/dot_general | solution.py:151
  557.9 16.0 %fusion.32 = bf16[32,144,1,8,16]{1,4,3,0,2:T(8,128)(2,1)} fusion(bf16[32,144,8,16]{1,3,2,0:T(8,128)(2,1)} %bitcast.304, f32[32,8,144,144]{2,3,1,0:T(8,128)} %get-tuple-element.113, f32[32,8,144]{2,1,0:T(8,128)S(1)} %copy-done.36), kind=kOutput, calls=%fused_computation.134 | convolution fusion | flops 180486144 | bytes 23740416 | tf_op jit(solution)/shard_map/whqk,wqhd->wkhd/dot_general | solution.py:256
  573.8 24.9 %multiply_reduce_fusion.1 = (f32[32,8,144]{2,1,0:T(8,128)S(1)}, f32[32,8,144,144]{2,3,1,0:T(8,128)}) fusion(f32[32,8,144,144]{2,3,1,0:T(8,128)} %get-tuple-element.113, f32[32,8,144]{2,1,0:T(8,128)S(1)} %copy-done.36, bf16[32,144,8,16]{1,3,2,0:T(8,128)(2,1)S(1)} %bitcast.305, bf16[32,144,3,8,16]{1,4,3,2,0:T(8,128)(2,1)S(1)} %bitcast.297), kind=kOutput, calls=%fused_computation.10 | convolution fusion | flops 185757696 | bytes 47071232 | tf_op jit(solution)/shard_map/wqhd,wkhd->whqk/dot_general | solution.py:262
  598.7 33.5 %multiply_convert_fusion.1 = bf16[32,8,144,144]{2,3,1,0:T(8,128)(2,1)} fusion(f32[32,8,144,144]{2,3,1,0:T(8,128)} %get-tuple-element.120, f32[32,8,144,144]{2,3,1,0:T(8,128)} %get-tuple-element.113, f32[32,8,144]{2,1,0:T(8,128)S(1)} %get-tuple-element.119, f32[32,8,144]{2,1,0:T(8,128)S(1)} %copy-done.36), kind=kLoop, calls=%fused_computation.9 | loop fusion | flops 21233664 | bytes 53379072 | tf_op jit(solution)/shard_map/convert_element_type | solution.py:268
  632.3 9.9 multiply_bitcast_fusion.2
  642.2 9.1 multiply_bitcast_fusion.3
  665.9 8.9 collective-permute-done.6
  720.6 16.1 %fusion.35 = bf16[32,144,1,8,16]{1,4,3,0,2:T(8,128)(2,1)} fusion(bf16[32,144,8,16]{1,3,2,0:T(8,128)(2,1)} %bitcast.306, f32[32,8,144,144]{2,3,1,0:T(8,128)} %get-tuple-element.107, f32[32,8,144]{2,1,0:T(8,128)S(1)} %copy-done.37), kind=kOutput, calls=%fused_computation.135 | convolution fusion | flops 180486144 | bytes 23740416 | tf_op jit(solution)/shard_map/whqk,wqhd->wkhd/dot_general | solution.py:256
  736.7 24.7 %multiply_reduce_fusion = (f32[32,8,144]{2,1,0:T(8,128)S(1)}, f32[32,8,144,144]{2,3,1,0:T(8,128)}) fusion(f32[32,8,144,144]{2,3,1,0:T(8,128)} %get-tuple-element.107, f32[32,8,144]{2,1,0:T(8,128)S(1)} %copy-done.37, bf16[32,144,8,16]{1,3,2,0:T(8,128)(2,1)S(1)} %bitcast.307, bf16[32,144,3,8,16]{1,4,3,2,0:T(8,128)(2,1)S(1)} %bitcast.290), kind=kOutput, calls=%fused_computation.7 | convolution fusion | flops 185757696 | bytes 47071232 | tf_op jit(solution)/shard_map/wqhd,wkhd->whqk/dot_general | solution.py:262
  761.4 33.6 %multiply_convert_fusion = bf16[32,8,144,144]{2,3,1,0:T(8,128)(2,1)} fusion(f32[32,8,144,144]{2,3,1,0:T(8,128)} %get-tuple-element.123, f32[32,8,144,144]{2,3,1,0:T(8,128)} %get-tuple-element.107, f32[32,8,144]{2,1,0:T(8,128)S(1)} %get-tuple-element.122, f32[32,8,144]{2,1,0:T(8,128)S(1)} %copy-done.37), kind=kLoop, calls=%fused_computation.6 | loop fusion | flops 21233664 | bytes 53379072 | tf_op jit(solution)/shard_map/convert_element_type | solution.py:268
  795.0 9.9 multiply_bitcast_fusion
  804.9 9.1 multiply_bitcast_fusion.1
  827.2 57.8 %gather_fusion = bf16[16384,128]{1,0:T(8,128)(2,1)} fusion(bf16[4609,128]{1,0:T(8,128)(2,1)S(1)} %concatenate.55, s32[16384]{0:T(1024)S(1)} %broadcast_clamp_fusion), kind=kCustom, calls=%fused_computation | custom fusion | bytes 8454144 | tf_op jit(solution)/shard_map/gather | solution.py:433
  901.8 7.2 fusion.62
  927.6 8.7 copy.158
  953.8 27.2 %all-to-all-done.2 = bf16[8,2048,128]{2,1,0:T(8,128)(2,1)} async-done(((bf16[8,2048,128]{2,1,0:T(8,128)(2,1)}), bf16[8,2048,128]{2,1,0:T(8,128)(2,1)}, u32[]{:S(2)}, u32[]{:S(2)}) %all-to-all-start.2) | async-done | bytes 4194336 | tf_op jit(solution)/shard_map/all_to_all | solution.py:434
  981.1 24.6 %gather_fusion.1 = bf16[8192,128]{1,0:T(8,128)(2,1)S(1)} fusion(bf16[16384,128]{1,0:T(8,128)(2,1)} %bitcast.74, s32[8192]{0:T(1024)S(1)} %copy-done.102), kind=kCustom, calls=%fused_computation.1 | custom fusion | bytes 4227072 | tf_op jit(solution)/shard_map/gather | solution.py:437
  1018.7 13.5 %concatenate.56 = f32[141440]{0:T(1024)} concatenate(f32[704]{0:T(1024)S(1)} %reshape.564, f32[64]{0:T(128)S(1)} %get-tuple-element.124, f32[8192]{0:T(1024)S(1)} %convolution_bitcast_fusion.6, f32[128]{0:T(128)S(1)} %convert_reduce_fusion.4, f32[49152]{0:T(1024)S(1)} %copy-done.81, f32[16384]{0:T(1024)S(1)} %convolution_bitcast_fusion.3, f32[32768]{0:T(1024)S(1)} %bitcast.336, ...), dimensions={0} | concatenate | bytes 1131520 | tf_op jit(solution)/shard_map/concatenate | solution.py:73
  1036.7 38.7 %all-reduce.1 = (f32[6]{0:T(128)}, f32[]{:T(128)}) all-reduce(f32[6]{0:T(128)} %concatenate.59, f32[]{:T(128)} %get-tuple-element.30), channel_id=1, replica_groups=mesh['tile'=8,'row'=4] {'tile','row'}, use_global_device_ids=true, to_apply=%region_56.57 | all-reduce | flops 7 | bytes 56 | tf_op jit(solution)/shard_map/psum | solution.py:442
  1077.3 85.8 %all-reduce.5.cloned.1.call-done = (f32[141440]{0:T(1024)}, f32[132352]{0:T(1024)}) async-done(((f32[141440]{0:T(1024)}, f32[132352]{0:T(1024)}), (f32[141440]{0:T(1024)}, f32[132352]{0:T(1024)})) %all-reduce.5.cloned.1.call-update) | async-done | bytes 1095184 | tf_op jit(solution)/shard_map/psum | solution.py:442
  (520 shorter events, 310.9 us)
Async XLA Ops:
  7.2 52.8 %copy-start = (bf16[11,8192]{1,0:T(8,128)(2,1)S(1)}, bf16[11,8192]{1,0:T(8,128)(2,1)}, u32[]{:S(2)}) copy-start(bf16[11,8192]{1,0:T(8,128)(2,1)} %param.9) | copy-start | bytes 540676
  7.2 45.6 %copy-start.38 = (bf16[24,192,128]{2,1,0:T(8,128)(2,1)S(1)}, bf16[24,192,128]{2,1,0:T(8,128)(2,1)}, u32[]{:S(2)}) copy-start(bf16[24,192,128]{2,1,0:T(8,128)(2,1)} %param.14) | copy-start | bytes 3538948
  7.2 51.1 %copy-start.40 = (f32[273792]{0:T(1024)S(1)}, f32[273792]{0:T(1024)}, u32[]{:S(2)}) copy-start(f32[273792]{0:T(1024)} %param.15) | copy-start | bytes 3285508
  13.0 51.4 %copy-start.103 = (s32[8192,1]{0,1:T(1,128)}, s32[8192,1]{0,1:T(1,128)S(1)}, u32[]{:S(2)}) copy-start(s32[8192,1]{0,1:T(1,128)S(1)} %compare_select_fusion.2) | copy-start | bytes 98308
  45.5 43.0 %all-to-all-start = ((s32[8,1,2048]{2,1,0:T(1,128)}), s32[8,1,2048]{2,1,0:T(1,128)S(1)}, u32[]{:S(2)}, u32[]{:S(2)}) async-start(s32[8,1,2048]{2,1,0:T(1,128)} %bitcast.7), calls=%async_computation | async-start | bytes 131072 | tf_op jit(solution)/shard_map/all_to_all | solution.py:390
  53.6 362.4 %collective-permute-start = (f32[6,192,128]{2,1,0:T(8,128)}, f32[6,192,128]{2,1,0:T(8,128)}, u32[]{:S(2)}, u32[]{:S(2)}) collective-permute-start(f32[6,192,128]{2,1,0:T(8,128)} %slice.334), channel_id=1, source_target_pairs={{0,28},{4,0},{8,4},{12,8},{16,12},{20,16},{24,20},{28,24},{1,29},{... | collective-permute-start | bytes 1769480 | tf_op jit(solution)/shard_map/ppermute | solution.py:29
  59.0 340.2 %copy-start.108 = (f32[128]{0:T(128)}, f32[128]{0:T(128)S(1)}, u32[]{:S(2)}) copy-start(f32[128]{0:T(128)S(1)} %get-tuple-element.83) | copy-start | bytes 1540
  59.0 347.3 %copy-start.112 = (f32[128]{0:T(128)}, f32[128]{0:T(128)S(1)}, u32[]{:S(2)}) copy-start(f32[128]{0:T(128)S(1)} %get-tuple-element.80) | copy-start | bytes 1540
  59.1 34.5 %copy-start.42 = (bf16[273792]{0:T(1024)(128)(2,1)}, bf16[273792]{0:T(1024)(128)(2,1)S(1)}, u32[]{:S(2)}) copy-start(bf16[273792]{0:T(1024)(128)(2,1)S(1)} %convert.31) | copy-start | bytes 1642756
  88.4 109.1 %copy-start.107 = (s32[24,192]{1,0:T(8,128)S(1)}, s32[24,192]{1,0:T(8,128)}, u32[]{:S(2)}) copy-start(s32[24,192]{1,0:T(8,128)} %param.13) | copy-start | bytes 55300
  88.4 122.4 %all-to-all-start.1 = ((bf16[8,2048,128]{2,1,0:T(8,128)(2,1)}), bf16[8,2048,128]{2,1,0:T(8,128)(2,1)}, u32[]{:S(2)}, u32[]{:S(2)}) async-start(bf16[8,2048,128]{2,1,0:T(8,128)(2,1)} %bitcast.319), calls=%async_computation.1 | async-start | bytes 8388608 | tf_op jit(solution)/shard_map/all_to_all | solution.py:405
  197.4 117.0 %copy-start.100 = (f32[4608]{0:T(1024)}, f32[4608]{0:T(1024)S(1)}, u32[]{:S(2)}) copy-start(f32[4608]{0:T(1024)S(1)} %get-tuple-element.99) | copy-start | bytes 55300
  197.5 5.2 collective-permute-start.2
  198.5 124.6 %copy-start.68 = (bf16[128,384,1]{1,0,2:T(8,128)(2,1)}, bf16[128,384,1]{1,0,2:T(8,128)(2,1)S(1)}, u32[]{:S(2)}) copy-start(bf16[128,384,1]{1,0,2:T(8,128)(2,1)S(1)} %reshape.624) | copy-start | bytes 294916
  202.7 1.7 collective-permute-start.3
  205.7 200.7 %copy-start.58 = (f32[32,144]{1,0:T(8,128)}, f32[32,144]{1,0:T(8,128)S(1)}, u32[]{:S(2)}) copy-start(f32[32,144]{1,0:T(8,128)S(1)} %get-tuple-element.130) | copy-start | bytes 55300
  415.0 17.9 %collective-permute-start.4 = (f32[6,192,128]{2,1,0:T(8,128)}, f32[6,192,128]{2,1,0:T(8,128)}, u32[]{:S(2)}, u32[]{:S(2)}) collective-permute-start(f32[6,192,128]{2,1,0:T(8,128)} %slice.354), channel_id=1, source_target_pairs={{0,28},{4,0},{8,4},{12,8},{16,12},{20,16},{24,20},{28,24},{1,29},{... | collective-permute-start | bytes 1769480 | tf_op jit(solution)/shard_map/ppermute | solution.py:29
  416.0 27.4 %copy-start.70 = (bf16[128,384,1]{1,0,2:T(8,128)(2,1)}, bf16[128,384,1]{1,0,2:T(8,128)(2,1)S(1)}, u32[]{:S(2)}) copy-start(bf16[128,384,1]{1,0,2:T(8,128)(2,1)S(1)} %reshape.628) | copy-start | bytes 294916
  416.9 4.3 collective-permute-start.1
  433.6 4.6 collective-permute-start.5
  514.3 31.5 %copy-start.4 = (f32[32,144,128]{2,1,0:T(8,128)}, f32[32,144,128]{2,1,0:T(8,128)S(1)}, u32[]{:S(2)}) copy-start(f32[32,144,128]{2,1,0:T(8,128)S(1)} %get-tuple-element.63) | copy-start | bytes 7077892
  514.4 31.4 %copy-start.75 = (f32[32,144]{1,0:T(8,128)}, f32[32,144]{1,0:T(8,128)S(1)}, u32[]{:S(2)}) copy-start(f32[32,144]{1,0:T(8,128)S(1)} %broadcast_multiply_fusion.1) | copy-start | bytes 55300
  516.4 29.4 %copy-start.85 = (f32[32,144]{1,0:T(8,128)}, f32[32,144]{1,0:T(8,128)S(1)}, u32[]{:S(2)}) copy-start(f32[32,144]{1,0:T(8,128)S(1)} %fusion.78) | copy-start | bytes 55300
  662.7 12.1 %collective-permute-start.6 = (bf16[6,192,128]{2,1,0:T(8,128)(2,1)S(1)}, bf16[6,192,128]{2,1,0:T(8,128)(2,1)S(1)}, u32[]{:S(2)}, u32[]{:S(2)}) collective-permute-start(bf16[6,192,128]{2,1,0:T(8,128)(2,1)S(1)} %slice.428), channel_id=1, source_target_pairs={{0,4},{4,8},{8,12},{12,16},{16,20},{20,24},{24,28},{28,0},{1,5},{5... | collective-permute-start | bytes 884744 | tf_op jit(solution)/shard_map/ppermute | solution.py:29
  674.9 3.6 collective-permute-start.7
  714.4 22.3 %slice-start = ((s8[6291456]{0:T(1024)(128)(4,1)}), s8[2097152]{0:T(1024)(128)(4,1)S(1)}, s32[]{:S(2)}) async-start(s8[6291456]{0:T(1024)(128)(4,1)} %bitcast.288), calls=%async_computation.4 | async-start | bytes 4194304
  885.0 96.0 %all-to-all-start.2 = ((bf16[8,2048,128]{2,1,0:T(8,128)(2,1)}), bf16[8,2048,128]{2,1,0:T(8,128)(2,1)}, u32[]{:S(2)}, u32[]{:S(2)}) async-start(bf16[8,2048,128]{2,1,0:T(8,128)(2,1)} %bitcast.318), calls=%async_computation.2 | async-start | bytes 8388608 | tf_op jit(solution)/shard_map/all_to_all | solution.py:434
  889.8 273.3 %all-reduce.5.cloned.1.call-start = ((), (), s32[]{:S(2)}) async-start(), calls=%async_computation.3 | async-start | bytes 2203648 | tf_op jit(solution)/shard_map/psum | solution.py:442
  951.7 29.3 %copy-start.102 = (s32[8192]{0:T(1024)S(1)}, s32[8192]{0:T(1024)}, u32[]{:S(2)}) copy-start(s32[8192]{0:T(1024)} %broadcast_clamp_fusion.1) | copy-start | bytes 98308
  981.1 24.7 %copy-start.106 = (pred[8192]{0:T(1024)(128)(4,1)S(1)}, pred[8192]{0:T(1024)(128)(4,1)}, u32[]{:S(2)}) copy-start(pred[8192]{0:T(1024)(128)(4,1)} %get-tuple-element.71) | copy-start | bytes 24580
  1032.2 134.7 %copy-start.41 = (f32[273792]{0:T(1024)S(1)}, f32[273792]{0:T(1024)}, u32[]{:S(2)}) copy-start(f32[273792]{0:T(1024)} %param.15) | copy-start | bytes 3285508
  1032.2 134.7 %copy-start.64 = (f32[273792]{0:T(1024)S(1)}, f32[273792]{0:T(1024)}, u32[]{:S(2)}) copy-start(f32[273792]{0:T(1024)} %param.16) | copy-start | bytes 3285508
  (131 other events, 738.7 us)
Sparse Core Ops, SparseCore 0:
  1032.4 130.6 all-reduce.4
where the time goes:
time: 1190 us; the launch traced here: 1180 us
  other arithmetic  407 us (34%)
  matrix products  288 us (24%)
  local copies, waits for them, and re-layouts  263 us (22%)
  waiting for transfers between devices  135 us (11%)
  blocking collectives  38.7 us (3%)
  starting transfers between devices  28.8 us (2%)
  between operations  19.1 us (2%)
    scatter-add x1, other arithmetic, local(): jax.ops.segment_sum(slot_out.astype(jnp.float32), safe_cells, num_segment...  104 us
    scatter-add x1, other arithmetic, local(): jax.ops.segment_sum(slot_live.astype(jnp.float32), safe_cells, num_segmen...  102 us
    psum x1, waiting for transfers between devices, local(): lax.psum((flat_rest, flat_two, square_sums, live_total), ('tile', 'row'))  85.8 us
    convert_element_type x2, other arithmetic, layer_backward(): grad_scores = grad_scores.astype(jnp.bfloat16)  67.1 us
    gather x1, local copies, waits for them, and re-layouts, local(): slot_grads = grad_table[safe_cells]  57.8 us
    dot_general x2, matrix products, layer_backward(): jnp.einsum('wqhd,wkhd->whqk', grad_mix, packed[:, :, 2], preferred_elemen...  49.6 us
    psum x1, blocking collectives, local(): lax.psum((flat_rest, flat_two, square_sums, live_total), ('tile', 'row'))  38.7 us
    reduce_sum x2, other arithmetic, layer_forward(): row_total = jnp.sum(exponent, axis=-1, keepdims=True)  38.4 us
  transfers between devices with their start and end apart: 12, of which 9 were waited for; matrix products, arithmetic and copies ran while one was open for 36% of the time, Pallas kernels for 0%

commit v1 on v0

v1 whole, which is shorter than its diff:
```python
import jax
import jax.numpy as jnp
from jax import lax
from jax.experimental import pallas as pl
from jax.experimental.pallas import tpu as pltpu
from jax.sharding import PartitionSpec as P

D = 128
HEADS = 8
HD = 16
FF = 256
H1 = 64
WIN = 12
C_IN = 11
QS = 6
QC = 36
QP = 40
SLOTS = 144
KEYS = HEADS * SLOTS
LAYER_ROWS = 1034
POINT_ROWS = 71
GRAD_ROWS = 1040
BLOCK = 256
CHUNK = 512
LO = 512
NW = 2

clip_norm = 0.01
beta_one = 0.9
beta_two = 0.999
step_count = 10
learn_rate = 0.1
decay_rate = 0.05
adam_eps = 1e-08

F32 = jnp.float32
BF16 = jnp.bfloat16
GELU_C = 0.7978845608028654
GELU_A = 0.044715


def mm(a, b):
    return lax.dot_general(a, b, (((1,), (0,)), ((), ())), preferred_element_type=F32)


def mm_nt(a, b):
    return lax.dot_general(a, b, (((1,), (1,)), ((), ())), preferred_element_type=F32)


def mm_tn(a, b):
    return lax.dot_general(a, b, (((0,), (0,)), ((), ())), preferred_element_type=F32)


def lane_iota(rows=1):
    return lax.broadcasted_iota(jnp.int32, (rows, D), 1)


def part8(v):
    return jnp.sum(v.reshape(v.shape[0] // 8, 8, v.shape[1]), axis=0)


def gelu_parts(v):
    sq = v * v
    t = jnp.tanh(v * (GELU_C + (GELU_C * GELU_A) * sq))
    half = 0.5 + 0.5 * t
    slope = half + (0.5 * v) * (1.0 - t * t) * (GELU_C + (3.0 * GELU_C * GELU_A) * sq)
    return v * half, slope


def gelu_only(v):
    t = jnp.tanh(v * (GELU_C + (GELU_C * GELU_A) * (v * v)))
    return v * (0.5 + 0.5 * t)


def normalize(y):
    center = y - jnp.mean(y, axis=-1, keepdims=True)
    rs = lax.rsqrt(jnp.mean(center * center, axis=-1, keepdims=True) + 1e-05)
    return center * rs, rs


def norm_pull(gx, xhat, rs):
    return rs * (
        gx
        - jnp.mean(gx, axis=-1, keepdims=True)
        - xhat * jnp.mean(gx * xhat, axis=-1, keepdims=True)
    )


def load_layer(par, base, w):
    for part in range(3):
        m = par[pl.ds(base + part, D, stride=3), :]
        w["qkv"][:, part * D : (part + 1) * D] = m.astype(BF16)
        if "qkv_t" in w:
            w["qkv_t"][part * D : (part + 1) * D, :] = m.T.astype(BF16)
    m = par[pl.ds(base + 384, D), :]
    w["out"][...] = m.astype(BF16)
    if "out_t" in w:
        w["out_t"][...] = m.T.astype(BF16)
    for part in range(2):
        m = par[pl.ds(base + 512 + part, D, stride=2), :]
        w["fin"][:, part * D : (part + 1) * D] = m.astype(BF16)
        if "fin_t" in w:
            w["fin_t"][part * D : (part + 1) * D, :] = m.T.astype(BF16)
        m = par[pl.ds(base + 768 + part * D, D), :]
        w["fout"][part * D : (part + 1) * D, :] = m.astype(BF16)
        if "fout_t" in w:
            w["fout_t"][:, part * D : (part + 1) * D] = m.T.astype(BF16)


WEIGHT_SHAPES = {
    "qkv": (D, 3 * D),
    "qkv_t": (3 * D, D),
    "out": (D, D),
    "out_t": (D, D),
    "fin": (D, FF),
    "fin_t": (FF, D),
    "fout": (FF, D),
    "fout_t": (D, FF),
}


def vec(par, base, row):
    return par[base + 1024 + row : base + 1025 + row, :]


def vec2(par, base, row):
    return jnp.concatenate([vec(par, base, row), vec(par, base, row + 1)], axis=1)


def head_lanes():
    return lane_iota() // HD


def head_rows(m):
    lanes = head_lanes()
    keep = [jnp.where(lanes == h, 1.0, 0.0).astype(BF16) for h in range(HEADS)]
    top = m[:D]
    rest = m[D:]
    return jnp.concatenate([top * k for k in keep] + [rest * k for k in keep], axis=0)


def window_bias(groups):
    keys = jnp.concatenate(
        [groups[:D]] + [groups[D:]] * HEADS + [jnp.ones((D, D), BF16)], axis=0
    )
    same = mm_nt(groups, keys)
    rows = lax.broadcasted_iota(jnp.int32, (SLOTS, D), 0)
    lanes = lane_iota(SLOTS)
    first = (same[:, :D] > 0.5) | (rows == lanes)
    last = (same[:, D : 2 * D] > 0.5) | (rows == lanes % HD + D)
    return (
        jnp.where(first, 0.0, -1000000000.0),
        jnp.where(last, 0.0, -1000000000.0),
        same[:, 2 * D :],
    )


def attend(qs, key, val, bias_first, bias_last):
    scores = mm_nt(key, head_rows(qs))
    probs = []
    for h in range(HEADS + 1):
        part = scores[:, h * D : (h + 1) * D] + (bias_first if h < HEADS else bias_last)
        expo = jnp.exp(part - jnp.max(part, axis=0, keepdims=True))
        probs.append((expo * (1.0 / jnp.sum(expo, axis=0, keepdims=True))).astype(BF16))
    probs = jnp.concatenate(probs, axis=1)
    return probs, query_pull(val, probs)


def attend_pull(probs, qs, key, val, gmix):
    rows = head_rows(gmix)
    pulled = mm_nt(val, rows)
    gs = []
    for h in range(HEADS + 1):
        cols = slice(h * D, (h + 1) * D)
        p = probs[:, cols].astype(F32)
        both = p * pulled[:, cols]
        gs.append((both - p * jnp.sum(both, axis=0, keepdims=True)).astype(BF16))
    gs = jnp.concatenate(gs, axis=1)
    return query_pull(key * 0.25, gs), mm(gs, head_rows(qs)).astype(BF16), mm(probs, rows).astype(BF16)


def query_pull(rows, cols):
    full = mm_tn(rows, cols)
    top = jnp.concatenate(
        [full[h * HD : (h + 1) * HD, h * D : (h + 1) * D] for h in range(HEADS)], axis=0
    )
    chan = lax.broadcasted_iota(jnp.int32, (D, D), 0)
    lanes = lane_iota(D)
    rest = jnp.where(chan // HD == lanes // HD, full[:, HEADS * D :], 0.0).astype(BF16)
    fold = jnp.where(
        lax.broadcasted_iota(jnp.int32, (HD, D), 0) == lane_iota(HD) % HD, 1.0, 0.0
    ).astype(BF16)
    return jnp.concatenate([top.T.astype(BF16), mm_nt(fold, rest).astype(BF16)], axis=0)


def split_qkv(packed, w):
    rows = slice(w * SLOTS, (w + 1) * SLOTS)
    return packed[rows, :D] * 0.25, packed[rows, D : 2 * D], packed[rows, 2 * D :]


def layer_forward(x, groups, par, base, w, sums):
    count = x.shape[0] // SLOTS
    low = x.astype(BF16)
    qkv_bias = jnp.concatenate(
        [vec(par, base, 0), jnp.zeros((1, D), F32), vec(par, base, 1)], axis=1
    )
    packed = (mm(low, w["qkv"][...]) + qkv_bias).astype(BF16)
    probs, mixes, lives = [], [], []
    for i in range(count):
        bias_first, bias_last, live = window_bias(groups[i])
        qs, key, val = split_qkv(packed, i)
        prob, mix = attend(qs, key, val, bias_first, bias_last)
        probs.append(prob)
        mixes.append(mix)
        lives.append(live)
    mix = jnp.concatenate(mixes, axis=0)
    live = jnp.concatenate(lives, axis=0)
    attn_out = mm(mix, w["out"][...]) + vec(par, base, 2)
    first = x + attn_out
    xhat1, rs1 = normalize(first)
    normed = (xhat1 * vec(par, base, 3) + vec(par, base, 4)) * live
    normed_low = normed.astype(BF16)
    pre = mm(normed_low, w["fin"][...]) + vec2(par, base, 5)
    act, slope = gelu_parts(pre)
    hidden = act.astype(BF16)
    ffn = mm(hidden, w["fout"][...]) + vec(par, base, 7)
    second = normed + ffn
    xhat2, rs2 = normalize(second)
    result = (xhat2 * vec(par, base, 8) + vec(par, base, 9)) * live
    sums[0] += part8(attn_out * attn_out * live)
    sums[1] += part8(ffn * ffn * live)
    sums[2] += part8(result * result)
    sums[3] += part8(live)
    return dict(
        low=low,
        packed=packed,
        probs=probs,
        mix=mix,
        live=live,
        first=first,
        second=second,
        xhat1=xhat1,
        rs1=rs1,
        xhat2=xhat2,
        rs2=rs2,
        normed_low=normed_low,
        slope=slope,
        hidden=hidden,
        result=result,
    )


def layer_backward(grad, k, par, base, w, acc):
    live = k["live"]
    gl = grad * live
    acc["vec"][8] += part8(gl * k["xhat2"])
    acc["vec"][9] += part8(gl)
    g2 = norm_pull(gl * vec(par, base, 8), k["xhat2"], k["rs2"])
    g_ffn = g2.astype(BF16)
    acc["fout"][...] += mm_tn(k["hidden"], g_ffn)
    acc["vec"][7] += part8(g_ffn.astype(F32))
    g_pre = (mm(g_ffn, w["fout_t"][...]) * k["slope"]).astype(BF16)
    acc["fin"][...] += mm_tn(k["normed_low"], g_pre)
    for part in range(2):
        acc["vec"][5 + part] += part8(g_pre[:, part * D : (part + 1) * D].astype(F32))
    g_norm = (g2 + mm(g_pre, w["fin_t"][...])) * live
    acc["vec"][3] += part8(g_norm * k["xhat1"])
    acc["vec"][4] += part8(g_norm)
    g1 = norm_pull(g_norm * vec(par, base, 3), k["xhat1"], k["rs1"])
    g_attn = g1.astype(BF16)
    acc["out"][...] += mm_tn(k["mix"], g_attn)
    acc["vec"][2] += part8(g_attn.astype(F32))
    g_mix = mm(g_attn, w["out_t"][...]).astype(BF16)
    pieces = []
    for i in range(grad.shape[0] // SLOTS):
        rows = slice(i * SLOTS, (i + 1) * SLOTS)
        qs, key, val = split_qkv(k["packed"], i)
        pieces.append(
            jnp.concatenate(
                attend_pull(k["probs"][i], qs, key, val, g_mix[rows]), axis=1
            )
        )
    g_packed = jnp.concatenate(pieces, axis=0)
    acc["qkv"][...] += mm_tn(k["low"], g_packed)
    acc["vec"][0] += part8(g_packed[:, :D].astype(F32))
    acc["vec"][1] += part8(g_packed[:, 2 * D :].astype(F32))
    return g1 + mm(g_packed, w["qkv_t"][...])


ACC_SHAPES = {
    "qkv": (D, 3 * D),
    "out": (D, D),
    "fin": (D, FF),
    "fout": (FF, D),
    "vec": (10, 8, D),
}


def clear(acc):
    for ref in acc.values():
        ref[...] = jnp.zeros(ref.shape, ref.dtype)


def store_grads(acc, out):
    for part in range(3):
        out[pl.ds(part, D, stride=3), :] = acc["qkv"][:, part * D : (part + 1) * D]
    out[pl.ds(384, D), :] = acc["out"][...]
    for part in range(2):
        out[pl.ds(512 + part, D, stride=2), :] = acc["fin"][:, part * D : (part + 1) * D]
    out[pl.ds(768, FF), :] = acc["fout"][...]
    out[pl.ds(1024, 16), :] = jnp.concatenate(
        [jnp.sum(acc["vec"][i], axis=0, keepdims=True) for i in range(10)]
        + [jnp.zeros((6, D), F32)],
        axis=0,
    )


def gather_windows(scratch, pick):
    for i in range(NW):
        for r in range(2):
            for c in range(2):
                at = i * SLOTS + (2 * r + c) * QC
                scratch[pl.ds(at, QC), :] = pick(r, 2 * i + c)
    return scratch[...]


def spread_windows(scratch, value, put):
    scratch[...] = value
    for i in range(NW):
        for r in range(2):
            for c in range(2):
                put(r, 2 * i + c, scratch[pl.ds(i * SLOTS + (2 * r + c) * QC, QC), :])


def whole(shape, space=pltpu.VMEM):
    return pl.BlockSpec(shape, lambda *_: (0,) * len(shape), memory_space=space)


def params_for(limit=56):
    return pltpu.CompilerParams(
        dimension_semantics=("arbitrary",), vmem_limit_bytes=limit * 1024 * 1024
    )


def first_layer(pillars, par, quads_x, quads_y):
    across = quads_x // 2
    along = quads_y // (2 * NW)
    windows = quads_x * quads_y // 4
    base = POINT_ROWS

    def kernel(pil, par_ref, *refs):
        outs, scratch = refs[:12], refs[12:]
        (
            field,
            probs_out,
            packed_out,
            mix_out,
            first_out,
            second_out,
            low_out,
            live_out,
            sums_out,
            row_out,
            col_out,
            cor_out,
        ) = outs
        names = ["qkv", "out", "fin", "fout"]
        w = dict(zip(names, scratch[:4]))
        wide, pout, sums = scratch[4:]
        step = pl.program_id(0)
        a = step // along
        b = step % along

        @pl.when(step == 0)
        def _():
            load_layer(par_ref, base, w)
            m = par_ref[pl.ds(6, H1), :].astype(BF16)
            pout[...] = jnp.concatenate([m, m], axis=0)
            sums[...] = jnp.zeros(sums.shape, F32)

        cells = gather_windows(wide, lambda r, c: pil[r, c, :QC, :])
        lanes = lane_iota()
        total = jnp.where(lanes < H1, cells, 0.0)
        count = cells[:, H1 : H1 + 1]
        high = total.astype(BF16).astype(F32)
        both = (high + pltpu.roll(total - high, H1, axis=1)).astype(BF16)
        pillar = mm(both, pout[...]) + count * par_ref[70:71, :]
        x = pillar / jnp.maximum(count, 1.0)
        onehot = jnp.where((lanes > H1) & (lanes < H1 + 4) & (count > 0.0), cells, 0.0).astype(BF16)
        groups = [onehot[i * SLOTS : (i + 1) * SLOTS] for i in range(NW)]
        k = layer_forward(x, groups, par_ref, base, w, sums)
        for i in range(NW):
            rows = slice(i * SLOTS, (i + 1) * SLOTS)
            probs_out[i] = k["probs"][i]
            packed_out[i] = k["packed"][rows]
            mix_out[i] = k["mix"][rows]
            first_out[i] = k["first"][rows]
            second_out[i] = k["second"][rows]
            low_out[i] = k["low"][rows]
            live_out[i] = k["live"][rows]

        def put(r, c, v):
            field[r, c, :QC, :] = v

        spread_windows(wide, k["result"], put)

        @pl.when(a == 0)
        def _():
            for c in range(2 * NW):
                row_out[c] = field[0, c, :QC, :].astype(BF16)

        @pl.when(b == 0)
        def _():
            for r in range(2):
                col_out[r] = field[r, 0, :QC, :].astype(BF16)

        @pl.when(step == 0)
        def _():
            cor_out[0] = field[0, 0, :QC, :].astype(BF16)

        @pl.when(step == pl.num_programs(0) - 1)
        def _():
            sums_out[...] = sums[...]

    def win_spec(width):
        return pl.BlockSpec((NW, SLOTS, width), lambda s: (s, 0, 0))

    quad_spec = pl.BlockSpec((2, 2 * NW, QP, D), lambda s: (s // along, s % along, 0, 0))
    shape = jax.ShapeDtypeStruct
    return pl.pallas_call(
        kernel,
        grid=(across * along,),
        in_specs=[quad_spec, whole(par.shape)],
        out_specs=[
            quad_spec,
            win_spec(KEYS),
            win_spec(3 * D),
            win_spec(D),
            win_spec(D),
            win_spec(D),
            win_spec(D),
            win_spec(D),
            whole((4, 8, D)),
            pl.BlockSpec((2 * NW, QC, D), lambda s: (jnp.minimum(s, along - 1), 0, 0)),
            pl.BlockSpec((2, QC, D), lambda s: (s // along, 0, 0)),
            whole((1, QC, D)),
        ],
        out_shape=[
            shape((quads_x, quads_y, QP, D), F32),
            shape((windows, SLOTS, KEYS), BF16),
            shape((windows, SLOTS, 3 * D), BF16),
            shape((windows, SLOTS, D), BF16),
            shape((windows, SLOTS, D), F32),
            shape((windows, SLOTS, D), F32),
            shape((windows, SLOTS, D), BF16),
            shape((windows, SLOTS, D), F32),
            shape((4, 8, D), F32),
            shape((quads_y, QC, D), BF16),
            shape((quads_x, QC, D), BF16),
            shape((1, QC, D), BF16),
        ],
        scratch_shapes=[pltpu.VMEM(WEIGHT_SHAPES[n], BF16) for n in ["qkv", "out", "fin", "fout"]]
        + [
            pltpu.VMEM((NW * SLOTS, D), F32),
            pltpu.VMEM((D, D), BF16),
            pltpu.VMEM((4, 8, D), F32),
        ],
        compiler_params=params_for(),
        name="first_layer",
    )(pillars, par)


def second_layer(flags, field, halos, tags, tag_halos, cot, cot_halos, par, scale):
    quads_x, quads_y = field.shape[:2]
    across = quads_x // 2
    along = quads_y // (2 * NW)
    base = POINT_ROWS + LAYER_ROWS
    wnames = list(WEIGHT_SHAPES)
    anames = list(ACC_SHAPES)

    def kernel(flag, *refs):
        ins, refs = refs[:13], refs[13:]
        outs, scratch = refs[:6], refs[6:]
        fields, tagss, cots, par_ref = ins[:4], ins[4:8], ins[8:12], ins[12]
        grads, weights, row_out, col_out, cor_out, sums_out = outs
        w = dict(zip(wnames, scratch))
        scratch = scratch[len(wnames) :]
        acc = dict(zip(anames, scratch))
        wide, sums, ext_x, ext_t, ext_g = scratch[len(anames) :]
        step = pl.program_id(0)
        a = step // along
        b = step % along

        @pl.when(step == 0)
        def _():
            load_layer(par_ref, base, w)
            sums[...] = jnp.zeros(sums.shape, F32)
            clear(acc)
            lanes = lane_iota()

            def moved(v, region):
                return pltpu.roll(v, 3 * region, axis=1)

            def fill(ext, srcs, turn_row, turn_col, turn_cor):
                main, row, col, cor = srcs

                def one(i, _):
                    ext[i // quads_y, i % quads_y, :QC, :] = main[
                        i // quads_y, i % quads_y, :QC, :
                    ].astype(F32)
                    return 0

                lax.fori_loop(0, quads_x * quads_y, one, 0, unroll=4)

                def one_row(i, _):
                    ext[quads_x, i, :QC, :] = turn_row(row[i].astype(F32))
                    return 0

                lax.fori_loop(1, quads_y, one_row, 0)
                for i in range(1, quads_x):
                    ext[i, quads_y, :QC, :] = turn_col(col[i].astype(F32))
                ext[quads_x, quads_y, :QC, :] = turn_cor(cor[0].astype(F32))

            def same(v):
                return v

            last_x = flag[0] > 0
            last_y = flag[1] > 0

            def tag_row(v):
                return jnp.where(last_x, moved(v, 2), v)

            def tag_col(v):
                return jnp.where(last_y, moved(v, 1), v)

            fill(ext_x, fields, same, same, same)
            fill(ext_t, tagss, tag_row, tag_col, lambda v: tag_row(tag_col(v)))
            fill(ext_g, cots, same, same, same)

        def picker(ext):
            return lambda r, c: ext[2 * a + 1 + r, 2 * NW * b + 1 + c, :QC, :]

        tag = gather_windows(wide, picker(ext_t)).astype(BF16)
        groups = [tag[i * SLOTS : (i + 1) * SLOTS] for i in range(NW)]
        x = gather_windows(wide, picker(ext_x))
        k = layer_forward(x, groups, par_ref, base, w, sums)
        grad = gather_windows(wide, picker(ext_g)) * scale
        gx = layer_backward(grad, k, par_ref, base, w, acc)

        def put(r, c, v):
            grads[r, c, :QC, :] = v

        spread_windows(wide, gx, put)

        @pl.when(a == across - 1)
        def _():
            for c in range(2 * NW):
                row_out[c] = grads[1, c, :QC, :].astype(BF16)

        @pl.when(b == along - 1)
        def _():
            for r in range(2):
                col_out[r] = grads[r, 2 * NW - 1, :QC, :].astype(BF16)

        @pl.when(step == pl.num_programs(0) - 1)
        def _():
            cor_out[0] = grads[1, 2 * NW - 1, :QC, :].astype(BF16)
            sums_out[...] = sums[...]
            store_grads(acc, weights)

    shape = jax.ShapeDtypeStruct
    quad_spec = pl.BlockSpec((2, 2 * NW, QP, D), lambda s: (s // along, s % along, 0, 0))
    ext = pltpu.VMEM((quads_x + 1, quads_y + 1, QP, D), F32)
    arrays = [field, *halos, tags, *tag_halos, cot, *cot_halos, par]
    return pl.pallas_call(
        kernel,
        grid=(across * along,),
        in_specs=[pl.BlockSpec(memory_space=pltpu.SMEM)] + [whole(v.shape) for v in arrays],
        out_specs=[
            quad_spec,
            whole((GRAD_ROWS, D)),
            pl.BlockSpec(
                (2 * NW, QC, D), lambda s: (jnp.maximum(s - (across - 1) * along, 0), 0, 0)
            ),
            pl.BlockSpec((2, QC, D), lambda s: (s // along, 0, 0)),
            whole((1, QC, D)),
            whole((4, 8, D)),
        ],
        out_shape=[
            shape((quads_x, quads_y, QP, D), F32),
            shape((GRAD_ROWS, D), F32),
            shape((quads_y, QC, D), BF16),
            shape((quads_x, QC, D), BF16),
            shape((1, QC, D), BF16),
            shape((4, 8, D), F32),
        ],
        scratch_shapes=[pltpu.VMEM(WEIGHT_SHAPES[n], BF16) for n in wnames]
        + [pltpu.VMEM(ACC_SHAPES[n], F32) for n in anames]
        + [
            pltpu.VMEM((NW * SLOTS, D), F32),
            pltpu.VMEM((4, 8, D), F32),
            ext,
            ext,
            ext,
        ],
        compiler_params=params_for(),
        name="second_layer",
    )(flags, *arrays)


def first_layer_back(grads, halos, pillars, saved, par):
    quads_x, quads_y = grads.shape[:2]
    across = quads_x // 2
    along = quads_y // (2 * NW)
    base = POINT_ROWS
    wnames = list(WEIGHT_SHAPES)
    anames = list(ACC_SHAPES)

    def kernel(*refs):
        ins, refs = refs[:13], refs[13:]
        outs, scratch = refs[:3], refs[3:]
        main, row, col, cor, pil = ins[:5]
        probs, packed, mix, first, second, low, live = ins[5:12]
        par_ref = ins[12]
        cell_out, weights, point_weights = outs
        w = dict(zip(wnames, scratch))
        scratch = scratch[len(wnames) :]
        acc = dict(zip(anames, scratch))
        wide, ext, pacc = scratch[len(anames) :]
        step = pl.program_id(0)
        a = step // along
        b = step % along

        @pl.when(step == 0)
        def _():
            load_layer(par_ref, base, w)
            clear(acc)
            pacc[...] = jnp.zeros(pacc.shape, F32)
            for r in range(1, quads_x):

                def one(i, _):
                    ext[r, i, :QC, :] = main[r - 1, i - 1, :QC, :]
                    return 0

                lax.fori_loop(1, quads_y, one, 0)
                ext[r, 0, :QC, :] = col[r - 1].astype(F32)

            def one_row(i, _):
                ext[0, i, :QC, :] = row[i - 1].astype(F32)
                return 0

            lax.fori_loop(1, quads_y, one_row, 0)
            ext[0, 0, :QC, :] = cor[0].astype(F32)

        grad = gather_windows(wide, lambda r, c: ext[2 * a + r, 2 * NW * b + c, :QC, :])

        def rows_of(ref):
            return jnp.concatenate([ref[i] for i in range(NW)], axis=0)

        k = dict(
            low=rows_of(low),
            packed=rows_of(packed),
            probs=[probs[i] for i in range(NW)],
            mix=rows_of(mix),
            live=rows_of(live),
        )
        k["xhat1"], k["rs1"] = normalize(rows_of(first))
        k["xhat2"], k["rs2"] = normalize(rows_of(second))
        normed = (k["xhat1"] * vec(par_ref, base, 3) + vec(par_ref, base, 4)) * k["live"]
        k["normed_low"] = normed.astype(BF16)
        act, k["slope"] = gelu_parts(mm(k["normed_low"], w["fin"][...]) + vec2(par_ref, base, 5))
        k["hidden"] = act.astype(BF16)
        gx = layer_backward(grad, k, par_ref, base, w, acc)

        cells = gather_windows(wide, lambda r, c: pil[r, c, :QC, :])
        lanes = lane_iota()
        total = jnp.where(lanes <= H1, cells, 0.0)
        g_pillar = (gx / jnp.maximum(cells[:, H1 : H1 + 1], 1.0)).astype(BF16)
        high = total.astype(BF16)
        rest = (total - high.astype(F32)).astype(BF16)
        pacc[...] += mm_tn(high, g_pillar) + mm_tn(rest, g_pillar)

        def put(r, c, v):
            cell_out[r, c, :QC, :] = v
            cell_out[r, c, QC:, :] = jnp.zeros((QP - QC, D), F32)

        spread_windows(wide, g_pillar.astype(F32), put)

        @pl.when(step == pl.num_programs(0) - 1)
        def _():
            store_grads(acc, weights)
            point_weights[...] = pacc[:72, :]

    def win_spec(width):
        return pl.BlockSpec((NW, SLOTS, width), lambda s: (s, 0, 0))

    shape = jax.ShapeDtypeStruct
    quad_spec = pl.BlockSpec((2, 2 * NW, QP, D), lambda s: (s // along, s % along, 0, 0))
    return pl.pallas_call(
        kernel,
        grid=(across * along,),
        in_specs=[whole(grads.shape)]
        + [whole(v.shape) for v in halos]
        + [quad_spec]
        + [win_spec(v.shape[2]) for v in saved]
        + [whole(par.shape)],
        out_specs=[quad_spec, whole((GRAD_ROWS, D)), whole((72, D))],
        out_shape=[
            shape((quads_x, quads_y, QP, D), F32),
            shape((GRAD_ROWS, D), F32),
            shape((72, D), F32),
        ],
        scratch_shapes=[pltpu.VMEM(WEIGHT_SHAPES[n], BF16) for n in wnames]
        + [pltpu.VMEM(ACC_SHAPES[n], F32) for n in anames]
        + [
            pltpu.VMEM((NW * SLOTS, D), F32),
            pltpu.VMEM((quads_x, quads_y, QP, D), F32),
            pltpu.VMEM((D, D), F32),
        ],
        compiler_params=params_for(),
        name="first_layer_back",
    )(grads, *halos, pillars, *saved, par)


def one_hot(hit):
    return jnp.where(hit, 1.0, 0.0).astype(BF16)


def bin_points(feats, tiles, cells, valid, tile_count, capacity, extent_y, quads_y):
    blocks = tiles.shape[0]
    groups = tile_count * capacity // LO
    lots = 4
    wide = lots * BLOCK

    def kernel(feat_ref, tile_ref, cell_ref, valid_ref, out_ref, slot_ref, code_ref, acc):
        real = valid_ref[...] > 0
        t = jnp.where(real, tile_ref[...], tile_count)
        i0 = lax.broadcasted_iota(jnp.int32, (BLOCK, BLOCK), 0)
        i1 = lax.broadcasted_iota(jnp.int32, (BLOCK, BLOCK), 1)
        upto = one_hot(i0 <= i1)
        j0 = lax.broadcasted_iota(jnp.int32, (blocks, blocks), 0)
        j1 = lax.broadcasted_iota(jnp.int32, (blocks, blocks), 1)
        earlier = one_hot(j1 < j0)
        slot = jnp.full((blocks, BLOCK), -1.0, F32)
        for k in range(tile_count):
            hit = t == k
            run = mm(one_hot(hit), upto)
            total = jnp.broadcast_to(run[:, BLOCK - 1 :], (blocks, D)).astype(BF16)
            at = mm(earlier, total)[:, :1] + (k * capacity - 1.0)
            slot = jnp.where(hit, run + at, slot)
        slot_ref[...] = slot.astype(jnp.int32)

        def part(v, by):
            return ((v.astype(F32) + 0.5) * (1.0 / by)).astype(jnp.int32)

        cell = cell_ref[...]
        cx = part(cell, extent_y)
        cy = cell - cx * extent_y
        qx, qy = part(cx, QS), part(cy, QS)
        row = (qx * quads_y + qy) * QP + (cx - qx * QS) * QS + (cy - qy * QS)
        hi = row // LO
        lo = row - hi * LO
        low_part = lo % 256
        code_ref[0] = jnp.where(real, 1.0, 0.0)
        code_ref[1] = (hi + 1).astype(F32)
        code_ref[2] = (lo - low_part).astype(F32)
        code_ref[3] = low_part.astype(F32)
        acc[...] = jnp.zeros(acc.shape, F32)
        span = lax.broadcasted_iota(jnp.int32, (LO, wide), 0)

        def one(j, _):
            def line(ref, *lead):
                return jnp.concatenate(
                    [ref[(*lead, pl.ds(j * lots + u, 1), slice(None))] for u in range(lots)], axis=1
                )

            at = line(slot_ref)
            feat = feat_ref[:, pl.ds(pl.multiple_of(j * wide, wide), wide)].astype(F32)
            rows = jnp.concatenate(
                [feat] + [line(code_ref, i) for i in range(4)] + [jnp.zeros((1, wide), F32)], axis=0
            ).astype(BF16)
            group = at // LO
            place = one_hot(span == at % LO)
            spread = jnp.concatenate([rows * one_hot(group == g) for g in range(groups)], axis=0)
            acc[...] += mm_nt(spread, place)
            return 0

        lax.fori_loop(0, blocks // lots, one, 0)
        for k in range(tile_count):
            for at in range(0, capacity, LO):
                g, low = (k * capacity + at) // LO, (k * capacity + at) % LO
                size = min(LO, capacity)
                out_ref[k, :, at : at + size] = acc[g * 16 : g * 16 + 16, low : low + size].astype(
                    BF16
                )

    return pl.pallas_call(
        kernel,
        out_shape=jax.ShapeDtypeStruct((tile_count, 16, capacity), BF16),
        scratch_shapes=[
            pltpu.VMEM((blocks, BLOCK), jnp.int32),
            pltpu.VMEM((4, blocks, BLOCK), F32),
            pltpu.VMEM((groups * 16, LO), F32),
        ],
        compiler_params=pltpu.CompilerParams(vmem_limit_bytes=48 * 1024 * 1024),
        name="bin_points",
    )(feats, tiles, cells, valid)


def unpack_point_in(par_ref, win):
    lanes = lane_iota()
    flat = par_ref[0:6, :]
    turned = pltpu.roll(flat, H1, axis=1)
    even = jnp.where(lanes < H1, flat, turned)
    odd = jnp.where(lanes < H1, turned, flat)
    rows = []
    for k in range(C_IN):
        src = even if k % 2 == 0 else odd
        rows.append(src[k // 2 : k // 2 + 1])
    rows.append(jnp.zeros((5, D), F32))
    win[:, :D] = jnp.concatenate(rows, axis=0).astype(BF16)
    at = lax.broadcasted_iota(jnp.int32, (16, D), 0)
    win[:, D : 2 * D] = one_hot(at == 12)
    win[:, 2 * D :] = one_hot((at == 13) | (at == 14))
    return odd[5:6]


def encode_points(recv, held, par, base_rows, quads):
    sources, _, capacity = recv.shape
    chunk = min(CHUNK, capacity)
    groups = -(-quads * QP // LO)
    pairs = -(-groups // 2)

    def kernel(held_ref, recv_ref, par_ref, base_ref, out_ref, tag_ref, win, acc):
        bias = unpack_point_in(par_ref, win)
        acc[...] = jnp.zeros(acc.shape, F32)
        lanes = lane_iota()
        own = jnp.where(lanes < H1, 1.0, 2.0)
        count_of = (lanes + 1).astype(F32)
        span = lax.broadcasted_iota(jnp.int32, (LO, chunk), 0)

        def source(s, _):
            def piece(j, _):
                cols = recv_ref[s, :, pl.ds(pl.multiple_of(j * chunk, chunk), chunk)]
                wide = cols.astype(F32)
                place = one_hot(span == (wide[13:14] + wide[14:15]).astype(jnp.int32))
                both = mm_tn(cols, win[:, : 2 * D])
                act = gelu_only(both[:, :D] + bias)
                group = both[:, D:]
                spread = [
                    jnp.where(group == own + 2.0 * g, act, 0.0).astype(BF16) for g in range(pairs)
                ]
                spread.append(one_hot(group == count_of))
                acc[...] += mm(place, jnp.concatenate(spread, axis=1))
                return 0

            lax.fori_loop(0, (held_ref[s] + chunk - 1) // chunk, piece, 0)
            return 0

        lax.fori_loop(0, sources, source, 0)
        for g in range(groups):
            rows = min(LO, quads * QP - g * LO)
            v = acc[:rows, g // 2 * D : g // 2 * D + D]
            if g % 2 == 1:
                v = pltpu.roll(v, H1, axis=1)
            count = acc[:rows, pairs * D + g : pairs * D + g + 1]
            v = jnp.where(lanes < H1, v, jnp.where(lanes == H1, count, 0.0))
            out_ref[g * LO : g * LO + rows, :] = v + base_ref[g * LO : g * LO + rows, :]

        def finish(i, _):
            total = out_ref[pl.ds(pl.multiple_of(i * QP, 8), QP), :]
            count = total[:, H1 : H1 + 1]
            tag = jnp.where((lanes > H1) & (lanes < H1 + 4) & (count > 0.0), total, 0.0)
            tag_ref[i] = tag[:QC, :].astype(BF16)
            return 0

        lax.fori_loop(0, quads, finish, 0, unroll=4)

    shape = jax.ShapeDtypeStruct
    return pl.pallas_call(
        kernel,
        in_specs=[pl.BlockSpec(memory_space=pltpu.SMEM)]
        + [pl.BlockSpec(memory_space=pltpu.VMEM)] * 3,
        out_shape=[shape((quads * QP, D), F32), shape((quads, QC, D), BF16)],
        scratch_shapes=[pltpu.VMEM((16, 3 * D), BF16), pltpu.VMEM((LO, (pairs + 1) * D), F32)],
        compiler_params=pltpu.CompilerParams(vmem_limit_bytes=56 * 1024 * 1024),
        name="encode_points",
    )(held, recv, par, base_rows)


def points_back(recv, held, par, cell_grads):
    sources, _, capacity = recv.shape
    chunk = min(CHUNK, capacity)
    total_rows = cell_grads.shape[0]
    groups = -(-total_rows // LO)

    def kernel(held_ref, recv_ref, par_ref, grad_ref, out_ref, win, table, pout_t, acc):
        bias = unpack_point_in(par_ref, win)
        for g in range(groups):
            rows = min(LO, total_rows - g * LO)
            table[:rows, g * D : g * D + D] = grad_ref[g * LO : g * LO + rows, :].astype(BF16)
            if rows < LO:
                table[rows:, g * D : g * D + D] = jnp.zeros((LO - rows, D), BF16)
        m = jnp.concatenate([par_ref[pl.ds(6, H1), :], jnp.zeros((D - H1, D), F32)], axis=0)
        pout_t[...] = m.T.astype(BF16)
        acc[...] = jnp.zeros((16, D), F32)
        lanes = lane_iota()

        def source(s, _):
            def piece(j, _):
                cols = recv_ref[s, :, pl.ds(pl.multiple_of(j * chunk, chunk), chunk)]
                made = mm_tn(cols, win[...])
                group = made[:, D : 2 * D]
                at = made[:, 2 * D :].astype(jnp.int32)
                place = jnp.concatenate(
                    [one_hot(at == lanes + k * D) for k in range(LO // D)], axis=1
                )
                got = jnp.zeros((chunk, D), F32)
                for g in range(0, groups, 2):
                    both = mm(place, table[:, g * D : min(g + 2, groups) * D])
                    for u in range(both.shape[1] // D):
                        got = jnp.where(group == g + u + 1.0, both[:, u * D : u * D + D], got)
                slope = gelu_parts(made[:, :D] + bias)[1]
                acc[...] += mm(cols, (mm(got.astype(BF16), pout_t[...]) * slope).astype(BF16))
                return 0

            lax.fori_loop(0, (held_ref[s] + chunk - 1) // chunk, piece, 0)
            return 0

        lax.fori_loop(0, sources, source, 0)
        rows = []
        for k in range(6):
            odd = pltpu.roll(acc[2 * k + 1 : 2 * k + 2, :], H1, axis=1)
            rows.append(jnp.where(lanes < H1, acc[2 * k : 2 * k + 1, :], odd))
        rows.append(jnp.zeros((2, D), F32))
        out_ref[...] = jnp.concatenate(rows, axis=0)

    return pl.pallas_call(
        kernel,
        in_specs=[pl.BlockSpec(memory_space=pltpu.SMEM)]
        + [pl.BlockSpec(memory_space=pltpu.VMEM)] * 3,
        out_shape=jax.ShapeDtypeStruct((8, D), F32),
        scratch_shapes=[
            pltpu.VMEM((16, 3 * D), BF16),
            pltpu.VMEM((LO, groups * D), BF16),
            pltpu.VMEM((D, D), BF16),
            pltpu.VMEM((16, D), F32),
        ],
        compiler_params=pltpu.CompilerParams(vmem_limit_bytes=48 * 1024 * 1024),
        name="points_back",
    )(held, recv, par, cell_grads)


def update(total, params, first_moment, second_moment):
    rows = params.shape[0]
    moves = [
        (2 * GRAD_ROWS + 72, 0, 6),
        (2 * GRAD_ROWS, 6, 65),
        (GRAD_ROWS, POINT_ROWS, LAYER_ROWS),
        (0, POINT_ROWS + LAYER_ROWS, LAYER_ROWS),
    ]

    def kernel(tot, par, mom1, mom2, norm_ref, new_par, new1, new2, low, rms, grad):
        for src, dst, length in moves:
            grad[pl.ds(dst, length), :] = tot[pl.ds(src, length), :].astype(F32)
        g = grad[...]
        norm = jnp.sqrt(jnp.sum(g * g))
        norm_ref[0, 0] = norm
        factor = jnp.minimum(1.0, clip_norm / (norm + 1e-06))
        clipped = g * factor
        first = beta_one * mom1[...] + (1.0 - beta_one) * clipped
        second = beta_two * mom2[...] + (1.0 - beta_two) * clipped * clipped
        new1[...] = first
        new2[...] = second
        first_hat = first / (1.0 - beta_one**step_count)
        second_hat = second / (1.0 - beta_two**step_count)
        p = par[...]
        p = p - learn_rate * (first_hat / (jnp.sqrt(second_hat) + adam_eps) + decay_rate * p)
        new_par[...] = p
        low[...] = p.astype(BF16)
        base = 2 * GRAD_ROWS + 80
        stats = tot[base : base + 8, :].astype(F32)
        sums = jnp.sum(stats, axis=1, keepdims=True)
        live = jnp.maximum(sums[6:7], 1.0)
        rms[...] = jnp.broadcast_to(jnp.sqrt(sums / (live * D)), (8, D))

    shape = jax.ShapeDtypeStruct
    flat = shape((rows, D), F32)
    return pl.pallas_call(
        kernel,
        out_specs=[pl.BlockSpec(memory_space=pltpu.SMEM)]
        + [pl.BlockSpec(memory_space=pltpu.VMEM)] * 5,
        out_shape=[shape((1, 1), F32), flat, flat, flat, shape((rows, D), BF16), shape((8, D), F32)],
        scratch_shapes=[pltpu.VMEM((rows, D), F32)],
        compiler_params=pltpu.CompilerParams(vmem_limit_bytes=48 * 1024 * 1024),
        name="update",
    )(total, params, first_moment, second_moment)


def shifted(x, axes, by):
    if len(axes) == 1:
        count = lax.axis_size(axes[0])
        return lax.ppermute(x, axes[0], [(i, (i + by) % count) for i in range(count)])
    tiles, rows = lax.axis_size(axes[0]), lax.axis_size(axes[1])
    pairs = [
        (i * rows + j, (i + by) % tiles * rows + (j + by) % rows)
        for i in range(tiles)
        for j in range(rows)
    ]
    return lax.ppermute(x, axes, pairs)


def exchange(row, col, cor, by):
    return (
        shifted(row, ("tile",), by),
        shifted(col, ("row",), by),
        shifted(cor, ("tile", "row"), by),
    )


def by_quads(grid, quads_x, quads_y):
    trailing = grid.shape[2:]
    grid = grid.reshape((quads_x, QS, quads_y, QS) + trailing)
    return jnp.swapaxes(grid, 1, 2).reshape((quads_x, quads_y, QC) + trailing)


def reduce_all(x):
    tiles, rows = lax.axis_size("tile"), lax.axis_size("row")
    count = tiles * rows
    share = x.shape[0] // count
    parts = lax.all_to_all(
        x.reshape(count, share, D), ("tile", "row"), split_axis=0, concat_axis=0, tiled=True
    )
    mine = jnp.sum(parts.astype(F32), axis=0).astype(x.dtype)
    spread = jnp.broadcast_to(mine[None], (count, share, D))
    return lax.all_to_all(
        spread, ("tile", "row"), split_axis=0, concat_axis=0, tiled=True
    ).reshape(x.shape)


def local(
    point_feats,
    point_tile,
    point_cell,
    point_valid,
    pillar_frame,
    cotangent,
    params,
    first_moment,
    second_moment,
):
    tile_count = lax.axis_size("tile")
    row_count = lax.axis_size("row")
    device_count = tile_count * row_count
    extent_x, extent_y = pillar_frame.shape
    cell_count = extent_x * extent_y
    quads_x, quads_y = extent_x // QS, extent_y // QS
    quads = quads_x * quads_y
    points = point_cell.shape[0]
    capacity = 2 * points // tile_count
    par = params.reshape(-1, D)

    cot = by_quads(cotangent, quads_x, quads_y)
    cot_halos = exchange(cot[0], cot[:, 0], cot[0, :1], -1)

    shape = (points // BLOCK, BLOCK)
    send = bin_points(
        point_feats,
        point_tile.reshape(shape),
        point_cell.reshape(shape),
        point_valid.reshape(shape),
        tile_count,
        capacity,
        extent_y,
        quads_y,
    )
    recv = lax.all_to_all(send, "tile", split_axis=0, concat_axis=0, tiled=True)
    held = jnp.sum(recv[:, 11].astype(jnp.int32), axis=1)

    frames = by_quads(pillar_frame, quads_x, quads_y)
    frames = jnp.pad(frames, ((0, 0), (0, 0), (0, QP - QC)), constant_values=-1).reshape(-1)
    lanes = jnp.arange(D, dtype=jnp.int32)
    base_rows = (frames[:, None] == lanes[None] - (H1 + 1)).astype(F32)
    pillars, tags = encode_points(recv, held, par, base_rows, quads)
    pillars = pillars.reshape(quads_x, quads_y, QP, D)
    tags = tags.reshape(quads_x, quads_y, QC, D)
    tag_halos = exchange(tags[0], tags[:, 0], tags[0, :1], -1)

    first = first_layer(pillars, par, quads_x, quads_y)
    field, saved, sums_one = first[0], first[1:8], first[8]
    halos = exchange(*first[9:], -1)
    flags = jnp.stack(
        [
            (lax.axis_index("tile") == tile_count - 1).astype(jnp.int32),
            (lax.axis_index("row") == row_count - 1).astype(jnp.int32),
        ]
    )
    grads, grad_two, g_row, g_col, g_cor, sums_two = second_layer(
        flags, field, halos, tags, tag_halos, cot, cot_halos, par, 1.0 / (cell_count * device_count)
    )
    grad_halos = exchange(g_row, g_col, g_cor, 1)
    cell_grads, grad_one, grad_pout = first_layer_back(grads, grad_halos, pillars, saved, par)
    grad_pin = points_back(recv, held, par, cell_grads.reshape(quads * QP, D))

    stats = jnp.concatenate(
        [
            jnp.sum(sums_one, axis=1)[:3],
            jnp.sum(sums_two, axis=1)[:3],
            jnp.sum(sums_one, axis=1)[3:] / D,
            jnp.zeros((1, D), F32),
        ],
        axis=0,
    )
    pieces = jnp.concatenate([grad_two, grad_one, grad_pout, grad_pin, stats], axis=0)
    step = device_count * 8
    pieces = jnp.pad(pieces, ((0, -pieces.shape[0] % step), (0, 0)))
    total = reduce_all(pieces)
    norm, new_params, new_first, new_second, low, rms = update(
        total, par, first_moment.reshape(-1, D), second_moment.reshape(-1, D)
    )
    return (
        norm[0, 0],
        new_params.reshape(-1),
        new_first.reshape(-1),
        new_second.reshape(-1),
        low.reshape(-1),
        rms[:6, 0],
    )


def solution(mesh):
    return jax.shard_map(
        local,
        mesh=mesh,
        in_specs=(
            P(None, ("tile", "row")),
            P(("tile", "row"), None),
            P(("tile", "row")),
            P(("tile", "row")),
            P("tile", "row"),
            P("tile", "row", None),
            P(),
            P(),
            P(),
        ),
        out_specs=(P(), P(), P(), P(), P(), P()),
        check_vma=False,
    )
```

time: 1190 us -> 392 us (0.33)
  other arithmetic: 407 us -> 7.19 us
  matrix products: 288 us -> 0 us
  Pallas kernels: 0 us -> 260 us
  local copies, waits for them, and re-layouts: 263 us -> 12.6 us
  waiting for transfers between devices: 135 us -> 21.5 us
  blocking collectives: 38.7 us -> 65.3 us
  between operations: 19.1 us -> 1.11 us
    dot_general x41 -> x0, matrix products: 288 us -> none  [the longest x2 49.6 us: layer_backward(): jnp.einsum('wqhd,wkhd->whqk', grad_mix, packed[:, :, 2], preferred_elemen...]
    pallas_call x0 -> x7, Pallas kernels: none -> 260 us  [the longest x1 83.1 us: second_layer(): pl.pallas_call(kernel, grid=(across * along,), in_specs=[pl.BlockSpec(mem...]
    scatter-add x2 -> x0, other arithmetic: 205 us -> none  [the longest x1 104 us: local(): jax.ops.segment_sum(slot_out.astype(jnp.float32), safe_cells, num_segment...]
    reduce_sum x25 -> x4, other arithmetic: 98.8 us -> 1.67 us  [the longest x1 0.85 us: local(): held = jnp.sum(recv[:, 11].astype(jnp.int32), axis=1)]
    psum x1 -> x0, waiting for transfers between devices: 85.8 us -> none  [local(): lax.psum((flat_rest, flat_two, square_sums, live_total), ('tile', 'row'))]
    gather x2 -> x0, local copies, waits for them, and re-layouts: 82.4 us -> none  [the longest x1 57.8 us: local(): slot_grads = grad_table[safe_cells]]
    convert_element_type x16 -> x1, other arithmetic: 76.5 us -> 3.45 us  [local(): base_rows = (frames[:, None] == lanes[None] - (H1 + 1)).astype(F32)]
    all_to_all x0 -> x2, blocking collectives: none -> 65.3 us  [the longest x1 32.8 us: reduce_all(): lax.all_to_all(x.reshape(count, share, D), ('tile', 'row'), split_axis=0,...]
  transfers between devices with their start and end apart: 12 -> 13, of which waited for: 9 -> 4; matrix products, arithmetic and copies ran while one was open for 36% -> 3% of each run, Pallas kernels for 0% -> 19%
where the time goes in v1:
time: 392 us; the launch traced here: 389 us
  Pallas kernels  260 us (66%)
  blocking collectives  65.3 us (17%)
  starting transfers between devices  21.7 us (6%)
  waiting for transfers between devices  21.5 us (5%)
  local copies, waits for them, and re-layouts  12.6 us (3%)
  other arithmetic  7.19 us (2%)
    pallas_call x1, Pallas kernels, second_layer(): pl.pallas_call(kernel, grid=(across * along,), in_specs=[pl.BlockSpec(mem...  83.1 us
    pallas_call x1, Pallas kernels, first_layer_back(): pl.pallas_call(kernel, grid=(across * along,), in_specs=[whole(grads.shap...  52.2 us
    pallas_call x1, Pallas kernels, first_layer(): pl.pallas_call(kernel, grid=(across * along,), in_specs=[quad_spec, whole...  40.6 us
    pallas_call x1, Pallas kernels, points_back(): pl.pallas_call(kernel, in_specs=[pl.BlockSpec(memory_space=pltpu.SMEM)] +...  37 us
    pallas_call x1, Pallas kernels, encode_points(): pl.pallas_call(kernel, in_specs=[pl.BlockSpec(memory_space=pltpu.SMEM)] +...  34.7 us
    all_to_all x1, blocking collectives, reduce_all(): lax.all_to_all(x.reshape(count, share, D), ('tile', 'row'), split_axis=0,...  32.8 us
    all_to_all x1, blocking collectives, reduce_all(): lax.all_to_all(spread, ('tile', 'row'), split_axis=0, concat_axis=0, tile...  32.5 us
    ppermute x4, waiting for transfers between devices, shifted(): return lax.ppermute(x, axes, pairs)  17.1 us
  transfers between devices with their start and end apart: 13, of which 4 were waited for; matrix products, arithmetic and copies ran while one was open for 3% of the time, Pallas kernels for 19%

profile of v1, /device:TPU:0, one launch (start us, length us, event | category | flops | bytes accessed | tf_op | source)
XLA Modules:
  0.0 388.9 jit_solution(7344024734459218336)
XLA Ops:
  1.1 1.5 reduce.6
  2.6 0.8 reshape.82.cell_ref
  3.4 0.8 reshape.83.valid_ref
  4.2 0.9 copy-done.6
  5.1 8.4 %bin_points.1 = bf16[8,16,2048]{2,1,0:T(8,128)(2,1)} custom-call(bf16[11,8192]{1,0:T(8,128)(2,1)S(1)} %copy-done.6, s32[32,256]{1,0:T(8,128)S(1)} %reshape.81.tile_ref, s32[32,256]{1,0:T(8,128)S(1)} %reshape.82.cell_ref, s32[32,256]{1,0:T(8,128)S(1)} %reshape.83.valid_ref), custom_call_target="tpu_custom_call" | custom-call | tf_op jit(solution)/shard_map/bin_points/pallas_call | solution.py:797
  13.6 7.3 %all-to-all-start = ((bf16[8,16,2048]{2,1,0:T(8,128)(2,1)}), bf16[8,16,2048]{2,1,0:T(8,128)(2,1)S(1)}, u32[]{:S(2)}, u32[]{:S(2)}) async-start(bf16[8,16,2048]{2,1,0:T(8,128)(2,1)} %bin_points.1), calls=%async_computation | async-start | bytes 1048576 | tf_op jit(solution)/shard_map/all_to_all | solution.py:1077
  21.6 0.7 collective-permute-start.7
  22.8 5.1 %collective-permute-start.8 = (bf16[1,36,128]{2,1,0:T(8,128)(2,1)S(1)}, bf16[1,36,128]{2,1,0:T(8,128)(2,1)S(1)}, u32[]{:S(2)}, u32[]{:S(2)}) collective-permute-start(bf16[1,36,128]{2,1,0:T(8,128)(2,1)S(1)} %slice_bitcast_fusion.1), channel_id=1, source_target_pairs={{0,31},{1,28},{2,29},{3,30},{4,3},{5,0},{6,1},{7,2},{8,7},{9,4},{1... | collective-permute-start | bytes 27656 | tf_op jit(solution)/shard_map/ppermute | solution.py:1010
  29.7 3.4 compare_convert_fusion.base_ref
  33.2 3.6 all-to-all-done.recv_ref
  36.8 0.9 fusion.held_ref
  37.6 34.7 %encode_points.1 = (f32[5120,128]{1,0:T(8,128)}, bf16[128,36,128]{2,1,0:T(8,128)(2,1)}) custom-call(s32[8]{0:T(128)} %fusion.held_ref, bf16[8,16,2048]{2,1,0:T(8,128)(2,1)} %copy-done.1, f32[2139,128]{1,0:T(8,128)} %bitcast.32, f32[5120,128]{1,0:T(8,128)} %compare_convert_fusion.base_ref), custom_call_target="tpu_custom_call" | custom-call | tf_op jit(solution)/shard_map/encode_points/pallas_call | solution.py:880
  72.3 0.7 slice_bitcast_fusion.2
  73.0 1.0 slice.36
  74.0 3.2 collective-permute-start.5
  77.2 2.1 collective-permute-start.3
  79.3 40.6 %first_layer.1 = (f32[4,32,40,128]{3,2,1,0:T(8,128)}, bf16[32,144,1152]{2,1,0:T(8,128)(2,1)}, bf16[32,144,384]{2,1,0:T(8,128)(2,1)}, bf16[32,144,128]{2,1,0:T(8,...) custom-call(f32[4,32,40,128]{3,2,1,0:T(8,128)} %bitcast.42, ...), custom_call_target="tpu_custom_call" | custom-call | tf_op jit(solution)/shard_map/first_layer/pallas_call | solution.py:430
  120.0 0.8 slice_bitcast_fusion
  121.8 7.4 %collective-permute-done.2.refs_3_ = bf16[1,36,128]{2,1,0:T(8,128)(2,1)S(1)} collective-permute-done((bf16[1,36,128]{2,1,0:T(8,128)(2,1)}, bf16[1,36,128]{2,1,0:T(8,128)(2,1)S(1)}, u32[]{:S(2)}, u32[]{:S(2)}) %collective-permute-start.2) | collective-permute-done | bytes 9248 | tf_op jit(solution)/shard_map/ppermute | solution.py:1010
  129.2 0.8 collective-permute-done.refs_1_
  130.0 0.7 copy-done.15
  130.7 83.1 %second_layer.1 = (f32[4,32,40,128]{3,2,1,0:T(8,128)}, f32[1040,128]{1,0:T(8,128)}, bf16[32,36,128]{2,1,0:T(8,128)(2,1)}, bf16[4,36,128]{2,1,0:T(8,128)(2,1)}, b...) custom-call(s32[2]{0:T(128)} %add_convert_fusion.flag, f32[4,32,40,128]{3,2,1,0:T(8,128)} %get-tuple-element.36.refs_0_, ...), custom_call_target="tpu_custom_call" | custom-call | tf_op jit(solution)/shard_map/second_layer/pallas_call | solution.py:575
  213.8 2.1 collective-permute-start.9
  216.0 0.7 reduce_sum.42
  216.7 9.7 %collective-permute-done.11.refs_3_ = bf16[1,36,128]{2,1,0:T(8,128)(2,1)S(1)} collective-permute-done((bf16[1,36,128]{2,1,0:T(8,128)(2,1)}, bf16[1,36,128]{2,1,0:T(8,128)(2,1)S(1)}, u32[]{:S(2)}, u32[]{:S(2)}) %collective-permute-start.11) | collective-permute-done | bytes 9248 | tf_op jit(solution)/shard_map/ppermute | solution.py:1010
  227.2 52.2 %first_layer_back.1 = (f32[4,32,40,128]{3,2,1,0:T(8,128)}, f32[1040,128]{1,0:T(8,128)}, f32[72,128]{1,0:T(8,128)}) custom-call(f32[4,32,40,128]{3,2,1,0:T(8,128)} %get-tuple-element.42.refs_0_, bf16[32,36,128]{2,1,0:T(8,128)(2,1)} %copy-done.12, bf16[4,36,128]{2,1,0:T(8,128)(2,1)} %copy-done.16, bf16[1,36,128]{2,1,0:T(8,128)(2,1)} %copy-done.26, ...), custom_call_target="tpu_custom_call" | custom-call | tf_op jit(solution)/shard_map/first_layer_back/pallas_call | solution.py:699
  279.5 1.7 copy-done.3
  281.2 37.0 %points_back.1 = f32[8,128]{1,0:T(8,128)S(1)} custom-call(s32[8]{0:T(128)S(1)} %copy-done.7, bf16[8,16,2048]{2,1,0:T(8,128)(2,1)S(1)} %copy-done.2, f32[2139,128]{1,0:T(8,128)S(1)} %bitcast.36, f32[5120,128]{1,0:T(8,128)S(1)} %bitcast.39), custom_call_target="tpu_custom_call" | custom-call | tf_op jit(solution)/shard_map/points_back/pallas_call | solution.py:938
  318.2 0.8 concatenate.3
  319.2 32.8 %all_to_all.15 = f32[32,72,128]{2,1,0:T(8,128)S(1)} all-to-all(f32[32,72,128]{2,1,0:T(8,128)S(1)} %bitcast.48), channel_id=1, replica_groups=mesh['tile'=8,'row'=4] {'tile','row'}, dimensions={0} | all-to-all | bytes 2359296 | tf_op jit(solution)/shard_map/all_to_all | solution.py:1031
  352.2 32.5 %all_to_all.16 = f32[32,72,128]{2,1,0:T(8,128)S(1)} all-to-all(f32[32,72,128]{2,1,0:T(8,128)S(1)} %broadcast_in_dim.5), channel_id=1, replica_groups=mesh['tile'=8,'row'=4] {'tile','row'}, dimensions={0} | all-to-all | bytes 2359296 | tf_op jit(solution)/shard_map/all_to_all | solution.py:1036
  384.7 3.6 update.1
  (92 shorter events, 6.2 us)
Async XLA Ops:
  4.2 1.0 copy-start.6
  5.1 15.7 %copy-start.9 = (bf16[24,192,128]{2,1,0:T(8,128)(2,1)S(1)}, bf16[24,192,128]{2,1,0:T(8,128)(2,1)}, u32[]{:S(2)}) copy-start(bf16[24,192,128]{2,1,0:T(8,128)(2,1)} %param.14) | copy-start | bytes 3538948
  13.6 23.2 %all-to-all-start = ((bf16[8,16,2048]{2,1,0:T(8,128)(2,1)}), bf16[8,16,2048]{2,1,0:T(8,128)(2,1)S(1)}, u32[]{:S(2)}, u32[]{:S(2)}) async-start(bf16[8,16,2048]{2,1,0:T(8,128)(2,1)} %bin_points.1), calls=%async_computation | async-start | bytes 1048576 | tf_op jit(solution)/shard_map/all_to_all | solution.py:1077
  21.6 99.2 %collective-permute-start.7 = (bf16[4,36,128]{2,1,0:T(8,128)(2,1)S(1)}, bf16[4,36,128]{2,1,0:T(8,128)(2,1)S(1)}, u32[]{:S(2)}, u32[]{:S(2)}) collective-permute-start(bf16[4,36,128]{2,1,0:T(8,128)(2,1)S(1)} %bitcast.55), channel_id=1, source_target_pairs={{0,3},{1,0},{2,1},{3,2},{4,7},{5,4},{6,5},{7,6},{8,11},{9,8},{10,9... | collective-permute-start | bytes 110600 | tf_op jit(solution)/shard_map/ppermute | solution.py:1003
  22.8 5.2 %copy-start.8 = (bf16[4,32,36,128]{3,2,1,0:T(8,128)(2,1)}, bf16[4,32,36,128]{3,2,1,0:T(8,128)(2,1)S(1)}, u32[]{:S(2)}) copy-start(bf16[4,32,36,128]{3,2,1,0:T(8,128)(2,1)S(1)} %copy.30.refs_8_) | copy-start | bytes 3538948
  22.8 6.1 %copy-start.21 = (s32[24,192]{1,0:T(8,128)S(1)}, s32[24,192]{1,0:T(8,128)}, u32[]{:S(2)}) copy-start(s32[24,192]{1,0:T(8,128)} %param.13) | copy-start | bytes 55300
  22.8 97.0 %collective-permute-start.8 = (bf16[1,36,128]{2,1,0:T(8,128)(2,1)S(1)}, bf16[1,36,128]{2,1,0:T(8,128)(2,1)S(1)}, u32[]{:S(2)}, u32[]{:S(2)}) collective-permute-start(bf16[1,36,128]{2,1,0:T(8,128)(2,1)S(1)} %slice_bitcast_fusion.1), channel_id=1, source_target_pairs={{0,31},{1,28},{2,29},{3,30},{4,3},{5,0},{6,1},{7,2},{8,7},{9,4},{1... | collective-permute-start | bytes 27656 | tf_op jit(solution)/shard_map/ppermute | solution.py:1010
  28.2 92.6 %collective-permute-start.6 = (bf16[32,36,128]{2,1,0:T(8,128)(2,1)S(1)}, bf16[32,36,128]{2,1,0:T(8,128)(2,1)S(1)}, u32[]{:S(2)}, u32[]{:S(2)}) collective-permute-start(bf16[32,36,128]{2,1,0:T(8,128)(2,1)S(1)} %copy.27), channel_id=1, source_target_pairs={{0,28},{4,0},{8,4},{12,8},{16,12},{20,16},{24,20},{28,24},{1,29},{... | collective-permute-start | bytes 884744 | tf_op jit(solution)/shard_map/ppermute | solution.py:1003
  36.8 0.9 copy-start.1
  74.0 46.9 %collective-permute-start.5 = (bf16[1,36,128]{2,1,0:T(8,128)(2,1)S(1)}, bf16[1,36,128]{2,1,0:T(8,128)(2,1)S(1)}, u32[]{:S(2)}, u32[]{:S(2)}) collective-permute-start(bf16[1,36,128]{2,1,0:T(8,128)(2,1)S(1)} %slice_bitcast_fusion.2), channel_id=1, source_target_pairs={{0,31},{1,28},{2,29},{3,30},{4,3},{5,0},{6,1},{7,2},{8,7},{9,4},{1... | collective-permute-start | bytes 27656 | tf_op jit(solution)/shard_map/ppermute | solution.py:1010
  77.2 52.0 %collective-permute-start.3 = (bf16[32,36,128]{2,1,0:T(8,128)(2,1)S(1)}, bf16[32,36,128]{2,1,0:T(8,128)(2,1)S(1)}, u32[]{:S(2)}, u32[]{:S(2)}) collective-permute-start(bf16[32,36,128]{2,1,0:T(8,128)(2,1)S(1)} %slice.36), channel_id=1, source_target_pairs={{0,28},{4,0},{8,4},{12,8},{16,12},{20,16},{24,20},{28,24},{1,29},{... | collective-permute-start | bytes 884744 | tf_op jit(solution)/shard_map/ppermute | solution.py:1003
  119.9 10.1 %copy-start.23 = (bf16[1,36,128]{2,1,0:T(8,128)(2,1)}, bf16[1,36,128]{2,1,0:T(8,128)(2,1)S(1)}, u32[]{:S(2)}) copy-start(bf16[1,36,128]{2,1,0:T(8,128)(2,1)S(1)} %collective-permute-done.8.refs_11_) | copy-start | bytes 27652
  119.9 10.0 %collective-permute-start = (bf16[32,36,128]{2,1,0:T(8,128)(2,1)}, bf16[32,36,128]{2,1,0:T(8,128)(2,1)S(1)}, u32[]{:S(2)}, u32[]{:S(2)}) collective-permute-start(bf16[32,36,128]{2,1,0:T(8,128)(2,1)} %get-tuple-element.37), channel_id=1, source_target_pairs={{0,28},{4,0},{8,4},{12,8},{16,12},{20,16},{24,20},{28,24},{1,29},{... | collective-permute-start | bytes 884744 | tf_op jit(solution)/shard_map/ppermute | solution.py:1003
  120.8 9.2 %copy-start.17 = (bf16[4,36,128]{2,1,0:T(8,128)(2,1)}, bf16[4,36,128]{2,1,0:T(8,128)(2,1)S(1)}, u32[]{:S(2)}) copy-start(bf16[4,36,128]{2,1,0:T(8,128)(2,1)S(1)} %collective-permute-done.7.refs_10_) | copy-start | bytes 110596
  120.8 8.4 %collective-permute-start.4 = (bf16[4,36,128]{2,1,0:T(8,128)(2,1)S(1)}, bf16[4,36,128]{2,1,0:T(8,128)(2,1)S(1)}, u32[]{:S(2)}, u32[]{:S(2)}) collective-permute-start(bf16[4,36,128]{2,1,0:T(8,128)(2,1)S(1)} %slice_bitcast_fusion), channel_id=1, source_target_pairs={{0,3},{1,0},{2,1},{3,2},{4,7},{5,4},{6,5},{7,6},{8,11},{9,8},{10,9... | collective-permute-start | bytes 110600 | tf_op jit(solution)/shard_map/ppermute | solution.py:1003
  120.8 9.1 %copy-start.13 = (bf16[32,36,128]{2,1,0:T(8,128)(2,1)}, bf16[32,36,128]{2,1,0:T(8,128)(2,1)S(1)}, u32[]{:S(2)}) copy-start(bf16[32,36,128]{2,1,0:T(8,128)(2,1)S(1)} %collective-permute-done.6.refs_9_) | copy-start | bytes 884740
  120.9 8.3 %collective-permute-start.2 = (bf16[1,36,128]{2,1,0:T(8,128)(2,1)}, bf16[1,36,128]{2,1,0:T(8,128)(2,1)S(1)}, u32[]{:S(2)}, u32[]{:S(2)}) collective-permute-start(bf16[1,36,128]{2,1,0:T(8,128)(2,1)} %get-tuple-element.39), channel_id=1, source_target_pairs={{0,31},{1,28},{2,29},{3,30},{4,3},{5,0},{6,1},{7,2},{8,7},{9,4},{1... | collective-permute-start | bytes 27656 | tf_op jit(solution)/shard_map/ppermute | solution.py:1010
  120.9 9.0 %copy-start.24 = (bf16[1,36,128]{2,1,0:T(8,128)(2,1)}, bf16[1,36,128]{2,1,0:T(8,128)(2,1)S(1)}, u32[]{:S(2)}) copy-start(bf16[1,36,128]{2,1,0:T(8,128)(2,1)S(1)} %collective-permute-done.5.refs_7_) | copy-start | bytes 27652
  120.9 8.2 %collective-permute-start.1 = (bf16[4,36,128]{2,1,0:T(8,128)(2,1)}, bf16[4,36,128]{2,1,0:T(8,128)(2,1)S(1)}, u32[]{:S(2)}, u32[]{:S(2)}) collective-permute-start(bf16[4,36,128]{2,1,0:T(8,128)(2,1)} %get-tuple-element.38), channel_id=1, source_target_pairs={{0,3},{1,0},{2,1},{3,2},{4,7},{5,4},{6,5},{7,6},{8,11},{9,8},{10,9... | collective-permute-start | bytes 110600 | tf_op jit(solution)/shard_map/ppermute | solution.py:1003
  130.7 85.2 %copy-start.22 = (f32[4,8,128]{2,1,0:T(8,128)S(1)}, f32[4,8,128]{2,1,0:T(8,128)}, u32[]{:S(2)}) copy-start(f32[4,8,128]{2,1,0:T(8,128)} %get-tuple-element.56) | copy-start | bytes 49156
  213.8 12.7 %collective-permute-start.9 = (bf16[32,36,128]{2,1,0:T(8,128)(2,1)}, bf16[32,36,128]{2,1,0:T(8,128)(2,1)S(1)}, u32[]{:S(2)}, u32[]{:S(2)}) collective-permute-start(bf16[32,36,128]{2,1,0:T(8,128)(2,1)} %get-tuple-element.43), channel_id=1, source_target_pairs={{0,4},{4,8},{8,12},{12,16},{16,20},{20,24},{24,28},{28,0},{1,5},{5... | collective-permute-start | bytes 884744 | tf_op jit(solution)/shard_map/ppermute | solution.py:1003
  215.9 10.6 %collective-permute-start.11 = (bf16[1,36,128]{2,1,0:T(8,128)(2,1)}, bf16[1,36,128]{2,1,0:T(8,128)(2,1)S(1)}, u32[]{:S(2)}, u32[]{:S(2)}) collective-permute-start(bf16[1,36,128]{2,1,0:T(8,128)(2,1)} %get-tuple-element.45), channel_id=1, source_target_pairs={{0,5},{1,6},{2,7},{3,4},{4,9},{5,10},{6,11},{7,8},{8,13},{9,14},{1... | collective-permute-start | bytes 27656 | tf_op jit(solution)/shard_map/ppermute | solution.py:1010
  215.9 10.6 %collective-permute-start.10 = (bf16[4,36,128]{2,1,0:T(8,128)(2,1)}, bf16[4,36,128]{2,1,0:T(8,128)(2,1)S(1)}, u32[]{:S(2)}, u32[]{:S(2)}) collective-permute-start(bf16[4,36,128]{2,1,0:T(8,128)(2,1)} %get-tuple-element.44), channel_id=1, source_target_pairs={{0,1},{1,2},{2,3},{3,0},{4,5},{5,6},{6,7},{7,4},{8,9},{9,10},{10,1... | collective-permute-start | bytes 110600 | tf_op jit(solution)/shard_map/ppermute | solution.py:1003
  227.2 52.2 %copy-start = (f32[273792]{0:T(1024)S(1)}, f32[273792]{0:T(1024)}, u32[]{:S(2)}) copy-start(f32[273792]{0:T(1024)} %param.15) | copy-start | bytes 3285508
  227.2 52.2 %copy-start.2 = (bf16[8,16,2048]{2,1,0:T(8,128)(2,1)S(1)}, bf16[8,16,2048]{2,1,0:T(8,128)(2,1)}, u32[]{:S(2)}) copy-start(bf16[8,16,2048]{2,1,0:T(8,128)(2,1)} %copy-done.1) | copy-start | bytes 1572868
  227.2 52.3 %copy-start.7 = (s32[8]{0:T(128)S(1)}, s32[8]{0:T(128)}, u32[]{:S(2)}) copy-start(s32[8]{0:T(128)} %fusion.held_ref) | copy-start | bytes 100
  279.5 1.7 copy-start.3
  281.2 37.0 %copy-start.10 = (f32[1040,128]{1,0:T(8,128)S(1)}, f32[1040,128]{1,0:T(8,128)}, u32[]{:S(2)}) copy-start(f32[1040,128]{1,0:T(8,128)} %get-tuple-element.41) | copy-start | bytes 1597444
  281.2 37.0 %copy-start.11 = (f32[1040,128]{1,0:T(8,128)S(1)}, f32[1040,128]{1,0:T(8,128)}, u32[]{:S(2)}) copy-start(f32[1040,128]{1,0:T(8,128)} %get-tuple-element.53) | copy-start | bytes 1597444
  281.2 37.0 %copy-start.20 = (f32[72,128]{1,0:T(8,128)S(1)}, f32[72,128]{1,0:T(8,128)}, u32[]{:S(2)}) copy-start(f32[72,128]{1,0:T(8,128)} %get-tuple-element.54) | copy-start | bytes 110596
  352.2 32.5 %copy-start.4 = (f32[273792]{0:T(1024)S(1)}, f32[273792]{0:T(1024)}, u32[]{:S(2)}) copy-start(f32[273792]{0:T(1024)} %param.16) | copy-start | bytes 3285508
  352.2 32.5 %copy-start.5 = (f32[273792]{0:T(1024)S(1)}, f32[273792]{0:T(1024)}, u32[]{:S(2)}) copy-start(f32[273792]{0:T(1024)} %param.17) | copy-start | bytes 3285508
  (8 other events, 6.0 us)

commit v2 on v1

--- a/solution.py
+++ b/solution.py
@@ -301,7 +301,7 @@
         ref[...] = jnp.zeros(ref.shape, ref.dtype)
 
 
-def store_grads(acc, out):
+def store_grads(acc, sums, out):
     for part in range(3):
         out[pl.ds(part, D, stride=3), :] = acc["qkv"][:, part * D : (part + 1) * D]
     out[pl.ds(384, D), :] = acc["out"][...]
@@ -310,7 +310,8 @@
     out[pl.ds(768, FF), :] = acc["fout"][...]
     out[pl.ds(1024, 16), :] = jnp.concatenate(
         [jnp.sum(acc["vec"][i], axis=0, keepdims=True) for i in range(10)]
-        + [jnp.zeros((6, D), F32)],
+        + [jnp.sum(sums[i], axis=0, keepdims=True) for i in range(4)]
+        + [jnp.zeros((2, D), F32)],
         axis=0,
     )
 
@@ -340,6 +341,10 @@
     return pltpu.CompilerParams(
         dimension_semantics=("arbitrary",), vmem_limit_bytes=limit * 1024 * 1024
     )
+
+
+def cost_of(flops):
+    return pl.CostEstimate(flops=flops, bytes_accessed=1 << 24, transcendentals=0)
 
 
 def first_layer(pillars, par, quads_x, quads_y):
@@ -470,7 +475,7 @@
     )(pillars, par)
 
 
-def second_layer(flags, field, halos, tags, tag_halos, cot, cot_halos, par, scale):
+def second_layer(flags, field, halos, tags, tag_halos, cot, cot_halos, par, scale, grad_rows):
     quads_x, quads_y = field.shape[:2]
     across = quads_x // 2
     along = quads_y // (2 * NW)
@@ -480,9 +485,9 @@
 
     def kernel(flag, *refs):
         ins, refs = refs[:13], refs[13:]
-        outs, scratch = refs[:6], refs[6:]
+        outs, scratch = refs[:5], refs[5:]
         fields, tagss, cots, par_ref = ins[:4], ins[4:8], ins[8:12], ins[12]
-        grads, weights, row_out, col_out, cor_out, sums_out = outs
+        grads, weights, row_out, col_out, cor_out = outs
         w = dict(zip(wnames, scratch))
         scratch = scratch[len(wnames) :]
         acc = dict(zip(anames, scratch))
@@ -565,8 +570,7 @@
         @pl.when(step == pl.num_programs(0) - 1)
         def _():
             cor_out[0] = grads[1, 2 * NW - 1, :QC, :].astype(BF16)
-            sums_out[...] = sums[...]
-            store_grads(acc, weights)
+            store_grads(acc, sums, weights)
 
     shape = jax.ShapeDtypeStruct
     quad_spec = pl.BlockSpec((2, 2 * NW, QP, D), lambda s: (s // along, s % along, 0, 0))
@@ -578,21 +582,19 @@
         in_specs=[pl.BlockSpec(memory_space=pltpu.SMEM)] + [whole(v.shape) for v in arrays],
         out_specs=[
             quad_spec,
-            whole((GRAD_ROWS, D)),
+            whole((grad_rows, D)),
             pl.BlockSpec(
                 (2 * NW, QC, D), lambda s: (jnp.maximum(s - (across - 1) * along, 0), 0, 0)
             ),
             pl.BlockSpec((2, QC, D), lambda s: (s // along, 0, 0)),
             whole((1, QC, D)),
-            whole((4, 8, D)),
         ],
         out_shape=[
             shape((quads_x, quads_y, QP, D), F32),
-            shape((GRAD_ROWS, D), F32),
+            shape((grad_rows, D), F32),
             shape((quads_y, QC, D), BF16),
             shape((quads_x, QC, D), BF16),
             shape((1, QC, D), BF16),
-            shape((4, 8, D), F32),
         ],
         scratch_shapes=[pltpu.VMEM(WEIGHT_SHAPES[n], BF16) for n in wnames]
         + [pltpu.VMEM(ACC_SHAPES[n], F32) for n in anames]
@@ -608,7 +610,7 @@
     )(flags, *arrays)
 
 
-def first_layer_back(grads, halos, pillars, saved, par):
+def first_layer_back(grads, halos, pillars, saved, sums, par, grad_rows):
     quads_x, quads_y = grads.shape[:2]
     across = quads_x // 2
     along = quads_y // (2 * NW)
@@ -617,16 +619,16 @@
     anames = list(ACC_SHAPES)
 
     def kernel(*refs):
-        ins, refs = refs[:13], refs[13:]
-        outs, scratch = refs[:3], refs[3:]
+        ins, refs = refs[:14], refs[14:]
+        outs, scratch = refs[:2], refs[2:]
         main, row, col, cor, pil = ins[:5]
         probs, packed, mix, first, second, low, live = ins[5:12]
-        par_ref = ins[12]
-        cell_out, weights, point_weights = outs
+        sums_ref, par_ref = ins[12:]
+        cell_out, weights = outs
         w = dict(zip(wnames, scratch))
         scratch = scratch[len(wnames) :]
         acc = dict(zip(anames, scratch))
-        wide, ext, pacc = scratch[len(anames) :]
+        wide, ext, pout_t, pacc = scratch[len(anames) :]
         step = pl.program_id(0)
         a = step // along
         b = step % along
@@ -636,6 +638,8 @@
             load_layer(par_ref, base, w)
             clear(acc)
             pacc[...] = jnp.zeros(pacc.shape, F32)
+            m = par_ref[pl.ds(6, H1), :]
+            pout_t[...] = jnp.concatenate([m, m], axis=0).T.astype(BF16)
             for r in range(1, quads_x):
 
                 def one(i, _):
@@ -684,12 +688,12 @@
             cell_out[r, c, :QC, :] = v
             cell_out[r, c, QC:, :] = jnp.zeros((QP - QC, D), F32)
 
-        spread_windows(wide, g_pillar.astype(F32), put)
+        spread_windows(wide, mm(g_pillar, pout_t[...]), put)
 
         @pl.when(step == pl.num_programs(0) - 1)
         def _():
-            store_grads(acc, weights)
-            point_weights[...] = pacc[:72, :]
+            store_grads(acc, sums_ref, weights)
+            weights[GRAD_ROWS : GRAD_ROWS + 72, :] = pacc[:72, :]
 
     def win_spec(width):
         return pl.BlockSpec((NW, SLOTS, width), lambda s: (s, 0, 0))
@@ -703,23 +707,21 @@
         + [whole(v.shape) for v in halos]
         + [quad_spec]
         + [win_spec(v.shape[2]) for v in saved]
-        + [whole(par.shape)],
-        out_specs=[quad_spec, whole((GRAD_ROWS, D)), whole((72, D))],
-        out_shape=[
-            shape((quads_x, quads_y, QP, D), F32),
-            shape((GRAD_ROWS, D), F32),
-            shape((72, D), F32),
-        ],
+        + [whole(sums.shape), whole(par.shape)],
+        out_specs=[quad_spec, whole((grad_rows, D))],
+        out_shape=[shape((quads_x, quads_y, QP, D), F32), shape((grad_rows, D), F32)],
         scratch_shapes=[pltpu.VMEM(WEIGHT_SHAPES[n], BF16) for n in wnames]
         + [pltpu.VMEM(ACC_SHAPES[n], F32) for n in anames]
         + [
             pltpu.VMEM((NW * SLOTS, D), F32),
             pltpu.VMEM((quads_x, quads_y, QP, D), F32),
+            pltpu.VMEM((D, D), BF16),
             pltpu.VMEM((D, D), F32),
         ],
         compiler_params=params_for(),
+        cost_estimate=cost_of(grads.size * 12000),
         name="first_layer_back",
-    )(grads, *halos, pillars, *saved, par)
+    )(grads, *halos, pillars, *saved, sums, par)
 
 
 def one_hot(hit):
@@ -893,47 +895,53 @@
     chunk = min(CHUNK, capacity)
     total_rows = cell_grads.shape[0]
     groups = -(-total_rows // LO)
-
-    def kernel(held_ref, recv_ref, par_ref, grad_ref, out_ref, win, table, pout_t, acc):
+    pairs = -(-groups // 2)
+
+    def kernel(held_ref, recv_ref, par_ref, grad_ref, out_ref, win, table, acc):
         bias = unpack_point_in(par_ref, win)
-        for g in range(groups):
-            rows = min(LO, total_rows - g * LO)
-            table[:rows, g * D : g * D + D] = grad_ref[g * LO : g * LO + rows, :].astype(BF16)
-            if rows < LO:
-                table[rows:, g * D : g * D + D] = jnp.zeros((LO - rows, D), BF16)
-        m = jnp.concatenate([par_ref[pl.ds(6, H1), :], jnp.zeros((D - H1, D), F32)], axis=0)
-        pout_t[...] = m.T.astype(BF16)
+        lanes = lane_iota()
+
+        def rows_of(g):
+            rows = max(0, min(LO, total_rows - g * LO))
+            got = [grad_ref[g * LO : g * LO + rows, :]] if rows else []
+            return jnp.concatenate(got + [jnp.zeros((LO - rows, D), F32)], axis=0) if rows < LO else got[0]
+
+        for j in range(pairs):
+            table[:, j * D : j * D + D] = jnp.where(
+                lanes < H1, rows_of(2 * j), rows_of(2 * j + 1)
+            ).astype(BF16)
         acc[...] = jnp.zeros((16, D), F32)
-        lanes = lane_iota()
+        own = jnp.where(lanes < H1, 1.0, 2.0)
+        spot = lanes.astype(F32)
 
         def source(s, _):
             def piece(j, _):
                 cols = recv_ref[s, :, pl.ds(pl.multiple_of(j * chunk, chunk), chunk)]
                 made = mm_tn(cols, win[...])
                 group = made[:, D : 2 * D]
-                at = made[:, 2 * D :].astype(jnp.int32)
-                place = jnp.concatenate(
-                    [one_hot(at == lanes + k * D) for k in range(LO // D)], axis=1
-                )
+                at = made[:, 2 * D :]
+                place = jnp.concatenate([one_hot(at == spot + k * D) for k in range(LO // D)], axis=1)
                 got = jnp.zeros((chunk, D), F32)
-                for g in range(0, groups, 2):
-                    both = mm(place, table[:, g * D : min(g + 2, groups) * D])
+                for p in range(0, pairs, 2):
+                    both = mm(place, table[:, p * D : min(p + 2, pairs) * D])
                     for u in range(both.shape[1] // D):
-                        got = jnp.where(group == g + u + 1.0, both[:, u * D : u * D + D], got)
+                        got = jnp.where(
+                            group == own + 2.0 * (p + u), both[:, u * D : u * D + D], got
+                        )
                 slope = gelu_parts(made[:, :D] + bias)[1]
-                acc[...] += mm(cols, (mm(got.astype(BF16), pout_t[...]) * slope).astype(BF16))
+                acc[...] += mm(cols, (got * slope).astype(BF16))
                 return 0
 
             lax.fori_loop(0, (held_ref[s] + chunk - 1) // chunk, piece, 0)
             return 0
 
         lax.fori_loop(0, sources, source, 0)
-        rows = []
-        for k in range(6):
-            odd = pltpu.roll(acc[2 * k + 1 : 2 * k + 2, :], H1, axis=1)
-            rows.append(jnp.where(lanes < H1, acc[2 * k : 2 * k + 1, :], odd))
-        rows.append(jnp.zeros((2, D), F32))
-        out_ref[...] = jnp.concatenate(rows, axis=0)
+        both = acc[...] + pltpu.roll(acc[...], H1, axis=1)
+        rows = [
+            jnp.where(lanes < H1, both[2 * k : 2 * k + 1, :], both[2 * k + 1 : 2 * k + 2, :])
+            for k in range(6)
+        ]
+        out_ref[...] = jnp.concatenate(rows + [jnp.zeros((2, D), F32)], axis=0)
 
     return pl.pallas_call(
         kernel,
@@ -942,27 +950,36 @@
         out_shape=jax.ShapeDtypeStruct((8, D), F32),
         scratch_shapes=[
             pltpu.VMEM((16, 3 * D), BF16),
-            pltpu.VMEM((LO, groups * D), BF16),
-            pltpu.VMEM((D, D), BF16),
+            pltpu.VMEM((LO, pairs * D), BF16),
             pltpu.VMEM((16, D), F32),
         ],
         compiler_params=pltpu.CompilerParams(vmem_limit_bytes=48 * 1024 * 1024),
+        cost_estimate=cost_of(recv.size * 100000),
         name="points_back",
     )(held, recv, par, cell_grads)
 
 
-def update(total, params, first_moment, second_moment):
+def update(shares, params, first_moment, second_moment):
     rows = params.shape[0]
+    count = shares.shape[0]
+    share = (shares.shape[1] - 16) // 2
     moves = [
-        (2 * GRAD_ROWS + 72, 0, 6),
-        (2 * GRAD_ROWS, 6, 65),
-        (GRAD_ROWS, POINT_ROWS, LAYER_ROWS),
-        (0, POINT_ROWS + LAYER_ROWS, LAYER_ROWS),
+        (1, GRAD_ROWS, 6, 65),
+        (1, 0, POINT_ROWS, LAYER_ROWS),
+        (0, 0, POINT_ROWS + LAYER_ROWS, LAYER_ROWS),
     ]
 
-    def kernel(tot, par, mom1, mom2, norm_ref, new_par, new1, new2, low, rms, grad):
-        for src, dst, length in moves:
-            grad[pl.ds(dst, length), :] = tot[pl.ds(src, length), :].astype(F32)
+    def kernel(got, par, mom1, mom2, norm_ref, new_par, new1, new2, low, rms, two, one, grad):
+        def unpack(s, point):
+            v = got[s].astype(F32)
+            at = pl.multiple_of(s * share, 8)
+            two[pl.ds(at, share), :] = v[:share]
+            one[pl.ds(at, share), :] = v[share : 2 * share]
+            return point + v[2 * share : 2 * share + 8]
+
+        grad[0:8, :] = lax.fori_loop(0, count, unpack, jnp.zeros((8, D), F32), unroll=4)
+        for which, src, dst, length in moves:
+            grad[pl.ds(dst, length), :] = (two, one)[which][pl.ds(src, length), :]
         g = grad[...]
         norm = jnp.sqrt(jnp.sum(g * g))
         norm_ref[0, 0] = norm
@@ -978,11 +995,12 @@
         p = p - learn_rate * (first_hat / (jnp.sqrt(second_hat) + adam_eps) + decay_rate * p)
         new_par[...] = p
         low[...] = p.astype(BF16)
-        base = 2 * GRAD_ROWS + 80
-        stats = tot[base : base + 8, :].astype(F32)
+        stats = jnp.concatenate(
+            [one[LAYER_ROWS : LAYER_ROWS + 3, :], two[LAYER_ROWS : LAYER_ROWS + 5, :]], axis=0
+        )
+        live = jnp.sum(one[LAYER_ROWS + 3 : LAYER_ROWS + 4, :], axis=1, keepdims=True)
         sums = jnp.sum(stats, axis=1, keepdims=True)
-        live = jnp.maximum(sums[6:7], 1.0)
-        rms[...] = jnp.broadcast_to(jnp.sqrt(sums / (live * D)), (8, D))
+        rms[...] = jnp.broadcast_to(jnp.sqrt(sums / jnp.maximum(live, D)), (8, D))
 
     shape = jax.ShapeDtypeStruct
     flat = shape((rows, D), F32)
@@ -991,10 +1009,10 @@
         out_specs=[pl.BlockSpec(memory_space=pltpu.SMEM)]
         + [pl.BlockSpec(memory_space=pltpu.VMEM)] * 5,
         out_shape=[shape((1, 1), F32), flat, flat, flat, shape((rows, D), BF16), shape((8, D), F32)],
-        scratch_shapes=[pltpu.VMEM((rows, D), F32)],
+        scratch_shapes=[pltpu.VMEM((count * share, D), F32)] * 2 + [pltpu.VMEM((rows, D), F32)],
         compiler_params=pltpu.CompilerParams(vmem_limit_bytes=48 * 1024 * 1024),
         name="update",
-    )(total, params, first_moment, second_moment)
+    )(shares, params, first_moment, second_moment)
 
 
 def shifted(x, axes, by):
@@ -1024,18 +1042,12 @@
     return jnp.swapaxes(grid, 1, 2).reshape((quads_x, quads_y, QC) + trailing)
 
 
-def reduce_all(x):
-    tiles, rows = lax.axis_size("tile"), lax.axis_size("row")
-    count = tiles * rows
-    share = x.shape[0] // count
-    parts = lax.all_to_all(
-        x.reshape(count, share, D), ("tile", "row"), split_axis=0, concat_axis=0, tiled=True
-    )
-    mine = jnp.sum(parts.astype(F32), axis=0).astype(x.dtype)
-    spread = jnp.broadcast_to(mine[None], (count, share, D))
-    return lax.all_to_all(
-        spread, ("tile", "row"), split_axis=0, concat_axis=0, tiled=True
-    ).reshape(x.shape)
+def all_to_all(x):
+    return lax.all_to_all(x, ("tile", "row"), split_axis=0, concat_axis=0, tiled=True)
+
+
+def scatter_sum(x, count):
+    return jnp.sum(all_to_all(x.reshape(count, x.shape[0] // count, D)), axis=0)
 
 
 def local(
@@ -1095,26 +1107,31 @@
             (lax.axis_index("row") == row_count - 1).astype(jnp.int32),
         ]
     )
-    grads, grad_two, g_row, g_col, g_cor, sums_two = second_layer(
-        flags, field, halos, tags, tag_halos, cot, cot_halos, par, 1.0 / (cell_count * device_count)
-    )
-    grad_halos = exchange(g_row, g_col, g_cor, 1)
-    cell_grads, grad_one, grad_pout = first_layer_back(grads, grad_halos, pillars, saved, par)
+    step = device_count * 8
+    grad_rows = -(-(GRAD_ROWS + 72) // step) * step
+    grads, grad_two, g_row, g_col, g_cor = second_layer(
+        flags,
+        field,
+        halos,
+        tags,
+        tag_halos,
+        cot,
+        cot_halos,
+        par,
+        1.0 / (cell_count * device_count),
+        grad_rows,
+    )
+    grad_two, grad_halos = lax.optimization_barrier((grad_two, exchange(g_row, g_col, g_cor, 1)))
+    sum_two = scatter_sum(grad_two, device_count)
+    cell_grads, grad_one = first_layer_back(
+        grads, grad_halos, pillars, saved, sums_one, par, grad_rows
+    )
+    grad_one, sum_two = lax.optimization_barrier((grad_one, sum_two))
+    sum_one = scatter_sum(grad_one, device_count)
     grad_pin = points_back(recv, held, par, cell_grads.reshape(quads * QP, D))
-
-    stats = jnp.concatenate(
-        [
-            jnp.sum(sums_one, axis=1)[:3],
-            jnp.sum(sums_two, axis=1)[:3],
-            jnp.sum(sums_one, axis=1)[3:] / D,
-            jnp.zeros((1, D), F32),
-        ],
-        axis=0,
-    )
-    pieces = jnp.concatenate([grad_two, grad_one, grad_pout, grad_pin, stats], axis=0)
-    step = device_count * 8
-    pieces = jnp.pad(pieces, ((0, -pieces.shape[0] % step), (0, 0)))
-    total = reduce_all(pieces)
+    share = jnp.concatenate([sum_two, sum_one, grad_pin, jnp.zeros((8, D), F32)], axis=0)
+    share = share.astype(BF16)
+    total = all_to_all(jnp.broadcast_to(share[None], (device_count,) + share.shape))
     norm, new_params, new_first, new_second, low, rms = update(
         total, par, first_moment.reshape(-1, D), second_moment.reshape(-1, D)
     )

time: 392 us -> 350 us (0.89); the launches traced: 389 us -> 352 us
  blocking collectives: 65.3 us -> 29.2 us
  starting transfers between devices: 21.7 us -> 41.2 us
  Pallas kernels: 260 us -> 244 us
    all_to_all x2 -> x1, blocking collectives: 65.3 us -> 29.2 us  [all_to_all(): lax.all_to_all(x, ('tile', 'row'), split_axis=0, concat_axis=0, tiled=True)]
    pallas_call x1, Pallas kernels: 37 us -> 24.5 us  [points_back(): pl.pallas_call(kernel, in_specs=[pl.BlockSpec(memory_space=pltpu.SMEM)] +...]
    all_to_all x0 -> x2, starting transfers between devices: none -> 9.49 us  [all_to_all(): lax.all_to_all(x, ('tile', 'row'), split_axis=0, concat_axis=0, tiled=True)]
    ppermute x8, starting transfers between devices: 5.95 us -> 14.2 us  [shifted(): lax.ppermute(x, axes[0], [(i, (i + by) % count) for i in range(count)])]
  transfers between devices with their start and end apart: 13 -> 15, of which waited for: 4 -> 4; matrix products, arithmetic and copies ran while one was open for 3% -> 3% of each run, Pallas kernels for 19% -> 42%
where the time goes in v2:
time: 350 us; the launch traced here: 352 us
  Pallas kernels  244 us (70%)
  starting transfers between devices  41.2 us (12%)
  blocking collectives  29.2 us (8%)
  waiting for transfers between devices  18.6 us (5%)
  local copies, waits for them, and re-layouts  11.1 us (3%)
  other arithmetic  6.59 us (2%)
    pallas_call x1, Pallas kernels, second_layer(): pl.pallas_call(kernel, grid=(across * along,), in_specs=[pl.BlockSpec(mem...  83.1 us
    pallas_call x1, Pallas kernels, first_layer_back(): pl.pallas_call(kernel, grid=(across * along,), in_specs=[whole(grads.shap...  51.3 us
    pallas_call x1, Pallas kernels, first_layer(): pl.pallas_call(kernel, grid=(across * along,), in_specs=[quad_spec, whole...  40.6 us
    pallas_call x1, Pallas kernels, encode_points(): pl.pallas_call(kernel, in_specs=[pl.BlockSpec(memory_space=pltpu.SMEM)] +...  32.6 us
    all_to_all x1, blocking collectives, all_to_all(): lax.all_to_all(x, ('tile', 'row'), split_axis=0, concat_axis=0, tiled=True)  29.2 us
    pallas_call x1, Pallas kernels, points_back(): pl.pallas_call(kernel, in_specs=[pl.BlockSpec(memory_space=pltpu.SMEM)] +...  24.5 us
    ppermute x4, waiting for transfers between devices, shifted(): return lax.ppermute(x, axes, pairs)  15.1 us
    ppermute x8, starting transfers between devices, shifted(): lax.ppermute(x, axes[0], [(i, (i + by) % count) for i in range(count)])  14.2 us
  transfers between devices with their start and end apart: 15, of which 4 were waited for; matrix products, arithmetic and copies ran while one was open for 3% of the time, Pallas kernels for 42%

profile of v2, /device:TPU:0, one launch (start us, length us, event | category | flops | bytes accessed | tf_op | source)
XLA Modules:
  0.0 352.1 jit_solution(2915642732499431611)
XLA Ops:
  1.1 1.5 reduce.6
  2.6 0.8 reshape.107.cell_ref
  3.4 0.8 reshape.108.valid_ref
  4.2 0.9 copy-done.5
  5.1 8.4 %bin_points.1 = bf16[8,16,2048]{2,1,0:T(8,128)(2,1)} custom-call(bf16[11,8192]{1,0:T(8,128)(2,1)S(1)} %copy-done.5, s32[32,256]{1,0:T(8,128)S(1)} %reshape.106.tile_ref, s32[32,256]{1,0:T(8,128)S(1)} %reshape.107.cell_ref, s32[32,256]{1,0:T(8,128)S(1)} %reshape.108.valid_ref), custom_call_target="tpu_custom_call" | custom-call | tf_op jit(solution)/shard_map/bin_points/pallas_call | solution.py:799
  13.6 7.3 %all-to-all-start = ((bf16[8,16,2048]{2,1,0:T(8,128)(2,1)}), bf16[8,16,2048]{2,1,0:T(8,128)(2,1)S(1)}, u32[]{:S(2)}, u32[]{:S(2)}) async-start(bf16[8,16,2048]{2,1,0:T(8,128)(2,1)} %bin_points.1), calls=%async_computation | async-start | bytes 1048576 | tf_op jit(solution)/shard_map/all_to_all | solution.py:1089
  22.0 4.6 %collective-permute-start.8 = (bf16[1,36,128]{2,1,0:T(8,128)(2,1)S(1)}, bf16[1,36,128]{2,1,0:T(8,128)(2,1)S(1)}, u32[]{:S(2)}, u32[]{:S(2)}) collective-permute-start(bf16[1,36,128]{2,1,0:T(8,128)(2,1)S(1)} %slice_bitcast_fusion.1), channel_id=1, source_target_pairs={{0,31},{1,28},{2,29},{3,30},{4,3},{5,0},{6,1},{7,2},{8,7},{9,4},{1... | collective-permute-start | bytes 27656 | tf_op jit(solution)/shard_map/ppermute | solution.py:1028
  26.7 1.5 collective-permute-start.7
  29.9 3.5 compare_convert_fusion.base_ref
  33.4 3.4 all-to-all-done.recv_ref
  36.8 0.8 fusion.held_ref
  37.5 32.6 %encode_points.1 = (f32[5120,128]{1,0:T(8,128)}, bf16[128,36,128]{2,1,0:T(8,128)(2,1)}) custom-call(s32[8]{0:T(128)} %fusion.held_ref, bf16[8,16,2048]{2,1,0:T(8,128)(2,1)} %copy-done.1, f32[2139,128]{1,0:T(8,128)} %bitcast.30, f32[5120,128]{1,0:T(8,128)} %compare_convert_fusion.base_ref), custom_call_target="tpu_custom_call" | custom-call | tf_op jit(solution)/shard_map/encode_points/pallas_call | solution.py:882
  70.2 40.6 %first_layer.1 = (f32[4,32,40,128]{3,2,1,0:T(8,128)}, bf16[32,144,1152]{2,1,0:T(8,128)(2,1)}, bf16[32,144,384]{2,1,0:T(8,128)(2,1)}, bf16[32,144,128]{2,1,0:T(8,...) custom-call(f32[4,32,40,128]{3,2,1,0:T(8,128)} %bitcast.39, ...), custom_call_target="tpu_custom_call" | custom-call | tf_op jit(solution)/shard_map/first_layer/pallas_call | solution.py:435
  110.8 8.3 %collective-permute-start = (bf16[32,36,128]{2,1,0:T(8,128)(2,1)}, bf16[32,36,128]{2,1,0:T(8,128)(2,1)S(1)}, u32[]{:S(2)}, u32[]{:S(2)}) collective-permute-start(bf16[32,36,128]{2,1,0:T(8,128)(2,1)} %get-tuple-element.41), channel_id=1, source_target_pairs={{0,28},{4,0},{8,4},{12,8},{16,12},{20,16},{24,20},{28,24},{1,29},{... | collective-permute-start | bytes 884744 | tf_op jit(solution)/shard_map/ppermute | solution.py:1021
  119.1 0.8 slice_bitcast_fusion
  119.9 1.0 slice.27
  121.0 0.7 slice_bitcast_fusion.2
  121.7 3.3 collective-permute-start.1
  125.4 2.2 collective-permute-done.2.refs_3_
  127.6 5.5 %collective-permute-start.5 = (bf16[1,36,128]{2,1,0:T(8,128)(2,1)S(1)}, bf16[1,36,128]{2,1,0:T(8,128)(2,1)S(1)}, u32[]{:S(2)}, u32[]{:S(2)}) collective-permute-start(bf16[1,36,128]{2,1,0:T(8,128)(2,1)S(1)} %slice_bitcast_fusion.2), channel_id=1, source_target_pairs={{0,31},{1,28},{2,29},{3,30},{4,3},{5,0},{6,1},{7,2},{8,7},{9,4},{1... | collective-permute-start | bytes 27656 | tf_op jit(solution)/shard_map/ppermute | solution.py:1028
  133.1 0.7 add_convert_fusion.flag
  133.7 0.7 collective-permute-done.5.refs_7_
  135.3 83.1 %second_layer.1 = (f32[4,32,40,128]{3,2,1,0:T(8,128)}, f32[1280,128]{1,0:T(8,128)}, bf16[32,36,128]{2,1,0:T(8,128)(2,1)}, bf16[4,36,128]{2,1,0:T(8,128)(2,1)}, bf16[1,36,128]{2,1,0:T(8,128)(2,1)}) custom-call(s32[2]{0:T(128)} %add_convert_fusion.flag, f32[4,32,40,128]{3,2,1,0:T(8,128)} %get-tuple-element.40.refs_0_, bf16[32,36,128]{2,1,0:T(8,128)(2,1)} %copy-done.12, ...), custom_call_target="tpu_custom_call" | custom-call | tf_op jit(solution)/shard_map/second_layer/pallas_call | solution.py:579
  218.7 12.2 %collective-permute-done.11.refs_3_ = bf16[1,36,128]{2,1,0:T(8,128)(2,1)S(1)} collective-permute-done((bf16[1,36,128]{2,1,0:T(8,128)(2,1)}, bf16[1,36,128]{2,1,0:T(8,128)(2,1)S(1)}, u32[]{:S(2)}, u32[]{:S(2)}) %collective-permute-start.11) | collective-permute-done | bytes 9248 | tf_op jit(solution)/shard_map/ppermute | solution.py:1028
  230.9 3.7 %all-to-all-start.1 = ((f32[32,40,128]{2,1,0:T(8,128)}), f32[32,40,128]{2,1,0:T(8,128)S(1)}, u32[]{:S(2)}, u32[]{:S(2)}) async-start(f32[32,40,128]{2,1,0:T(8,128)} %bitcast.50), calls=%async_computation.1 | async-start | bytes 1310720 | tf_op jit(solution)/shard_map/all_to_all | solution.py:1046
  234.7 51.3 %first_layer_back.1 = (f32[4,32,40,128]{3,2,1,0:T(8,128)}, f32[1280,128]{1,0:T(8,128)}) custom-call(f32[4,32,40,128]{3,2,1,0:T(8,128)} %get-tuple-element.45.refs_0_, bf16[32,36,128]{2,1,0:T(8,128)(2,1)} %copy-done.10, bf16[4,36,128]{2,1,0:T(8,128)(2,1)} %copy-done.14, bf16[1,36,128]{2,1,0:T(8,128)(2,1)} %copy-done.22, f32[4,32,40,128]{3,2,1,0:T(8,128)} %bitcast.40, ...), custom_call_target="tpu_custom_call" | custom-call | flops 7864320000 | bytes 16777216 | tf_op jit(solution)/shard_map/first_layer_back/pallas_call | solution.py:703
  286.1 5.8 %all-to-all-start.2 = ((f32[32,40,128]{2,1,0:T(8,128)}), f32[32,40,128]{2,1,0:T(8,128)S(1)}, u32[]{:S(2)}, u32[]{:S(2)}) async-start(f32[32,40,128]{2,1,0:T(8,128)} %bitcast.51), calls=%async_computation.2 | async-start | bytes 1310720 | tf_op jit(solution)/shard_map/all_to_all | solution.py:1046
  292.0 1.7 copy-done.7
  293.7 24.5 %points_back.1 = f32[8,128]{1,0:T(8,128)S(1)} custom-call(s32[8]{0:T(128)S(1)} %copy-done.6, bf16[8,16,2048]{2,1,0:T(8,128)(2,1)S(1)} %copy-done.2, f32[2139,128]{1,0:T(8,128)S(1)} %bitcast.34, f32[5120,128]{1,0:T(8,128)S(1)} %bitcast.38), custom_call_target="tpu_custom_call" | custom-call | flops 26214400000 | bytes 16777216 | tf_op jit(solution)/shard_map/points_back/pallas_call | solution.py:946
  318.6 29.2 %all_to_all.20.got = bf16[32,96,128]{2,1,0:T(8,128)(2,1)S(1)} all-to-all(bf16[32,96,128]{2,1,0:T(8,128)(2,1)S(1)} %broadcast_in_dim.5), channel_id=1, replica_groups=mesh['tile'=8,'row'=4] {'tile','row'}, dimensions={0} | all-to-all | bytes 1572864 | tf_op jit(solution)/shard_map/all_to_all | solution.py:1046
  347.8 3.7 %update.1 = (f32[1,1]{1,0:T(1,128)}, f32[2139,128]{1,0:T(8,128)}, f32[2139,128]{1,0:T(8,128)}, f32[2139,128]{1,0:T(8,128)}, bf16[2139,128]{1,0:T(8,128)(2,1)}, /*index=5*/f32[8,128]{1,0:T(8,128)S(1)}) custom-call(bf16[32,96,128]{2,1,0:T(8,128)(2,1)S(1)} %all_to_all.20.got, f32[2139,128]{1,0:T(8,128)S(1)} %bitcast.35, f32[2139,128]{1,0:T(8,128)S(1)} %bitcast.36, ...), custom_call_target="tpu_custom_call" | custom-call | tf_op jit(solution)/shard_map/update/pallas_call | solution.py:1007
  351.5 0.6 slice_reduce_fusion
  (86 shorter events, 5.4 us)
Async XLA Ops:
  4.2 1.0 copy-start.5
  5.1 15.7 %copy-start.9 = (bf16[24,192,128]{2,1,0:T(8,128)(2,1)S(1)}, bf16[24,192,128]{2,1,0:T(8,128)(2,1)}, u32[]{:S(2)}) copy-start(bf16[24,192,128]{2,1,0:T(8,128)(2,1)} %param.14) | copy-start | bytes 3538948
  13.6 23.2 %all-to-all-start = ((bf16[8,16,2048]{2,1,0:T(8,128)(2,1)}), bf16[8,16,2048]{2,1,0:T(8,128)(2,1)S(1)}, u32[]{:S(2)}, u32[]{:S(2)}) async-start(bf16[8,16,2048]{2,1,0:T(8,128)(2,1)} %bin_points.1), calls=%async_computation | async-start | bytes 1048576 | tf_op jit(solution)/shard_map/all_to_all | solution.py:1089
  22.0 6.2 %copy-start.8 = (bf16[4,32,36,128]{3,2,1,0:T(8,128)(2,1)}, bf16[4,32,36,128]{3,2,1,0:T(8,128)(2,1)S(1)}, u32[]{:S(2)}) copy-start(bf16[4,32,36,128]{3,2,1,0:T(8,128)(2,1)S(1)} %copy.30.refs_8_) | copy-start | bytes 3538948
  22.0 7.0 %copy-start.18 = (s32[24,192]{1,0:T(8,128)S(1)}, s32[24,192]{1,0:T(8,128)}, u32[]{:S(2)}) copy-start(s32[24,192]{1,0:T(8,128)} %param.13) | copy-start | bytes 55300
  22.0 98.9 %collective-permute-start.8 = (bf16[1,36,128]{2,1,0:T(8,128)(2,1)S(1)}, bf16[1,36,128]{2,1,0:T(8,128)(2,1)S(1)}, u32[]{:S(2)}, u32[]{:S(2)}) collective-permute-start(bf16[1,36,128]{2,1,0:T(8,128)(2,1)S(1)} %slice_bitcast_fusion.1), channel_id=1, source_target_pairs={{0,31},{1,28},{2,29},{3,30},{4,3},{5,0},{6,1},{7,2},{8,7},{9,4},{1... | collective-permute-start | bytes 27656 | tf_op jit(solution)/shard_map/ppermute | solution.py:1028
  26.7 95.0 %collective-permute-start.7 = (bf16[4,36,128]{2,1,0:T(8,128)(2,1)S(1)}, bf16[4,36,128]{2,1,0:T(8,128)(2,1)S(1)}, u32[]{:S(2)}, u32[]{:S(2)}) collective-permute-start(bf16[4,36,128]{2,1,0:T(8,128)(2,1)S(1)} %bitcast.53), channel_id=1, source_target_pairs={{0,3},{1,0},{2,1},{3,2},{4,7},{5,4},{6,5},{7,6},{8,11},{9,8},{10,9... | collective-permute-start | bytes 110600 | tf_op jit(solution)/shard_map/ppermute | solution.py:1021
  28.4 96.6 %collective-permute-start.6 = (bf16[32,36,128]{2,1,0:T(8,128)(2,1)S(1)}, bf16[32,36,128]{2,1,0:T(8,128)(2,1)S(1)}, u32[]{:S(2)}, u32[]{:S(2)}) collective-permute-start(bf16[32,36,128]{2,1,0:T(8,128)(2,1)S(1)} %copy.27), channel_id=1, source_target_pairs={{0,28},{4,0},{8,4},{12,8},{16,12},{20,16},{24,20},{28,24},{1,29},{... | collective-permute-start | bytes 884744 | tf_op jit(solution)/shard_map/ppermute | solution.py:1021
  110.8 23.7 %collective-permute-start = (bf16[32,36,128]{2,1,0:T(8,128)(2,1)}, bf16[32,36,128]{2,1,0:T(8,128)(2,1)S(1)}, u32[]{:S(2)}, u32[]{:S(2)}) collective-permute-start(bf16[32,36,128]{2,1,0:T(8,128)(2,1)} %get-tuple-element.41), channel_id=1, source_target_pairs={{0,28},{4,0},{8,4},{12,8},{16,12},{20,16},{24,20},{28,24},{1,29},{... | collective-permute-start | bytes 884744 | tf_op jit(solution)/shard_map/ppermute | solution.py:1021
  119.1 8.5 %collective-permute-start.2 = (bf16[1,36,128]{2,1,0:T(8,128)(2,1)}, bf16[1,36,128]{2,1,0:T(8,128)(2,1)S(1)}, u32[]{:S(2)}, u32[]{:S(2)}) collective-permute-start(bf16[1,36,128]{2,1,0:T(8,128)(2,1)} %get-tuple-element.43), channel_id=1, source_target_pairs={{0,31},{1,28},{2,29},{3,30},{4,3},{5,0},{6,1},{7,2},{8,7},{9,4},{1... | collective-permute-start | bytes 27656 | tf_op jit(solution)/shard_map/ppermute | solution.py:1028
  120.9 13.6 %copy-start.19 = (bf16[1,36,128]{2,1,0:T(8,128)(2,1)}, bf16[1,36,128]{2,1,0:T(8,128)(2,1)S(1)}, u32[]{:S(2)}) copy-start(bf16[1,36,128]{2,1,0:T(8,128)(2,1)S(1)} %collective-permute-done.8.refs_11_) | copy-start | bytes 27652
  120.9 13.6 %collective-permute-start.3 = (bf16[32,36,128]{2,1,0:T(8,128)(2,1)S(1)}, bf16[32,36,128]{2,1,0:T(8,128)(2,1)S(1)}, u32[]{:S(2)}, u32[]{:S(2)}) collective-permute-start(bf16[32,36,128]{2,1,0:T(8,128)(2,1)S(1)} %slice.27), channel_id=1, source_target_pairs={{0,28},{4,0},{8,4},{12,8},{16,12},{20,16},{24,20},{28,24},{1,29},{... | collective-permute-start | bytes 884744 | tf_op jit(solution)/shard_map/ppermute | solution.py:1021
  121.7 12.9 %copy-start.15 = (bf16[4,36,128]{2,1,0:T(8,128)(2,1)}, bf16[4,36,128]{2,1,0:T(8,128)(2,1)S(1)}, u32[]{:S(2)}) copy-start(bf16[4,36,128]{2,1,0:T(8,128)(2,1)S(1)} %collective-permute-done.7.refs_10_) | copy-start | bytes 110596
  121.7 12.8 %collective-permute-start.1 = (bf16[4,36,128]{2,1,0:T(8,128)(2,1)}, bf16[4,36,128]{2,1,0:T(8,128)(2,1)S(1)}, u32[]{:S(2)}, u32[]{:S(2)}) collective-permute-start(bf16[4,36,128]{2,1,0:T(8,128)(2,1)} %get-tuple-element.42), channel_id=1, source_target_pairs={{0,3},{1,0},{2,1},{3,2},{4,7},{5,4},{6,5},{7,6},{8,11},{9,8},{10,9... | collective-permute-start | bytes 110600 | tf_op jit(solution)/shard_map/ppermute | solution.py:1021
  125.0 9.6 %copy-start.11 = (bf16[32,36,128]{2,1,0:T(8,128)(2,1)}, bf16[32,36,128]{2,1,0:T(8,128)(2,1)S(1)}, u32[]{:S(2)}) copy-start(bf16[32,36,128]{2,1,0:T(8,128)(2,1)S(1)} %collective-permute-done.6.refs_9_) | copy-start | bytes 884740
  125.0 9.5 %collective-permute-start.4 = (bf16[4,36,128]{2,1,0:T(8,128)(2,1)S(1)}, bf16[4,36,128]{2,1,0:T(8,128)(2,1)S(1)}, u32[]{:S(2)}, u32[]{:S(2)}) collective-permute-start(bf16[4,36,128]{2,1,0:T(8,128)(2,1)S(1)} %slice_bitcast_fusion), channel_id=1, source_target_pairs={{0,3},{1,0},{2,1},{3,2},{4,7},{5,4},{6,5},{7,6},{8,11},{9,8},{10,9... | collective-permute-start | bytes 110600 | tf_op jit(solution)/shard_map/ppermute | solution.py:1021
  127.6 7.0 %copy-start.20 = (bf16[1,36,128]{2,1,0:T(8,128)(2,1)}, bf16[1,36,128]{2,1,0:T(8,128)(2,1)S(1)}, u32[]{:S(2)}) copy-start(bf16[1,36,128]{2,1,0:T(8,128)(2,1)S(1)} %collective-permute-done.2.refs_3_) | copy-start | bytes 27652
  127.6 6.9 %collective-permute-start.5 = (bf16[1,36,128]{2,1,0:T(8,128)(2,1)S(1)}, bf16[1,36,128]{2,1,0:T(8,128)(2,1)S(1)}, u32[]{:S(2)}, u32[]{:S(2)}) collective-permute-start(bf16[1,36,128]{2,1,0:T(8,128)(2,1)S(1)} %slice_bitcast_fusion.2), channel_id=1, source_target_pairs={{0,31},{1,28},{2,29},{3,30},{4,3},{5,0},{6,1},{7,2},{8,7},{9,4},{1... | collective-permute-start | bytes 27656 | tf_op jit(solution)/shard_map/ppermute | solution.py:1028
  218.5 12.4 %collective-permute-start.9 = (bf16[32,36,128]{2,1,0:T(8,128)(2,1)}, bf16[32,36,128]{2,1,0:T(8,128)(2,1)S(1)}, u32[]{:S(2)}, u32[]{:S(2)}) collective-permute-start(bf16[32,36,128]{2,1,0:T(8,128)(2,1)} %get-tuple-element.47), channel_id=1, source_target_pairs={{0,4},{4,8},{8,12},{12,16},{16,20},{20,24},{24,28},{28,0},{1,5},{5... | collective-permute-start | bytes 884744 | tf_op jit(solution)/shard_map/ppermute | solution.py:1021
  218.5 12.4 %collective-permute-start.10 = (bf16[4,36,128]{2,1,0:T(8,128)(2,1)}, bf16[4,36,128]{2,1,0:T(8,128)(2,1)S(1)}, u32[]{:S(2)}, u32[]{:S(2)}) collective-permute-start(bf16[4,36,128]{2,1,0:T(8,128)(2,1)} %get-tuple-element.48), channel_id=1, source_target_pairs={{0,1},{1,2},{2,3},{3,0},{4,5},{5,6},{6,7},{7,4},{8,9},{9,10},{10,1... | collective-permute-start | bytes 110600 | tf_op jit(solution)/shard_map/ppermute | solution.py:1021
  218.6 12.3 %collective-permute-start.11 = (bf16[1,36,128]{2,1,0:T(8,128)(2,1)}, bf16[1,36,128]{2,1,0:T(8,128)(2,1)S(1)}, u32[]{:S(2)}, u32[]{:S(2)}) collective-permute-start(bf16[1,36,128]{2,1,0:T(8,128)(2,1)} %get-tuple-element.49), channel_id=1, source_target_pairs={{0,5},{1,6},{2,7},{3,4},{4,9},{5,10},{6,11},{7,8},{8,13},{9,14},{1... | collective-permute-start | bytes 27656 | tf_op jit(solution)/shard_map/ppermute | solution.py:1028
  230.9 3.8 %copy-start.22 = (bf16[1,36,128]{2,1,0:T(8,128)(2,1)}, bf16[1,36,128]{2,1,0:T(8,128)(2,1)S(1)}, u32[]{:S(2)}) copy-start(bf16[1,36,128]{2,1,0:T(8,128)(2,1)S(1)} %collective-permute-done.11.refs_3_) | copy-start | bytes 27652
  230.9 3.8 %copy-start.14 = (bf16[4,36,128]{2,1,0:T(8,128)(2,1)}, bf16[4,36,128]{2,1,0:T(8,128)(2,1)S(1)}, u32[]{:S(2)}) copy-start(bf16[4,36,128]{2,1,0:T(8,128)(2,1)S(1)} %collective-permute-done.10.refs_2_) | copy-start | bytes 110596
  230.9 3.8 %copy-start.10 = (bf16[32,36,128]{2,1,0:T(8,128)(2,1)}, bf16[32,36,128]{2,1,0:T(8,128)(2,1)S(1)}, u32[]{:S(2)}) copy-start(bf16[32,36,128]{2,1,0:T(8,128)(2,1)S(1)} %collective-permute-done.9.refs_1_) | copy-start | bytes 884740
  230.9 55.1 %all-to-all-start.1 = ((f32[32,40,128]{2,1,0:T(8,128)}), f32[32,40,128]{2,1,0:T(8,128)S(1)}, u32[]{:S(2)}, u32[]{:S(2)}) async-start(f32[32,40,128]{2,1,0:T(8,128)} %bitcast.50), calls=%async_computation.1 | async-start | bytes 1310720 | tf_op jit(solution)/shard_map/all_to_all | solution.py:1046
  286.0 6.0 %copy-start = (f32[273792]{0:T(1024)S(1)}, f32[273792]{0:T(1024)}, u32[]{:S(2)}) copy-start(f32[273792]{0:T(1024)} %param.15) | copy-start | bytes 3285508
  286.0 5.9 %copy-start.2 = (bf16[8,16,2048]{2,1,0:T(8,128)(2,1)S(1)}, bf16[8,16,2048]{2,1,0:T(8,128)(2,1)}, u32[]{:S(2)}) copy-start(bf16[8,16,2048]{2,1,0:T(8,128)(2,1)} %copy-done.1) | copy-start | bytes 1572868
  286.0 5.9 %copy-start.6 = (s32[8]{0:T(128)S(1)}, s32[8]{0:T(128)}, u32[]{:S(2)}) copy-start(s32[8]{0:T(128)} %fusion.held_ref) | copy-start | bytes 100
  286.1 32.2 %all-to-all-start.2 = ((f32[32,40,128]{2,1,0:T(8,128)}), f32[32,40,128]{2,1,0:T(8,128)S(1)}, u32[]{:S(2)}, u32[]{:S(2)}) async-start(f32[32,40,128]{2,1,0:T(8,128)} %bitcast.51), calls=%async_computation.2 | async-start | bytes 1310720 | tf_op jit(solution)/shard_map/all_to_all | solution.py:1046
  292.0 1.7 copy-start.7
  318.3 29.4 %copy-start.3 = (f32[273792]{0:T(1024)S(1)}, f32[273792]{0:T(1024)}, u32[]{:S(2)}) copy-start(f32[273792]{0:T(1024)} %param.16) | copy-start | bytes 3285508
  318.4 29.4 %copy-start.4 = (f32[273792]{0:T(1024)S(1)}, f32[273792]{0:T(1024)}, u32[]{:S(2)}) copy-start(f32[273792]{0:T(1024)} %param.17) | copy-start | bytes 3285508
  (6 other events, 4.2 us)

commit v3 on v2

--- a/solution.py
+++ b/solution.py
@@ -23,7 +23,7 @@
 BLOCK = 256
 CHUNK = 512
 LO = 512
-NW = 2
+NW = 8
 
 clip_norm = 0.01
 beta_one = 0.9
@@ -127,16 +127,44 @@
     return jnp.concatenate([vec(par, base, row), vec(par, base, row + 1)], axis=1)
 
 
-def head_lanes():
-    return lane_iota() // HD
-
-
-def head_rows(m):
-    lanes = head_lanes()
-    keep = [jnp.where(lanes == h, 1.0, 0.0).astype(BF16) for h in range(HEADS)]
-    top = m[:D]
-    rest = m[D:]
-    return jnp.concatenate([top * k for k in keep] + [rest * k for k in keep], axis=0)
+def fold_rows():
+    return one_hot(lax.broadcasted_iota(jnp.int32, (HD, D), 0) == lane_iota(HD) % HD)
+
+
+def own_head():
+    return lax.broadcasted_iota(jnp.int32, (D, D), 0) // HD == lane_iota(D) // HD
+
+
+def turned(v):
+    return v.astype(F32).T
+
+
+def head_cols(v):
+    top = turned(v[:D]).astype(BF16)
+    none = jnp.zeros((HD, D), BF16)
+    pairs = []
+    for t in range(0, D, 2 * HD):
+        left = jnp.concatenate([top[t : t + HD], none], axis=0)
+        right = jnp.concatenate([none, top[t + HD : t + 2 * HD]], axis=0)
+        pairs.append(jnp.concatenate([left, right], axis=1))
+    return pairs, jnp.where(own_head(), mm_tn(v[D:], fold_rows()), 0.0).astype(BF16)
+
+
+def by_head(rows, cols):
+    pairs, rest = cols
+    parts = []
+    for t in range(HEADS // 2):
+        both = mm(rows[:, 2 * HD * t : 2 * HD * (t + 1)], pairs[t])
+        parts = parts + [both[:, :D], both[:, D:]]
+    return parts + [mm(rows, rest)]
+
+
+def head_sums(cols, parts):
+    pairs, rest = cols
+    sums = [
+        mm_nt(pairs[t], jnp.concatenate(parts[2 * t : 2 * t + 2], axis=1)) for t in range(HEADS // 2)
+    ]
+    return (jnp.concatenate(sums, axis=0) + mm_nt(rest, parts[HEADS])).T.astype(BF16)
 
 
 def window_bias(groups):
@@ -156,41 +184,63 @@
 
 
 def attend(qs, key, val, bias_first, bias_last):
-    scores = mm_nt(key, head_rows(qs))
     probs = []
-    for h in range(HEADS + 1):
-        part = scores[:, h * D : (h + 1) * D] + (bias_first if h < HEADS else bias_last)
+    cols = head_cols(qs)
+    yield
+    parts = by_head(key, cols)
+    yield
+    for h, part in enumerate(parts):
+        part = part + (bias_first if h < HEADS else bias_last)
         expo = jnp.exp(part - jnp.max(part, axis=0, keepdims=True))
         probs.append((expo * (1.0 / jnp.sum(expo, axis=0, keepdims=True))).astype(BF16))
-    probs = jnp.concatenate(probs, axis=1)
-    return probs, query_pull(val, probs)
+    yield
+    mix = yield from query_pull(val, probs)
+    return probs, mix
 
 
 def attend_pull(probs, qs, key, val, gmix):
-    rows = head_rows(gmix)
-    pulled = mm_nt(val, rows)
+    cols = head_cols(gmix)
     gs = []
-    for h in range(HEADS + 1):
-        cols = slice(h * D, (h + 1) * D)
-        p = probs[:, cols].astype(F32)
-        both = p * pulled[:, cols]
+    yield
+    parts = by_head(val, cols)
+    yield
+    g_val = head_sums(cols, probs)
+    yield
+    for p_low, pulled in zip(probs, parts):
+        p = p_low.astype(F32)
+        both = p * pulled
         gs.append((both - p * jnp.sum(both, axis=0, keepdims=True)).astype(BF16))
-    gs = jnp.concatenate(gs, axis=1)
-    return query_pull(key * 0.25, gs), mm(gs, head_rows(qs)).astype(BF16), mm(probs, rows).astype(BF16)
-
-
-def query_pull(rows, cols):
-    full = mm_tn(rows, cols)
-    top = jnp.concatenate(
-        [full[h * HD : (h + 1) * HD, h * D : (h + 1) * D] for h in range(HEADS)], axis=0
-    )
-    chan = lax.broadcasted_iota(jnp.int32, (D, D), 0)
-    lanes = lane_iota(D)
-    rest = jnp.where(chan // HD == lanes // HD, full[:, HEADS * D :], 0.0).astype(BF16)
-    fold = jnp.where(
-        lax.broadcasted_iota(jnp.int32, (HD, D), 0) == lane_iota(HD) % HD, 1.0, 0.0
-    ).astype(BF16)
-    return jnp.concatenate([top.T.astype(BF16), mm_nt(fold, rest).astype(BF16)], axis=0)
+    yield
+    g_key = head_sums(head_cols(qs), gs)
+    yield
+    g_query = yield from query_pull(key * 0.25, gs)
+    return g_query, g_key, g_val
+
+
+def query_pull(rows, parts):
+    flat = turned(rows).astype(BF16)
+    tops = []
+    for t in range(HEADS // 2):
+        at = 2 * HD * t
+        both = mm(flat[at : at + 2 * HD], jnp.concatenate(parts[2 * t : 2 * t + 2], axis=1))
+        tops = tops + [both[:HD, :D], both[HD:, D:]]
+    top = jnp.concatenate(tops, axis=0)
+    rest = jnp.where(own_head(), mm(flat, parts[HEADS]), 0.0).astype(BF16)
+    yield
+    return jnp.concatenate([top.T.astype(BF16), mm_nt(fold_rows(), rest).astype(BF16)], axis=0)
+
+
+def in_step(runs):
+    results = [None] * len(runs)
+    active = list(range(len(runs)))
+    while active:
+        for i in list(active):
+            try:
+                next(runs[i])
+            except StopIteration as end:
+                results[i] = end.value
+                active.remove(i)
+    return results
 
 
 def split_qkv(packed, w):
@@ -205,14 +255,11 @@
         [vec(par, base, 0), jnp.zeros((1, D), F32), vec(par, base, 1)], axis=1
     )
     packed = (mm(low, w["qkv"][...]) + qkv_bias).astype(BF16)
-    probs, mixes, lives = [], [], []
-    for i in range(count):
-        bias_first, bias_last, live = window_bias(groups[i])
-        qs, key, val = split_qkv(packed, i)
-        prob, mix = attend(qs, key, val, bias_first, bias_last)
-        probs.append(prob)
-        mixes.append(mix)
-        lives.append(live)
+    masks = [window_bias(group) for group in groups]
+    done = in_step([attend(*split_qkv(packed, i), *masks[i][:2]) for i in range(count)])
+    probs = [d[0] for d in done]
+    mixes = [d[1] for d in done]
+    lives = [m[2] for m in masks]
     mix = jnp.concatenate(mixes, axis=0)
     live = jnp.concatenate(lives, axis=0)
     attn_out = mm(mix, w["out"][...]) + vec(par, base, 2)
@@ -271,15 +318,11 @@
     acc["out"][...] += mm_tn(k["mix"], g_attn)
     acc["vec"][2] += part8(g_attn.astype(F32))
     g_mix = mm(g_attn, w["out_t"][...]).astype(BF16)
-    pieces = []
+    runs = []
     for i in range(grad.shape[0] // SLOTS):
         rows = slice(i * SLOTS, (i + 1) * SLOTS)
-        qs, key, val = split_qkv(k["packed"], i)
-        pieces.append(
-            jnp.concatenate(
-                attend_pull(k["probs"][i], qs, key, val, g_mix[rows]), axis=1
-            )
-        )
+        runs.append(attend_pull(k["probs"][i], *split_qkv(k["packed"], i), g_mix[rows]))
+    pieces = [jnp.concatenate(parts, axis=1) for parts in in_step(runs)]
     g_packed = jnp.concatenate(pieces, axis=0)
     acc["qkv"][...] += mm_tn(k["low"], g_packed)
     acc["vec"][0] += part8(g_packed[:, :D].astype(F32))
@@ -396,7 +439,8 @@
         k = layer_forward(x, groups, par_ref, base, w, sums)
         for i in range(NW):
             rows = slice(i * SLOTS, (i + 1) * SLOTS)
-            probs_out[i] = k["probs"][i]
+            for h in range(HEADS + 1):
+                probs_out[i, :, h * D : (h + 1) * D] = k["probs"][i][h]
             packed_out[i] = k["packed"][rows]
             mix_out[i] = k["mix"][rows]
             first_out[i] = k["first"][rows]
@@ -664,7 +708,9 @@
         k = dict(
             low=rows_of(low),
             packed=rows_of(packed),
-            probs=[probs[i] for i in range(NW)],
+            probs=[
+                [probs[i, :, h * D : (h + 1) * D] for h in range(HEADS + 1)] for i in range(NW)
+            ],
             mix=rows_of(mix),
             live=rows_of(live),
         )

time: 350 us -> 279 us (0.80)
  Pallas kernels: 244 us -> 160 us
  starting transfers between devices: 41.2 us -> 47.8 us
  blocking collectives: 29.2 us -> 35.6 us
    pallas_call x1, Pallas kernels: 83.1 us -> 50.2 us  [second_layer(): pl.pallas_call(kernel, grid=(across * along,), in_specs=[pl.BlockSpec(mem...]
    pallas_call x1, Pallas kernels: 40.6 us -> 23.8 us  [first_layer(): pl.pallas_call(kernel, grid=(across * along,), in_specs=[quad_spec, whole...]
    pallas_call x1, Pallas kernels: 51.3 us -> 34.7 us  [first_layer_back(): pl.pallas_call(kernel, grid=(across * along,), in_specs=[whole(grads.shap...]
    pallas_call x1, Pallas kernels: 32.6 us -> 23.5 us  [encode_points(): pl.pallas_call(kernel, in_specs=[pl.BlockSpec(memory_space=pltpu.SMEM)] +...]
    pallas_call x1, Pallas kernels: 24.5 us -> 15.6 us  [points_back(): pl.pallas_call(kernel, in_specs=[pl.BlockSpec(memory_space=pltpu.SMEM)] +...]
    ppermute x4, starting transfers between devices: 10.2 us -> 18.7 us  [shifted(): return lax.ppermute(x, axes, pairs)]
    all_to_all x1, blocking collectives: 29.2 us -> 35.6 us  [all_to_all(): lax.all_to_all(x, ('tile', 'row'), split_axis=0, concat_axis=0, tiled=True)]
    ppermute x4, waiting for transfers between devices: 15.1 us -> 11.5 us  [shifted(): return lax.ppermute(x, axes, pairs)]
  transfers between devices with their start and end apart: 15 -> 15, of which waited for: 4 -> 6; matrix products, arithmetic and copies ran while one was open for 3% -> 3% of each run, Pallas kernels for 42% -> 35%
where the time goes in v3:
time: 279 us
  Pallas kernels  160 us (57%)
  starting transfers between devices  47.8 us (17%)
  blocking collectives  35.6 us (13%)
  waiting for transfers between devices  16.8 us (6%)
  local copies, waits for them, and re-layouts  11 us (4%)
  other arithmetic  6.59 us (2%)
    pallas_call x1, Pallas kernels, second_layer(): pl.pallas_call(kernel, grid=(across * along,), in_specs=[pl.BlockSpec(mem...  50.2 us
    all_to_all x1, blocking collectives, all_to_all(): lax.all_to_all(x, ('tile', 'row'), split_axis=0, concat_axis=0, tiled=True)  35.6 us
    pallas_call x1, Pallas kernels, first_layer_back(): pl.pallas_call(kernel, grid=(across * along,), in_specs=[whole(grads.shap...  34.7 us
    pallas_call x1, Pallas kernels, first_layer(): pl.pallas_call(kernel, grid=(across * along,), in_specs=[quad_spec, whole...  23.8 us
    pallas_call x1, Pallas kernels, encode_points(): pl.pallas_call(kernel, in_specs=[pl.BlockSpec(memory_space=pltpu.SMEM)] +...  23.5 us
    ppermute x4, starting transfers between devices, shifted(): return lax.ppermute(x, axes, pairs)  18.7 us
    pallas_call x1, Pallas kernels, points_back(): pl.pallas_call(kernel, in_specs=[pl.BlockSpec(memory_space=pltpu.SMEM)] +...  15.6 us
    ppermute x8, starting transfers between devices, shifted(): lax.ppermute(x, axes[0], [(i, (i + by) % count) for i in range(count)])  11.5 us
  transfers between devices with their start and end apart: 15, of which 6 were waited for; matrix products, arithmetic and copies ran while one was open for 3% of the time, Pallas kernels for 35%

profile of v3, /device:TPU:0, one launch (start us, length us, event | category | flops | bytes accessed | tf_op | source)
XLA Modules:
  0.0 278.9 jit_solution(10356826828170666323)
XLA Ops:
  1.1 1.5 reduce.6
  2.6 0.8 reshape.107.cell_ref
  3.4 0.8 reshape.108.valid_ref
  4.2 0.9 copy-done.5
  5.1 8.4 %bin_points.1 = bf16[8,16,2048]{2,1,0:T(8,128)(2,1)} custom-call(bf16[11,8192]{1,0:T(8,128)(2,1)S(1)} %copy-done.5, s32[32,256]{1,0:T(8,128)S(1)} %reshape.106.tile_ref, s32[32,256]{1,0:T(8,128)S(1)} %reshape.107.cell_ref, s32[32,256]{1,0:T(8,128)S(1)} %reshape.108.valid_ref), custom_call_target="tpu_custom_call" | custom-call | tf_op jit(solution)/shard_map/bin_points/pallas_call | solution.py:845
  13.6 7.3 %all-to-all-start = ((bf16[8,16,2048]{2,1,0:T(8,128)(2,1)}), bf16[8,16,2048]{2,1,0:T(8,128)(2,1)S(1)}, u32[]{:S(2)}, u32[]{:S(2)}) async-start(bf16[8,16,2048]{2,1,0:T(8,128)(2,1)} %bin_points.1), calls=%async_computation | async-start | bytes 1048576 | tf_op jit(solution)/shard_map/all_to_all | solution.py:1135
  22.0 4.6 %collective-permute-start.8 = (bf16[1,36,128]{2,1,0:T(8,128)(2,1)S(1)}, bf16[1,36,128]{2,1,0:T(8,128)(2,1)S(1)}, u32[]{:S(2)}, u32[]{:S(2)}) collective-permute-start(bf16[1,36,128]{2,1,0:T(8,128)(2,1)S(1)} %slice_bitcast_fusion.1), channel_id=1, source_target_pairs={{0,31},{1,28},{2,29},{3,30},{4,3},{5,0},{6,1},{7,2},{8,7},{9,4},{1... | collective-permute-start | bytes 27656 | tf_op jit(solution)/shard_map/ppermute | solution.py:1074
  26.7 1.5 collective-permute-start.7
  29.9 3.5 %compare_convert_fusion.base_ref = f32[5120,128]{1,0:T(8,128)} fusion(s32[128]{0:T(128)S(1)} %iota_add_fusion, s32[5120]{0:T(1024)S(1)} %eq.23), kind=kLoop, calls=%fused_computation | loop fusion | flops 1310720 | bytes 2642432 | tf_op jit(solution)/shard_map/convert_element_type | solution.py:1141
  33.4 3.4 %all-to-all-done.recv_ref = bf16[8,16,2048]{2,1,0:T(8,128)(2,1)S(1)} async-done(((bf16[8,16,2048]{2,1,0:T(8,128)(2,1)}), bf16[8,16,2048]{2,1,0:T(8,128)(2,1)S(1)}, u32[]{:S(2)}, u32[]{:S(2)}) %all-to-all-start) | async-done | bytes 524320 | tf_op jit(solution)/shard_map/all_to_all | solution.py:1135
  36.8 0.8 fusion.held_ref
  37.5 23.5 %encode_points.1 = (f32[5120,128]{1,0:T(8,128)}, bf16[128,36,128]{2,1,0:T(8,128)(2,1)}) custom-call(s32[8]{0:T(128)} %fusion.held_ref, bf16[8,16,2048]{2,1,0:T(8,128)(2,1)} %copy-done.1, f32[2139,128]{1,0:T(8,128)} %bitcast.30, f32[5120,128]{1,0:T(8,128)} %compare_convert_fusion.base_ref), custom_call_target="tpu_custom_call" | custom-call | tf_op jit(solution)/shard_map/encode_points/pallas_call | solution.py:928
  61.0 23.8 %first_layer.1 = (f32[4,32,40,128]{3,2,1,0:T(8,128)}, bf16[32,144,1152]{2,1,0:T(8,128)(2,1)}, bf16[32,144,384]{2,1,0:T(8,128)(2,1)}, bf16[32,144,128]{2,1,0:T(8,...) custom-call(f32[4,32,40,128]{3,2,1,0:T(8,128)} %bitcast.39, ...), custom_call_target="tpu_custom_call" | custom-call | tf_op jit(solution)/shard_map/first_layer/pallas_call | solution.py:479
  84.8 7.3 %collective-permute-start = (bf16[32,36,128]{2,1,0:T(8,128)(2,1)}, bf16[32,36,128]{2,1,0:T(8,128)(2,1)S(1)}, u32[]{:S(2)}, u32[]{:S(2)}) collective-permute-start(bf16[32,36,128]{2,1,0:T(8,128)(2,1)} %get-tuple-element.41), channel_id=1, source_target_pairs={{0,28},{4,0},{8,4},{12,8},{16,12},{20,16},{24,20},{28,24},{1,29},{... | collective-permute-start | bytes 884744 | tf_op jit(solution)/shard_map/ppermute | solution.py:1067
  92.1 8.8 %collective-permute-start.2 = (bf16[1,36,128]{2,1,0:T(8,128)(2,1)}, bf16[1,36,128]{2,1,0:T(8,128)(2,1)S(1)}, u32[]{:S(2)}, u32[]{:S(2)}) collective-permute-start(bf16[1,36,128]{2,1,0:T(8,128)(2,1)} %get-tuple-element.43), channel_id=1, source_target_pairs={{0,31},{1,28},{2,29},{3,30},{4,3},{5,0},{6,1},{7,2},{8,7},{9,4},{1... | collective-permute-start | bytes 27656 | tf_op jit(solution)/shard_map/ppermute | solution.py:1074
  100.8 0.8 slice_bitcast_fusion
  101.6 1.0 slice.27
  103.0 0.7 slice_bitcast_fusion.2
  104.4 4.4 %collective-permute-start.5 = (bf16[1,36,128]{2,1,0:T(8,128)(2,1)S(1)}, bf16[1,36,128]{2,1,0:T(8,128)(2,1)S(1)}, u32[]{:S(2)}, u32[]{:S(2)}) collective-permute-start(bf16[1,36,128]{2,1,0:T(8,128)(2,1)S(1)} %slice_bitcast_fusion.2), channel_id=1, source_target_pairs={{0,31},{1,28},{2,29},{3,30},{4,3},{5,0},{6,1},{7,2},{8,7},{9,4},{1... | collective-permute-start | bytes 27656 | tf_op jit(solution)/shard_map/ppermute | solution.py:1074
  109.4 0.7 collective-permute-done.5.refs_7_
  110.2 0.9 collective-permute-done.3.refs_5_
  111.8 50.2 %second_layer.1 = (f32[4,32,40,128]{3,2,1,0:T(8,128)}, f32[1280,128]{1,0:T(8,128)}, bf16[32,36,128]{2,1,0:T(8,128)(2,1)}, bf16[4,36,128]{2,1,0:T(8,128)(2,1)}, bf16[1,36,128]{2,1,0:T(8,128)(2,1)}) custom-call(s32[2]{0:T(128)} %add_convert_fusion.flag, f32[4,32,40,128]{3,2,1,0:T(8,128)} %get-tuple-element.40.refs_0_, bf16[32,36,128]{2,1,0:T(8,128)(2,1)} %copy-done.12, ...), custom_call_target="tpu_custom_call" | custom-call | tf_op jit(solution)/shard_map/second_layer/pallas_call | solution.py:623
  162.1 1.2 collective-permute-start.10
  163.3 0.9 collective-permute-start.11
  164.2 10.8 %collective-permute-done.11.refs_3_ = bf16[1,36,128]{2,1,0:T(8,128)(2,1)S(1)} collective-permute-done((bf16[1,36,128]{2,1,0:T(8,128)(2,1)}, bf16[1,36,128]{2,1,0:T(8,128)(2,1)S(1)}, u32[]{:S(2)}, u32[]{:S(2)}) %collective-permute-start.11) | collective-permute-done | bytes 9248 | tf_op jit(solution)/shard_map/ppermute | solution.py:1074
  175.4 4.7 %all-to-all-start.1 = ((f32[32,40,128]{2,1,0:T(8,128)}), f32[32,40,128]{2,1,0:T(8,128)S(1)}, u32[]{:S(2)}, u32[]{:S(2)}) async-start(f32[32,40,128]{2,1,0:T(8,128)} %bitcast.50), calls=%async_computation.1 | async-start | bytes 1310720 | tf_op jit(solution)/shard_map/all_to_all | solution.py:1092
  180.2 34.7 %first_layer_back.1 = (f32[4,32,40,128]{3,2,1,0:T(8,128)}, f32[1280,128]{1,0:T(8,128)}) custom-call(f32[4,32,40,128]{3,2,1,0:T(8,128)} %get-tuple-element.45.refs_0_, bf16[32,36,128]{2,1,0:T(8,128)(2,1)} %copy-done.10, bf16[4,36,128]{2,1,0:T(8,128)(2,1)} %copy-done.14, bf16[1,36,128]{2,1,0:T(8,128)(2,1)} %copy-done.22, f32[4,32,40,128]{3,2,1,0:T(8,128)} %bitcast.40, ...), custom_call_target="tpu_custom_call" | custom-call | flops 7864320000 | bytes 16777216 | tf_op jit(solution)/shard_map/first_layer_back/pallas_call | solution.py:749
  215.0 5.6 %all-to-all-start.2 = ((f32[32,40,128]{2,1,0:T(8,128)}), f32[32,40,128]{2,1,0:T(8,128)S(1)}, u32[]{:S(2)}, u32[]{:S(2)}) async-start(f32[32,40,128]{2,1,0:T(8,128)} %bitcast.51), calls=%async_computation.2 | async-start | bytes 1310720 | tf_op jit(solution)/shard_map/all_to_all | solution.py:1092
  220.7 1.7 copy-done.7
  222.4 15.6 %points_back.1 = f32[8,128]{1,0:T(8,128)S(1)} custom-call(s32[8]{0:T(128)S(1)} %copy-done.6, bf16[8,16,2048]{2,1,0:T(8,128)(2,1)S(1)} %copy-done.2, f32[2139,128]{1,0:T(8,128)S(1)} %bitcast.34, f32[5120,128]{1,0:T(8,128)S(1)} %bitcast.38), custom_call_target="tpu_custom_call" | custom-call | flops 26214400000 | bytes 16777216 | tf_op jit(solution)/shard_map/points_back/pallas_call | solution.py:992
  238.9 35.6 %all_to_all.20.got = bf16[32,96,128]{2,1,0:T(8,128)(2,1)S(1)} all-to-all(bf16[32,96,128]{2,1,0:T(8,128)(2,1)S(1)} %broadcast_in_dim.5), channel_id=1, replica_groups=mesh['tile'=8,'row'=4] {'tile','row'}, dimensions={0} | all-to-all | bytes 1572864 | tf_op jit(solution)/shard_map/all_to_all | solution.py:1092
  274.6 3.7 %update.1 = (f32[1,1]{1,0:T(1,128)}, f32[2139,128]{1,0:T(8,128)}, f32[2139,128]{1,0:T(8,128)}, f32[2139,128]{1,0:T(8,128)}, bf16[2139,128]{1,0:T(8,128)(2,1)}, /*index=5*/f32[8,128]{1,0:T(8,128)S(1)}) custom-call(bf16[32,96,128]{2,1,0:T(8,128)(2,1)S(1)} %all_to_all.20.got, f32[2139,128]{1,0:T(8,128)S(1)} %bitcast.35, f32[2139,128]{1,0:T(8,128)S(1)} %bitcast.36, ...), custom_call_target="tpu_custom_call" | custom-call | tf_op jit(solution)/shard_map/update/pallas_call | solution.py:1053
  (86 shorter events, 7.9 us)
Async XLA Ops:
  4.2 1.0 copy-start.5
  5.1 15.7 %copy-start.9 = (bf16[24,192,128]{2,1,0:T(8,128)(2,1)S(1)}, bf16[24,192,128]{2,1,0:T(8,128)(2,1)}, u32[]{:S(2)}) copy-start(bf16[24,192,128]{2,1,0:T(8,128)(2,1)} %param.14) | copy-start | bytes 3538948
  13.6 23.2 %all-to-all-start = ((bf16[8,16,2048]{2,1,0:T(8,128)(2,1)}), bf16[8,16,2048]{2,1,0:T(8,128)(2,1)S(1)}, u32[]{:S(2)}, u32[]{:S(2)}) async-start(bf16[8,16,2048]{2,1,0:T(8,128)(2,1)} %bin_points.1), calls=%async_computation | async-start | bytes 1048576 | tf_op jit(solution)/shard_map/all_to_all | solution.py:1135
  22.0 6.2 %copy-start.8 = (bf16[4,32,36,128]{3,2,1,0:T(8,128)(2,1)}, bf16[4,32,36,128]{3,2,1,0:T(8,128)(2,1)S(1)}, u32[]{:S(2)}) copy-start(bf16[4,32,36,128]{3,2,1,0:T(8,128)(2,1)S(1)} %copy.30.refs_8_) | copy-start | bytes 3538948
  22.0 7.0 %copy-start.18 = (s32[24,192]{1,0:T(8,128)S(1)}, s32[24,192]{1,0:T(8,128)}, u32[]{:S(2)}) copy-start(s32[24,192]{1,0:T(8,128)} %param.13) | copy-start | bytes 55300
  22.0 80.6 %collective-permute-start.8 = (bf16[1,36,128]{2,1,0:T(8,128)(2,1)S(1)}, bf16[1,36,128]{2,1,0:T(8,128)(2,1)S(1)}, u32[]{:S(2)}, u32[]{:S(2)}) collective-permute-start(bf16[1,36,128]{2,1,0:T(8,128)(2,1)S(1)} %slice_bitcast_fusion.1), channel_id=1, source_target_pairs={{0,31},{1,28},{2,29},{3,30},{4,3},{5,0},{6,1},{7,2},{8,7},{9,4},{1... | collective-permute-start | bytes 27656 | tf_op jit(solution)/shard_map/ppermute | solution.py:1074
  26.7 77.1 %collective-permute-start.7 = (bf16[4,36,128]{2,1,0:T(8,128)(2,1)S(1)}, bf16[4,36,128]{2,1,0:T(8,128)(2,1)S(1)}, u32[]{:S(2)}, u32[]{:S(2)}) collective-permute-start(bf16[4,36,128]{2,1,0:T(8,128)(2,1)S(1)} %bitcast.53), channel_id=1, source_target_pairs={{0,3},{1,0},{2,1},{3,2},{4,7},{5,4},{6,5},{7,6},{8,11},{9,8},{10,9... | collective-permute-start | bytes 110600 | tf_op jit(solution)/shard_map/ppermute | solution.py:1067
  28.4 75.4 %collective-permute-start.6 = (bf16[32,36,128]{2,1,0:T(8,128)(2,1)S(1)}, bf16[32,36,128]{2,1,0:T(8,128)(2,1)S(1)}, u32[]{:S(2)}, u32[]{:S(2)}) collective-permute-start(bf16[32,36,128]{2,1,0:T(8,128)(2,1)S(1)} %copy.27), channel_id=1, source_target_pairs={{0,28},{4,0},{8,4},{12,8},{16,12},{20,16},{24,20},{28,24},{1,29},{... | collective-permute-start | bytes 884744 | tf_op jit(solution)/shard_map/ppermute | solution.py:1067
  84.8 25.4 %collective-permute-start = (bf16[32,36,128]{2,1,0:T(8,128)(2,1)}, bf16[32,36,128]{2,1,0:T(8,128)(2,1)S(1)}, u32[]{:S(2)}, u32[]{:S(2)}) collective-permute-start(bf16[32,36,128]{2,1,0:T(8,128)(2,1)} %get-tuple-element.41), channel_id=1, source_target_pairs={{0,28},{4,0},{8,4},{12,8},{16,12},{20,16},{24,20},{28,24},{1,29},{... | collective-permute-start | bytes 884744 | tf_op jit(solution)/shard_map/ppermute | solution.py:1067
  92.1 12.3 %collective-permute-start.2 = (bf16[1,36,128]{2,1,0:T(8,128)(2,1)}, bf16[1,36,128]{2,1,0:T(8,128)(2,1)S(1)}, u32[]{:S(2)}, u32[]{:S(2)}) collective-permute-start(bf16[1,36,128]{2,1,0:T(8,128)(2,1)} %get-tuple-element.43), channel_id=1, source_target_pairs={{0,31},{1,28},{2,29},{3,30},{4,3},{5,0},{6,1},{7,2},{8,7},{9,4},{1... | collective-permute-start | bytes 27656 | tf_op jit(solution)/shard_map/ppermute | solution.py:1074
  102.6 8.5 %copy-start.19 = (bf16[1,36,128]{2,1,0:T(8,128)(2,1)}, bf16[1,36,128]{2,1,0:T(8,128)(2,1)S(1)}, u32[]{:S(2)}) copy-start(bf16[1,36,128]{2,1,0:T(8,128)(2,1)S(1)} %collective-permute-done.8.refs_11_) | copy-start | bytes 27652
  102.6 8.5 %collective-permute-start.3 = (bf16[32,36,128]{2,1,0:T(8,128)(2,1)S(1)}, bf16[32,36,128]{2,1,0:T(8,128)(2,1)S(1)}, u32[]{:S(2)}, u32[]{:S(2)}) collective-permute-start(bf16[32,36,128]{2,1,0:T(8,128)(2,1)S(1)} %slice.27), channel_id=1, source_target_pairs={{0,28},{4,0},{8,4},{12,8},{16,12},{20,16},{24,20},{28,24},{1,29},{... | collective-permute-start | bytes 884744 | tf_op jit(solution)/shard_map/ppermute | solution.py:1067
  103.7 7.4 %copy-start.15 = (bf16[4,36,128]{2,1,0:T(8,128)(2,1)}, bf16[4,36,128]{2,1,0:T(8,128)(2,1)S(1)}, u32[]{:S(2)}) copy-start(bf16[4,36,128]{2,1,0:T(8,128)(2,1)S(1)} %collective-permute-done.7.refs_10_) | copy-start | bytes 110596
  103.7 6.4 %collective-permute-start.1 = (bf16[4,36,128]{2,1,0:T(8,128)(2,1)}, bf16[4,36,128]{2,1,0:T(8,128)(2,1)S(1)}, u32[]{:S(2)}, u32[]{:S(2)}) collective-permute-start(bf16[4,36,128]{2,1,0:T(8,128)(2,1)} %get-tuple-element.42), channel_id=1, source_target_pairs={{0,3},{1,0},{2,1},{3,2},{4,7},{5,4},{6,5},{7,6},{8,11},{9,8},{10,9... | collective-permute-start | bytes 110600 | tf_op jit(solution)/shard_map/ppermute | solution.py:1067
  103.8 7.3 %copy-start.11 = (bf16[32,36,128]{2,1,0:T(8,128)(2,1)}, bf16[32,36,128]{2,1,0:T(8,128)(2,1)S(1)}, u32[]{:S(2)}) copy-start(bf16[32,36,128]{2,1,0:T(8,128)(2,1)S(1)} %collective-permute-done.6.refs_9_) | copy-start | bytes 884740
  103.8 6.4 %collective-permute-start.4 = (bf16[4,36,128]{2,1,0:T(8,128)(2,1)S(1)}, bf16[4,36,128]{2,1,0:T(8,128)(2,1)S(1)}, u32[]{:S(2)}, u32[]{:S(2)}) collective-permute-start(bf16[4,36,128]{2,1,0:T(8,128)(2,1)S(1)} %slice_bitcast_fusion), channel_id=1, source_target_pairs={{0,3},{1,0},{2,1},{3,2},{4,7},{5,4},{6,5},{7,6},{8,11},{9,8},{10,9... | collective-permute-start | bytes 110600 | tf_op jit(solution)/shard_map/ppermute | solution.py:1067
  104.4 6.7 %copy-start.20 = (bf16[1,36,128]{2,1,0:T(8,128)(2,1)}, bf16[1,36,128]{2,1,0:T(8,128)(2,1)S(1)}, u32[]{:S(2)}) copy-start(bf16[1,36,128]{2,1,0:T(8,128)(2,1)S(1)} %collective-permute-done.2.refs_3_) | copy-start | bytes 27652
  104.4 5.8 %collective-permute-start.5 = (bf16[1,36,128]{2,1,0:T(8,128)(2,1)S(1)}, bf16[1,36,128]{2,1,0:T(8,128)(2,1)S(1)}, u32[]{:S(2)}, u32[]{:S(2)}) collective-permute-start(bf16[1,36,128]{2,1,0:T(8,128)(2,1)S(1)} %slice_bitcast_fusion.2), channel_id=1, source_target_pairs={{0,31},{1,28},{2,29},{3,30},{4,3},{5,0},{6,1},{7,2},{8,7},{9,4},{1... | collective-permute-start | bytes 27656 | tf_op jit(solution)/shard_map/ppermute | solution.py:1074
  162.0 13.4 %collective-permute-start.9 = (bf16[32,36,128]{2,1,0:T(8,128)(2,1)}, bf16[32,36,128]{2,1,0:T(8,128)(2,1)S(1)}, u32[]{:S(2)}, u32[]{:S(2)}) collective-permute-start(bf16[32,36,128]{2,1,0:T(8,128)(2,1)} %get-tuple-element.47), channel_id=1, source_target_pairs={{0,4},{4,8},{8,12},{12,16},{16,20},{20,24},{24,28},{28,0},{1,5},{5... | collective-permute-start | bytes 884744 | tf_op jit(solution)/shard_map/ppermute | solution.py:1067
  162.1 12.9 %collective-permute-start.10 = (bf16[4,36,128]{2,1,0:T(8,128)(2,1)}, bf16[4,36,128]{2,1,0:T(8,128)(2,1)S(1)}, u32[]{:S(2)}, u32[]{:S(2)}) collective-permute-start(bf16[4,36,128]{2,1,0:T(8,128)(2,1)} %get-tuple-element.48), channel_id=1, source_target_pairs={{0,1},{1,2},{2,3},{3,0},{4,5},{5,6},{6,7},{7,4},{8,9},{9,10},{10,1... | collective-permute-start | bytes 110600 | tf_op jit(solution)/shard_map/ppermute | solution.py:1067
  163.3 11.7 %collective-permute-start.11 = (bf16[1,36,128]{2,1,0:T(8,128)(2,1)}, bf16[1,36,128]{2,1,0:T(8,128)(2,1)S(1)}, u32[]{:S(2)}, u32[]{:S(2)}) collective-permute-start(bf16[1,36,128]{2,1,0:T(8,128)(2,1)} %get-tuple-element.49), channel_id=1, source_target_pairs={{0,5},{1,6},{2,7},{3,4},{4,9},{5,10},{6,11},{7,8},{8,13},{9,14},{1... | collective-permute-start | bytes 27656 | tf_op jit(solution)/shard_map/ppermute | solution.py:1074
  175.0 5.2 %copy-start.22 = (bf16[1,36,128]{2,1,0:T(8,128)(2,1)}, bf16[1,36,128]{2,1,0:T(8,128)(2,1)S(1)}, u32[]{:S(2)}) copy-start(bf16[1,36,128]{2,1,0:T(8,128)(2,1)S(1)} %collective-permute-done.11.refs_3_) | copy-start | bytes 27652
  175.0 5.2 %copy-start.14 = (bf16[4,36,128]{2,1,0:T(8,128)(2,1)}, bf16[4,36,128]{2,1,0:T(8,128)(2,1)S(1)}, u32[]{:S(2)}) copy-start(bf16[4,36,128]{2,1,0:T(8,128)(2,1)S(1)} %collective-permute-done.10.refs_2_) | copy-start | bytes 110596
  175.4 4.8 %copy-start.10 = (bf16[32,36,128]{2,1,0:T(8,128)(2,1)}, bf16[32,36,128]{2,1,0:T(8,128)(2,1)S(1)}, u32[]{:S(2)}) copy-start(bf16[32,36,128]{2,1,0:T(8,128)(2,1)S(1)} %collective-permute-done.9.refs_1_) | copy-start | bytes 884740
  175.4 39.5 %all-to-all-start.1 = ((f32[32,40,128]{2,1,0:T(8,128)}), f32[32,40,128]{2,1,0:T(8,128)S(1)}, u32[]{:S(2)}, u32[]{:S(2)}) async-start(f32[32,40,128]{2,1,0:T(8,128)} %bitcast.50), calls=%async_computation.1 | async-start | bytes 1310720 | tf_op jit(solution)/shard_map/all_to_all | solution.py:1092
  214.9 5.7 %copy-start = (f32[273792]{0:T(1024)S(1)}, f32[273792]{0:T(1024)}, u32[]{:S(2)}) copy-start(f32[273792]{0:T(1024)} %param.15) | copy-start | bytes 3285508
  215.0 5.7 %copy-start.2 = (bf16[8,16,2048]{2,1,0:T(8,128)(2,1)S(1)}, bf16[8,16,2048]{2,1,0:T(8,128)(2,1)}, u32[]{:S(2)}) copy-start(bf16[8,16,2048]{2,1,0:T(8,128)(2,1)} %copy-done.1) | copy-start | bytes 1572868
  215.0 5.7 %copy-start.6 = (s32[8]{0:T(128)S(1)}, s32[8]{0:T(128)}, u32[]{:S(2)}) copy-start(s32[8]{0:T(128)} %fusion.held_ref) | copy-start | bytes 100
  215.0 23.6 %all-to-all-start.2 = ((f32[32,40,128]{2,1,0:T(8,128)}), f32[32,40,128]{2,1,0:T(8,128)S(1)}, u32[]{:S(2)}, u32[]{:S(2)}) async-start(f32[32,40,128]{2,1,0:T(8,128)} %bitcast.51), calls=%async_computation.2 | async-start | bytes 1310720 | tf_op jit(solution)/shard_map/all_to_all | solution.py:1092
  220.7 1.7 copy-start.7
  238.7 35.9 %copy-start.3 = (f32[273792]{0:T(1024)S(1)}, f32[273792]{0:T(1024)}, u32[]{:S(2)}) copy-start(f32[273792]{0:T(1024)} %param.16) | copy-start | bytes 3285508
  238.7 35.8 %copy-start.4 = (f32[273792]{0:T(1024)S(1)}, f32[273792]{0:T(1024)}, u32[]{:S(2)}) copy-start(f32[273792]{0:T(1024)} %param.17) | copy-start | bytes 3285508
  (6 other events, 5.3 us)

commit v4 on v3

--- a/solution.py
+++ b/solution.py
@@ -20,7 +20,7 @@
 LAYER_ROWS = 1034
 POINT_ROWS = 71
 GRAD_ROWS = 1040
-BLOCK = 256
+BLOCK = 128
 CHUNK = 512
 LO = 512
 NW = 8
@@ -777,7 +777,7 @@
 def bin_points(feats, tiles, cells, valid, tile_count, capacity, extent_y, quads_y):
     blocks = tiles.shape[0]
     groups = tile_count * capacity // LO
-    lots = 4
+    lots = 8
     wide = lots * BLOCK
 
     def kernel(feat_ref, tile_ref, cell_ref, valid_ref, out_ref, slot_ref, code_ref, acc):
@@ -873,13 +873,43 @@
     return odd[5:6]
 
 
+def list_chunks(held_ref, todo, sources, chunk, most):
+    def source(s, n):
+        def put(j, n):
+            todo[n] = s * most + j
+            return n + 1
+
+        return lax.fori_loop(0, (held_ref[s] + chunk - 1) // chunk, put, n)
+
+    todo[0] = 0
+    return lax.fori_loop(0, sources, source, 0)
+
+
+def two_stage(count, todo, most, prepare, finish, even, odd):
+    def ready(i, buffers):
+        item = todo[jnp.minimum(i, jnp.maximum(count - 1, 0))]
+        prepare(item // most, item % most, jnp.where(i < count, 1.0, 0.0), buffers)
+
+    def pair(k, _):
+        ready(2 * k + 1, odd)
+        finish(even)
+        ready(2 * k + 2, even)
+        finish(odd)
+        return 0
+
+    ready(0, even)
+    lax.fori_loop(0, (count + 1) // 2, pair, 0)
+
+
 def encode_points(recv, held, par, base_rows, quads):
     sources, _, capacity = recv.shape
     chunk = min(CHUNK, capacity)
     groups = -(-quads * QP // LO)
     pairs = -(-groups // 2)
 
-    def kernel(held_ref, recv_ref, par_ref, base_ref, out_ref, tag_ref, win, acc):
+    most = capacity // chunk
+
+    def kernel(held_ref, recv_ref, par_ref, base_ref, out_ref, tag_ref, win, acc, todo, *buffers):
         bias = unpack_point_in(par_ref, win)
         acc[...] = jnp.zeros(acc.shape, F32)
         lanes = lane_iota()
@@ -887,25 +917,25 @@
         count_of = (lanes + 1).astype(F32)
         span = lax.broadcasted_iota(jnp.int32, (LO, chunk), 0)
 
-        def source(s, _):
-            def piece(j, _):
-                cols = recv_ref[s, :, pl.ds(pl.multiple_of(j * chunk, chunk), chunk)]
-                wide = cols.astype(F32)
-                place = one_hot(span == (wide[13:14] + wide[14:15]).astype(jnp.int32))
-                both = mm_tn(cols, win[:, : 2 * D])
-                act = gelu_only(both[:, :D] + bias)
-                group = both[:, D:]
-                spread = [
-                    jnp.where(group == own + 2.0 * g, act, 0.0).astype(BF16) for g in range(pairs)
-                ]
-                spread.append(one_hot(group == count_of))
-                acc[...] += mm(place, jnp.concatenate(spread, axis=1))
-                return 0
-
-            lax.fori_loop(0, (held_ref[s] + chunk - 1) // chunk, piece, 0)
-            return 0
-
-        lax.fori_loop(0, sources, source, 0)
+        def prepare(s, j, real, into):
+            place, spread = into
+            cols = recv_ref[s, :, pl.ds(pl.multiple_of(j * chunk, chunk), chunk)]
+            wide = cols.astype(F32)
+            place[...] = one_hot(span == (wide[13:14] + wide[14:15]).astype(jnp.int32))
+            both = mm_tn(cols, win[:, : 2 * D])
+            act = gelu_only(both[:, :D] + bias)
+            group = both[:, D:] * real
+            for g in range(pairs):
+                spread[:, g * D : g * D + D] = jnp.where(group == own + 2.0 * g, act, 0.0).astype(
+                    BF16
+                )
+            spread[:, pairs * D :] = one_hot(group == count_of)
+
+        def finish_chunk(held):
+            acc[...] += mm(held[0][...], held[1][...])
+
+        count = list_chunks(held_ref, todo, sources, chunk, most)
+        two_stage(count, todo, most, prepare, finish_chunk, buffers[:2], buffers[2:])
         for g in range(groups):
             rows = min(LO, quads * QP - g * LO)
             v = acc[:rows, g // 2 * D : g // 2 * D + D]
@@ -930,7 +960,9 @@
         in_specs=[pl.BlockSpec(memory_space=pltpu.SMEM)]
         + [pl.BlockSpec(memory_space=pltpu.VMEM)] * 3,
         out_shape=[shape((quads * QP, D), F32), shape((quads, QC, D), BF16)],
-        scratch_shapes=[pltpu.VMEM((16, 3 * D), BF16), pltpu.VMEM((LO, (pairs + 1) * D), F32)],
+        scratch_shapes=[pltpu.VMEM((16, 3 * D), BF16), pltpu.VMEM((LO, (pairs + 1) * D), F32)]
+        + [pltpu.SMEM((sources * most + 1,), jnp.int32)]
+        + [pltpu.VMEM((LO, chunk), BF16), pltpu.VMEM((chunk, (pairs + 1) * D), BF16)] * 2,
         compiler_params=pltpu.CompilerParams(vmem_limit_bytes=56 * 1024 * 1024),
         name="encode_points",
     )(held, recv, par, base_rows)
@@ -943,7 +975,11 @@
     groups = -(-total_rows // LO)
     pairs = -(-groups // 2)
 
-    def kernel(held_ref, recv_ref, par_ref, grad_ref, out_ref, win, table, acc):
+    most = capacity // chunk
+
+    def kernel(
+        held_ref, recv_ref, par_ref, grad_ref, out_ref, win, table, acc, todo, *buffers
+    ):
         bias = unpack_point_in(par_ref, win)
         lanes = lane_iota()
 
@@ -960,28 +996,29 @@
         own = jnp.where(lanes < H1, 1.0, 2.0)
         spot = lanes.astype(F32)
 
-        def source(s, _):
-            def piece(j, _):
-                cols = recv_ref[s, :, pl.ds(pl.multiple_of(j * chunk, chunk), chunk)]
-                made = mm_tn(cols, win[...])
-                group = made[:, D : 2 * D]
-                at = made[:, 2 * D :]
-                place = jnp.concatenate([one_hot(at == spot + k * D) for k in range(LO // D)], axis=1)
-                got = jnp.zeros((chunk, D), F32)
-                for p in range(0, pairs, 2):
-                    both = mm(place, table[:, p * D : min(p + 2, pairs) * D])
-                    for u in range(both.shape[1] // D):
-                        got = jnp.where(
-                            group == own + 2.0 * (p + u), both[:, u * D : u * D + D], got
-                        )
-                slope = gelu_parts(made[:, :D] + bias)[1]
-                acc[...] += mm(cols, (got * slope).astype(BF16))
-                return 0
-
-            lax.fori_loop(0, (held_ref[s] + chunk - 1) // chunk, piece, 0)
-            return 0
-
-        lax.fori_loop(0, sources, source, 0)
+        def prepare(s, j, real, into):
+            place, group, slope, kept = into
+            cols = recv_ref[s, :, pl.ds(pl.multiple_of(j * chunk, chunk), chunk)]
+            made = mm_tn(cols, win[...])
+            kept[...] = cols
+            group[...] = made[:, D : 2 * D] * real
+            for k in range(LO // D):
+                place[:, k * D : k * D + D] = one_hot(made[:, 2 * D :] == spot + k * D)
+            slope[...] = gelu_parts(made[:, :D] + bias)[1]
+
+        def finish_chunk(held):
+            place, group, slope, kept = held
+            got = jnp.zeros((chunk, D), F32)
+            for p in range(0, pairs, 2):
+                both = mm(place[...], table[:, p * D : min(p + 2, pairs) * D])
+                for u in range(both.shape[1] // D):
+                    got = jnp.where(
+                        group[...] == own + 2.0 * (p + u), both[:, u * D : u * D + D], got
+                    )
+            acc[...] += mm(kept[...], (got * slope[...]).astype(BF16))
+
+        count = list_chunks(held_ref, todo, sources, chunk, most)
+        two_stage(count, todo, most, prepare, finish_chunk, buffers[:4], buffers[4:])
         both = acc[...] + pltpu.roll(acc[...], H1, axis=1)
         rows = [
             jnp.where(lanes < H1, both[2 * k : 2 * k + 1, :], both[2 * k + 1 : 2 * k + 2, :])
@@ -998,7 +1035,15 @@
             pltpu.VMEM((16, 3 * D), BF16),
             pltpu.VMEM((LO, pairs * D), BF16),
             pltpu.VMEM((16, D), F32),
-        ],
+            pltpu.SMEM((sources * most + 1,), jnp.int32),
+        ]
+        + [
+            pltpu.VMEM((chunk, LO), BF16),
+            pltpu.VMEM((chunk, D), F32),
+            pltpu.VMEM((chunk, D), F32),
+            pltpu.VMEM((16, chunk), BF16),
+        ]
+        * 2,
         compiler_params=pltpu.CompilerParams(vmem_limit_bytes=48 * 1024 * 1024),
         cost_estimate=cost_of(recv.size * 100000),
         name="points_back",

time: 279 us -> 273 us (0.978); the launches traced: 279 us -> 276 us
    ppermute x8, starting transfers between devices: 11.5 us -> 18.5 us  [shifted(): lax.ppermute(x, axes[0], [(i, (i + by) % count) for i in range(count)])]
    ppermute x4, starting transfers between devices: 18.7 us -> 12.5 us  [shifted(): return lax.ppermute(x, axes, pairs)]
    unnamed x49 -> x54, local copies, waits for them, and re-layouts: 4.07 us -> 5.82 us
where the time goes in v4:
time: 273 us; the launch traced here: 276 us
  Pallas kernels  158 us (58%)
  starting transfers between devices  46.9 us (17%)
  blocking collectives  35.8 us (13%)
  waiting for transfers between devices  17.5 us (6%)
  local copies, waits for them, and re-layouts  11.2 us (4%)
  other arithmetic  5.03 us (2%)
    pallas_call x1, Pallas kernels, second_layer(): pl.pallas_call(kernel, grid=(across * along,), in_specs=[pl.BlockSpec(mem...  50.2 us
    all_to_all x1, blocking collectives, all_to_all(): lax.all_to_all(x, ('tile', 'row'), split_axis=0, concat_axis=0, tiled=True)  35.8 us
    pallas_call x1, Pallas kernels, first_layer_back(): pl.pallas_call(kernel, grid=(across * along,), in_specs=[whole(grads.shap...  34.7 us
    pallas_call x1, Pallas kernels, first_layer(): pl.pallas_call(kernel, grid=(across * along,), in_specs=[quad_spec, whole...  23.8 us
    pallas_call x1, Pallas kernels, encode_points(): pl.pallas_call(kernel, in_specs=[pl.BlockSpec(memory_space=pltpu.SMEM)] +...  21.2 us
    ppermute x8, starting transfers between devices, shifted(): lax.ppermute(x, axes[0], [(i, (i + by) % count) for i in range(count)])  18.5 us
    pallas_call x1, Pallas kernels, points_back(): pl.pallas_call(kernel, in_specs=[pl.BlockSpec(memory_space=pltpu.SMEM)] +...  15.8 us
    ppermute x4, waiting for transfers between devices, shifted(): return lax.ppermute(x, axes, pairs)  12.7 us
  transfers between devices with their start and end apart: 15, of which 6 were waited for; matrix products, arithmetic and copies ran while one was open for 3% of the time, Pallas kernels for 35%

profile of v4, /device:TPU:0, one launch (start us, length us, event | category | flops | bytes accessed | tf_op | source)
XLA Modules:
  0.0 275.8 jit_solution(2046658868748444009)
XLA Ops:
  0.6 0.9 copy-done.5
  1.6 0.8 copy-done.6
  2.3 0.8 copy-done.7
  3.1 0.8 copy-done.8
  3.9 8.9 %bin_points.1 = bf16[8,16,2048]{2,1,0:T(8,128)(2,1)} custom-call(bf16[11,8192]{1,0:T(8,128)(2,1)S(1)} %copy-done.5, s32[64,128]{1,0:T(8,128)S(1)} %bitcast.40, s32[64,128]{1,0:T(8,128)S(1)} %bitcast.41, s32[64,128]{1,0:T(8,128)S(1)} %bitcast.42), custom_call_target="tpu_custom_call" | custom-call | tf_op jit(solution)/shard_map/bin_points/pallas_call | solution.py:845
  12.7 7.3 %all-to-all-start = ((bf16[8,16,2048]{2,1,0:T(8,128)(2,1)}), bf16[8,16,2048]{2,1,0:T(8,128)(2,1)S(1)}, u32[]{:S(2)}, u32[]{:S(2)}) async-start(bf16[8,16,2048]{2,1,0:T(8,128)(2,1)} %bin_points.1), calls=%async_computation | async-start | bytes 1048576 | tf_op jit(solution)/shard_map/all_to_all | solution.py:1180
  21.2 4.6 %collective-permute-start.8 = (bf16[1,36,128]{2,1,0:T(8,128)(2,1)S(1)}, bf16[1,36,128]{2,1,0:T(8,128)(2,1)S(1)}, u32[]{:S(2)}, u32[]{:S(2)}) collective-permute-start(bf16[1,36,128]{2,1,0:T(8,128)(2,1)S(1)} %slice_bitcast_fusion.1), channel_id=1, source_target_pairs={{0,31},{1,28},{2,29},{3,30},{4,3},{5,0},{6,1},{7,2},{8,7},{9,4},{1... | collective-permute-start | bytes 27656 | tf_op jit(solution)/shard_map/ppermute | solution.py:1119
  25.9 1.5 collective-permute-start.7
  29.1 3.4 %compare_convert_fusion.base_ref = f32[5120,128]{1,0:T(8,128)} fusion(s32[128]{0:T(128)S(1)} %iota_add_fusion, s32[5120]{0:T(1024)S(1)} %eq.23), kind=kLoop, calls=%fused_computation | loop fusion | flops 1310720 | bytes 2642432 | tf_op jit(solution)/shard_map/convert_element_type | solution.py:1186
  32.5 3.4 %all-to-all-done.recv_ref = bf16[8,16,2048]{2,1,0:T(8,128)(2,1)S(1)} async-done(((bf16[8,16,2048]{2,1,0:T(8,128)(2,1)}), bf16[8,16,2048]{2,1,0:T(8,128)(2,1)S(1)}, u32[]{:S(2)}, u32[]{:S(2)}) %all-to-all-start) | async-done | bytes 524320 | tf_op jit(solution)/shard_map/all_to_all | solution.py:1180
  35.9 0.8 fusion.held_ref
  36.7 21.2 %encode_points.1 = (f32[5120,128]{1,0:T(8,128)}, bf16[128,36,128]{2,1,0:T(8,128)(2,1)}) custom-call(s32[8]{0:T(128)} %fusion.held_ref, bf16[8,16,2048]{2,1,0:T(8,128)(2,1)} %copy-done.1, f32[2139,128]{1,0:T(8,128)} %bitcast.32, f32[5120,128]{1,0:T(8,128)} %compare_convert_fusion.base_ref), custom_call_target="tpu_custom_call" | custom-call | tf_op jit(solution)/shard_map/encode_points/pallas_call | solution.py:958
  58.0 23.8 %first_layer.1 = (f32[4,32,40,128]{3,2,1,0:T(8,128)}, bf16[32,144,1152]{2,1,0:T(8,128)(2,1)}, bf16[32,144,384]{2,1,0:T(8,128)(2,1)}, bf16[32,144,128]{2,1,0:T(8,...) custom-call(f32[4,32,40,128]{3,2,1,0:T(8,128)} %bitcast.44, ...), custom_call_target="tpu_custom_call" | custom-call | tf_op jit(solution)/shard_map/first_layer/pallas_call | solution.py:479
  81.7 13.3 %collective-permute-start = (bf16[32,36,128]{2,1,0:T(8,128)(2,1)}, bf16[32,36,128]{2,1,0:T(8,128)(2,1)S(1)}, u32[]{:S(2)}, u32[]{:S(2)}) collective-permute-start(bf16[32,36,128]{2,1,0:T(8,128)(2,1)} %get-tuple-element.41), channel_id=1, source_target_pairs={{0,28},{4,0},{8,4},{12,8},{16,12},{20,16},{24,20},{28,24},{1,29},{... | collective-permute-start | bytes 884744 | tf_op jit(solution)/shard_map/ppermute | solution.py:1112
  95.1 3.7 %collective-permute-start.2 = (bf16[1,36,128]{2,1,0:T(8,128)(2,1)}, bf16[1,36,128]{2,1,0:T(8,128)(2,1)S(1)}, u32[]{:S(2)}, u32[]{:S(2)}) collective-permute-start(bf16[1,36,128]{2,1,0:T(8,128)(2,1)} %get-tuple-element.43), channel_id=1, source_target_pairs={{0,31},{1,28},{2,29},{3,30},{4,3},{5,0},{6,1},{7,2},{8,7},{9,4},{1... | collective-permute-start | bytes 27656 | tf_op jit(solution)/shard_map/ppermute | solution.py:1119
  98.8 0.8 slice_bitcast_fusion
  99.6 1.0 slice.27
  101.0 0.7 slice_bitcast_fusion.2
  101.7 1.5 collective-permute-start.1
  103.6 3.8 %collective-permute-start.5 = (bf16[1,36,128]{2,1,0:T(8,128)(2,1)S(1)}, bf16[1,36,128]{2,1,0:T(8,128)(2,1)S(1)}, u32[]{:S(2)}, u32[]{:S(2)}) collective-permute-start(bf16[1,36,128]{2,1,0:T(8,128)(2,1)S(1)} %slice_bitcast_fusion.2), channel_id=1, source_target_pairs={{0,31},{1,28},{2,29},{3,30},{4,3},{5,0},{6,1},{7,2},{8,7},{9,4},{1... | collective-permute-start | bytes 27656 | tf_op jit(solution)/shard_map/ppermute | solution.py:1119
  107.9 0.8 collective-permute-done.5.refs_7_
  108.8 0.8 collective-permute-done.3.refs_5_
  110.3 50.2 %second_layer.1 = (f32[4,32,40,128]{3,2,1,0:T(8,128)}, f32[1280,128]{1,0:T(8,128)}, bf16[32,36,128]{2,1,0:T(8,128)(2,1)}, bf16[4,36,128]{2,1,0:T(8,128)(2,1)}, bf16[1,36,128]{2,1,0:T(8,128)(2,1)}) custom-call(s32[2]{0:T(128)} %add_convert_fusion.flag, f32[4,32,40,128]{3,2,1,0:T(8,128)} %get-tuple-element.40.refs_0_, bf16[32,36,128]{2,1,0:T(8,128)(2,1)} %copy-done.15, ...), custom_call_target="tpu_custom_call" | custom-call | tf_op jit(solution)/shard_map/second_layer/pallas_call | solution.py:623
  160.6 0.7 collective-permute-start.10
  161.8 11.9 %collective-permute-done.11.refs_3_ = bf16[1,36,128]{2,1,0:T(8,128)(2,1)S(1)} collective-permute-done((bf16[1,36,128]{2,1,0:T(8,128)(2,1)}, bf16[1,36,128]{2,1,0:T(8,128)(2,1)S(1)}, u32[]{:S(2)}, u32[]{:S(2)}) %collective-permute-start.11) | collective-permute-done | bytes 9248 | tf_op jit(solution)/shard_map/ppermute | solution.py:1119
  173.9 3.1 %all-to-all-start.1 = ((f32[32,40,128]{2,1,0:T(8,128)}), f32[32,40,128]{2,1,0:T(8,128)S(1)}, u32[]{:S(2)}, u32[]{:S(2)}) async-start(f32[32,40,128]{2,1,0:T(8,128)} %bitcast.55), calls=%async_computation.1 | async-start | bytes 1310720 | tf_op jit(solution)/shard_map/all_to_all | solution.py:1137
  177.0 34.7 %first_layer_back.1 = (f32[4,32,40,128]{3,2,1,0:T(8,128)}, f32[1280,128]{1,0:T(8,128)}) custom-call(f32[4,32,40,128]{3,2,1,0:T(8,128)} %get-tuple-element.45.refs_0_, bf16[32,36,128]{2,1,0:T(8,128)(2,1)} %copy-done.13, bf16[4,36,128]{2,1,0:T(8,128)(2,1)} %copy-done.17, bf16[1,36,128]{2,1,0:T(8,128)(2,1)} %copy-done.25, f32[4,32,40,128]{3,2,1,0:T(8,128)} %bitcast.45, ...), custom_call_target="tpu_custom_call" | custom-call | flops 7864320000 | bytes 16777216 | tf_op jit(solution)/shard_map/first_layer_back/pallas_call | solution.py:749
  211.8 5.6 %all-to-all-start.2 = ((f32[32,40,128]{2,1,0:T(8,128)}), f32[32,40,128]{2,1,0:T(8,128)S(1)}, u32[]{:S(2)}, u32[]{:S(2)}) async-start(f32[32,40,128]{2,1,0:T(8,128)} %bitcast.56), calls=%async_computation.2 | async-start | bytes 1310720 | tf_op jit(solution)/shard_map/all_to_all | solution.py:1137
  217.4 1.7 copy-done.10
  219.2 15.8 %points_back.1 = f32[8,128]{1,0:T(8,128)S(1)} custom-call(s32[8]{0:T(128)S(1)} %copy-done.9, bf16[8,16,2048]{2,1,0:T(8,128)(2,1)S(1)} %copy-done.2, f32[2139,128]{1,0:T(8,128)S(1)} %bitcast.36, f32[5120,128]{1,0:T(8,128)S(1)} %bitcast.43), custom_call_target="tpu_custom_call" | custom-call | flops 26214400000 | bytes 16777216 | tf_op jit(solution)/shard_map/points_back/pallas_call | solution.py:1029
  235.7 35.8 %all_to_all.20.got = bf16[32,96,128]{2,1,0:T(8,128)(2,1)S(1)} all-to-all(bf16[32,96,128]{2,1,0:T(8,128)(2,1)S(1)} %broadcast_in_dim.5), channel_id=1, replica_groups=mesh['tile'=8,'row'=4] {'tile','row'}, dimensions={0} | all-to-all | bytes 1572864 | tf_op jit(solution)/shard_map/all_to_all | solution.py:1137
  271.4 3.7 %update.1 = (f32[1,1]{1,0:T(1,128)}, f32[2139,128]{1,0:T(8,128)}, f32[2139,128]{1,0:T(8,128)}, f32[2139,128]{1,0:T(8,128)}, bf16[2139,128]{1,0:T(8,128)(2,1)}, /*index=5*/f32[8,128]{1,0:T(8,128)S(1)}) custom-call(bf16[32,96,128]{2,1,0:T(8,128)(2,1)S(1)} %all_to_all.20.got, f32[2139,128]{1,0:T(8,128)S(1)} %bitcast.37, f32[2139,128]{1,0:T(8,128)S(1)} %bitcast.38, ...), custom_call_target="tpu_custom_call" | custom-call | tf_op jit(solution)/shard_map/update/pallas_call | solution.py:1098
  (87 shorter events, 7.2 us)
Async XLA Ops:
  0.6 1.0 copy-start.5
  3.9 16.2 %copy-start.12 = (bf16[24,192,128]{2,1,0:T(8,128)(2,1)S(1)}, bf16[24,192,128]{2,1,0:T(8,128)(2,1)}, u32[]{:S(2)}) copy-start(bf16[24,192,128]{2,1,0:T(8,128)(2,1)} %param.14) | copy-start | bytes 3538948
  12.7 23.2 %all-to-all-start = ((bf16[8,16,2048]{2,1,0:T(8,128)(2,1)}), bf16[8,16,2048]{2,1,0:T(8,128)(2,1)S(1)}, u32[]{:S(2)}, u32[]{:S(2)}) async-start(bf16[8,16,2048]{2,1,0:T(8,128)(2,1)} %bin_points.1), calls=%async_computation | async-start | bytes 1048576 | tf_op jit(solution)/shard_map/all_to_all | solution.py:1180
  21.2 6.2 %copy-start.11 = (bf16[4,32,36,128]{3,2,1,0:T(8,128)(2,1)}, bf16[4,32,36,128]{3,2,1,0:T(8,128)(2,1)S(1)}, u32[]{:S(2)}) copy-start(bf16[4,32,36,128]{3,2,1,0:T(8,128)(2,1)S(1)} %copy.30.refs_8_) | copy-start | bytes 3538948
  21.2 7.0 %copy-start.21 = (s32[24,192]{1,0:T(8,128)S(1)}, s32[24,192]{1,0:T(8,128)}, u32[]{:S(2)}) copy-start(s32[24,192]{1,0:T(8,128)} %param.13) | copy-start | bytes 55300
  21.2 79.4 %collective-permute-start.8 = (bf16[1,36,128]{2,1,0:T(8,128)(2,1)S(1)}, bf16[1,36,128]{2,1,0:T(8,128)(2,1)S(1)}, u32[]{:S(2)}, u32[]{:S(2)}) collective-permute-start(bf16[1,36,128]{2,1,0:T(8,128)(2,1)S(1)} %slice_bitcast_fusion.1), channel_id=1, source_target_pairs={{0,31},{1,28},{2,29},{3,30},{4,3},{5,0},{6,1},{7,2},{8,7},{9,4},{1... | collective-permute-start | bytes 27656 | tf_op jit(solution)/shard_map/ppermute | solution.py:1119
  25.9 75.8 %collective-permute-start.7 = (bf16[4,36,128]{2,1,0:T(8,128)(2,1)S(1)}, bf16[4,36,128]{2,1,0:T(8,128)(2,1)S(1)}, u32[]{:S(2)}, u32[]{:S(2)}) collective-permute-start(bf16[4,36,128]{2,1,0:T(8,128)(2,1)S(1)} %bitcast.58), channel_id=1, source_target_pairs={{0,3},{1,0},{2,1},{3,2},{4,7},{5,4},{6,5},{7,6},{8,11},{9,8},{10,9... | collective-permute-start | bytes 110600 | tf_op jit(solution)/shard_map/ppermute | solution.py:1112
  27.6 75.6 %collective-permute-start.6 = (bf16[32,36,128]{2,1,0:T(8,128)(2,1)S(1)}, bf16[32,36,128]{2,1,0:T(8,128)(2,1)S(1)}, u32[]{:S(2)}, u32[]{:S(2)}) collective-permute-start(bf16[32,36,128]{2,1,0:T(8,128)(2,1)S(1)} %copy.27), channel_id=1, source_target_pairs={{0,28},{4,0},{8,4},{12,8},{16,12},{20,16},{24,20},{28,24},{1,29},{... | collective-permute-start | bytes 884744 | tf_op jit(solution)/shard_map/ppermute | solution.py:1112
  81.7 27.0 %collective-permute-start = (bf16[32,36,128]{2,1,0:T(8,128)(2,1)}, bf16[32,36,128]{2,1,0:T(8,128)(2,1)S(1)}, u32[]{:S(2)}, u32[]{:S(2)}) collective-permute-start(bf16[32,36,128]{2,1,0:T(8,128)(2,1)} %get-tuple-element.41), channel_id=1, source_target_pairs={{0,28},{4,0},{8,4},{12,8},{16,12},{20,16},{24,20},{28,24},{1,29},{... | collective-permute-start | bytes 884744 | tf_op jit(solution)/shard_map/ppermute | solution.py:1112
  95.1 8.5 %collective-permute-start.2 = (bf16[1,36,128]{2,1,0:T(8,128)(2,1)}, bf16[1,36,128]{2,1,0:T(8,128)(2,1)S(1)}, u32[]{:S(2)}, u32[]{:S(2)}) collective-permute-start(bf16[1,36,128]{2,1,0:T(8,128)(2,1)} %get-tuple-element.43), channel_id=1, source_target_pairs={{0,31},{1,28},{2,29},{3,30},{4,3},{5,0},{6,1},{7,2},{8,7},{9,4},{1... | collective-permute-start | bytes 27656 | tf_op jit(solution)/shard_map/ppermute | solution.py:1119
  100.6 9.0 %copy-start.22 = (bf16[1,36,128]{2,1,0:T(8,128)(2,1)}, bf16[1,36,128]{2,1,0:T(8,128)(2,1)S(1)}, u32[]{:S(2)}) copy-start(bf16[1,36,128]{2,1,0:T(8,128)(2,1)S(1)} %collective-permute-done.8.refs_11_) | copy-start | bytes 27652
  100.6 9.0 %collective-permute-start.3 = (bf16[32,36,128]{2,1,0:T(8,128)(2,1)S(1)}, bf16[32,36,128]{2,1,0:T(8,128)(2,1)S(1)}, u32[]{:S(2)}, u32[]{:S(2)}) collective-permute-start(bf16[32,36,128]{2,1,0:T(8,128)(2,1)S(1)} %slice.27), channel_id=1, source_target_pairs={{0,28},{4,0},{8,4},{12,8},{16,12},{20,16},{24,20},{28,24},{1,29},{... | collective-permute-start | bytes 884744 | tf_op jit(solution)/shard_map/ppermute | solution.py:1112
  101.7 7.9 %copy-start.18 = (bf16[4,36,128]{2,1,0:T(8,128)(2,1)}, bf16[4,36,128]{2,1,0:T(8,128)(2,1)S(1)}, u32[]{:S(2)}) copy-start(bf16[4,36,128]{2,1,0:T(8,128)(2,1)S(1)} %collective-permute-done.7.refs_10_) | copy-start | bytes 110596
  101.7 7.1 %collective-permute-start.1 = (bf16[4,36,128]{2,1,0:T(8,128)(2,1)}, bf16[4,36,128]{2,1,0:T(8,128)(2,1)S(1)}, u32[]{:S(2)}, u32[]{:S(2)}) collective-permute-start(bf16[4,36,128]{2,1,0:T(8,128)(2,1)} %get-tuple-element.42), channel_id=1, source_target_pairs={{0,3},{1,0},{2,1},{3,2},{4,7},{5,4},{6,5},{7,6},{8,11},{9,8},{10,9... | collective-permute-start | bytes 110600 | tf_op jit(solution)/shard_map/ppermute | solution.py:1112
  103.2 6.4 %copy-start.14 = (bf16[32,36,128]{2,1,0:T(8,128)(2,1)}, bf16[32,36,128]{2,1,0:T(8,128)(2,1)S(1)}, u32[]{:S(2)}) copy-start(bf16[32,36,128]{2,1,0:T(8,128)(2,1)S(1)} %collective-permute-done.6.refs_9_) | copy-start | bytes 884740
  103.2 5.5 %collective-permute-start.4 = (bf16[4,36,128]{2,1,0:T(8,128)(2,1)S(1)}, bf16[4,36,128]{2,1,0:T(8,128)(2,1)S(1)}, u32[]{:S(2)}, u32[]{:S(2)}) collective-permute-start(bf16[4,36,128]{2,1,0:T(8,128)(2,1)S(1)} %slice_bitcast_fusion), channel_id=1, source_target_pairs={{0,3},{1,0},{2,1},{3,2},{4,7},{5,4},{6,5},{7,6},{8,11},{9,8},{10,9... | collective-permute-start | bytes 110600 | tf_op jit(solution)/shard_map/ppermute | solution.py:1112
  103.6 6.0 %copy-start.23 = (bf16[1,36,128]{2,1,0:T(8,128)(2,1)}, bf16[1,36,128]{2,1,0:T(8,128)(2,1)S(1)}, u32[]{:S(2)}) copy-start(bf16[1,36,128]{2,1,0:T(8,128)(2,1)S(1)} %collective-permute-done.2.refs_3_) | copy-start | bytes 27652
  103.6 5.1 %collective-permute-start.5 = (bf16[1,36,128]{2,1,0:T(8,128)(2,1)S(1)}, bf16[1,36,128]{2,1,0:T(8,128)(2,1)S(1)}, u32[]{:S(2)}, u32[]{:S(2)}) collective-permute-start(bf16[1,36,128]{2,1,0:T(8,128)(2,1)S(1)} %slice_bitcast_fusion.2), channel_id=1, source_target_pairs={{0,31},{1,28},{2,29},{3,30},{4,3},{5,0},{6,1},{7,2},{8,7},{9,4},{1... | collective-permute-start | bytes 27656 | tf_op jit(solution)/shard_map/ppermute | solution.py:1119
  160.5 13.4 %collective-permute-start.9 = (bf16[32,36,128]{2,1,0:T(8,128)(2,1)}, bf16[32,36,128]{2,1,0:T(8,128)(2,1)S(1)}, u32[]{:S(2)}, u32[]{:S(2)}) collective-permute-start(bf16[32,36,128]{2,1,0:T(8,128)(2,1)} %get-tuple-element.47), channel_id=1, source_target_pairs={{0,4},{4,8},{8,12},{12,16},{16,20},{20,24},{24,28},{28,0},{1,5},{5... | collective-permute-start | bytes 884744 | tf_op jit(solution)/shard_map/ppermute | solution.py:1112
  160.6 13.1 %collective-permute-start.10 = (bf16[4,36,128]{2,1,0:T(8,128)(2,1)}, bf16[4,36,128]{2,1,0:T(8,128)(2,1)S(1)}, u32[]{:S(2)}, u32[]{:S(2)}) collective-permute-start(bf16[4,36,128]{2,1,0:T(8,128)(2,1)} %get-tuple-element.48), channel_id=1, source_target_pairs={{0,1},{1,2},{2,3},{3,0},{4,5},{5,6},{6,7},{7,4},{8,9},{9,10},{10,1... | collective-permute-start | bytes 110600 | tf_op jit(solution)/shard_map/ppermute | solution.py:1112
  161.3 12.4 %collective-permute-start.11 = (bf16[1,36,128]{2,1,0:T(8,128)(2,1)}, bf16[1,36,128]{2,1,0:T(8,128)(2,1)S(1)}, u32[]{:S(2)}, u32[]{:S(2)}) collective-permute-start(bf16[1,36,128]{2,1,0:T(8,128)(2,1)} %get-tuple-element.49), channel_id=1, source_target_pairs={{0,5},{1,6},{2,7},{3,4},{4,9},{5,10},{6,11},{7,8},{8,13},{9,14},{1... | collective-permute-start | bytes 27656 | tf_op jit(solution)/shard_map/ppermute | solution.py:1119
  173.6 3.4 %copy-start.25 = (bf16[1,36,128]{2,1,0:T(8,128)(2,1)}, bf16[1,36,128]{2,1,0:T(8,128)(2,1)S(1)}, u32[]{:S(2)}) copy-start(bf16[1,36,128]{2,1,0:T(8,128)(2,1)S(1)} %collective-permute-done.11.refs_3_) | copy-start | bytes 27652
  173.7 3.4 %copy-start.17 = (bf16[4,36,128]{2,1,0:T(8,128)(2,1)}, bf16[4,36,128]{2,1,0:T(8,128)(2,1)S(1)}, u32[]{:S(2)}) copy-start(bf16[4,36,128]{2,1,0:T(8,128)(2,1)S(1)} %collective-permute-done.10.refs_2_) | copy-start | bytes 110596
  173.9 3.2 %copy-start.13 = (bf16[32,36,128]{2,1,0:T(8,128)(2,1)}, bf16[32,36,128]{2,1,0:T(8,128)(2,1)S(1)}, u32[]{:S(2)}) copy-start(bf16[32,36,128]{2,1,0:T(8,128)(2,1)S(1)} %collective-permute-done.9.refs_1_) | copy-start | bytes 884740
  173.9 37.9 %all-to-all-start.1 = ((f32[32,40,128]{2,1,0:T(8,128)}), f32[32,40,128]{2,1,0:T(8,128)S(1)}, u32[]{:S(2)}, u32[]{:S(2)}) async-start(f32[32,40,128]{2,1,0:T(8,128)} %bitcast.55), calls=%async_computation.1 | async-start | bytes 1310720 | tf_op jit(solution)/shard_map/all_to_all | solution.py:1137
  211.7 5.7 %copy-start = (f32[273792]{0:T(1024)S(1)}, f32[273792]{0:T(1024)}, u32[]{:S(2)}) copy-start(f32[273792]{0:T(1024)} %param.15) | copy-start | bytes 3285508
  211.7 5.7 %copy-start.2 = (bf16[8,16,2048]{2,1,0:T(8,128)(2,1)S(1)}, bf16[8,16,2048]{2,1,0:T(8,128)(2,1)}, u32[]{:S(2)}) copy-start(bf16[8,16,2048]{2,1,0:T(8,128)(2,1)} %copy-done.1) | copy-start | bytes 1572868
  211.7 5.7 %copy-start.9 = (s32[8]{0:T(128)S(1)}, s32[8]{0:T(128)}, u32[]{:S(2)}) copy-start(s32[8]{0:T(128)} %fusion.held_ref) | copy-start | bytes 100
  211.8 23.6 %all-to-all-start.2 = ((f32[32,40,128]{2,1,0:T(8,128)}), f32[32,40,128]{2,1,0:T(8,128)S(1)}, u32[]{:S(2)}, u32[]{:S(2)}) async-start(f32[32,40,128]{2,1,0:T(8,128)} %bitcast.56), calls=%async_computation.2 | async-start | bytes 1310720 | tf_op jit(solution)/shard_map/all_to_all | solution.py:1137
  217.4 1.7 copy-start.10
  235.4 36.0 %copy-start.3 = (f32[273792]{0:T(1024)S(1)}, f32[273792]{0:T(1024)}, u32[]{:S(2)}) copy-start(f32[273792]{0:T(1024)} %param.16) | copy-start | bytes 3285508
  235.4 36.0 %copy-start.4 = (f32[273792]{0:T(1024)S(1)}, f32[273792]{0:T(1024)}, u32[]{:S(2)}) copy-start(f32[273792]{0:T(1024)} %param.17) | copy-start | bytes 3285508
  (9 other events, 7.2 us)

commit v5 on v4

--- a/solution.py
+++ b/solution.py
@@ -24,6 +24,7 @@
 CHUNK = 512
 LO = 512
 NW = 8
+NF = 4
 
 clip_norm = 0.01
 beta_one = 0.9
@@ -360,7 +361,7 @@
 
 
 def gather_windows(scratch, pick):
-    for i in range(NW):
+    for i in range(scratch.shape[0] // SLOTS):
         for r in range(2):
             for c in range(2):
                 at = i * SLOTS + (2 * r + c) * QC
@@ -370,7 +371,7 @@
 
 def spread_windows(scratch, value, put):
     scratch[...] = value
-    for i in range(NW):
+    for i in range(scratch.shape[0] // SLOTS):
         for r in range(2):
             for c in range(2):
                 put(r, 2 * i + c, scratch[pl.ds(i * SLOTS + (2 * r + c) * QC, QC), :])
@@ -392,7 +393,7 @@
 
 def first_layer(pillars, par, quads_x, quads_y):
     across = quads_x // 2
-    along = quads_y // (2 * NW)
+    along = quads_y // (2 * NF)
     windows = quads_x * quads_y // 4
     base = POINT_ROWS
 
@@ -435,9 +436,9 @@
         pillar = mm(both, pout[...]) + count * par_ref[70:71, :]
         x = pillar / jnp.maximum(count, 1.0)
         onehot = jnp.where((lanes > H1) & (lanes < H1 + 4) & (count > 0.0), cells, 0.0).astype(BF16)
-        groups = [onehot[i * SLOTS : (i + 1) * SLOTS] for i in range(NW)]
+        groups = [onehot[i * SLOTS : (i + 1) * SLOTS] for i in range(NF)]
         k = layer_forward(x, groups, par_ref, base, w, sums)
-        for i in range(NW):
+        for i in range(NF):
             rows = slice(i * SLOTS, (i + 1) * SLOTS)
             for h in range(HEADS + 1):
                 probs_out[i, :, h * D : (h + 1) * D] = k["probs"][i][h]
@@ -455,7 +456,7 @@
 
         @pl.when(a == 0)
         def _():
-            for c in range(2 * NW):
+            for c in range(2 * NF):
                 row_out[c] = field[0, c, :QC, :].astype(BF16)
 
         @pl.when(b == 0)
@@ -472,9 +473,9 @@
             sums_out[...] = sums[...]
 
     def win_spec(width):
-        return pl.BlockSpec((NW, SLOTS, width), lambda s: (s, 0, 0))
-
-    quad_spec = pl.BlockSpec((2, 2 * NW, QP, D), lambda s: (s // along, s % along, 0, 0))
+        return pl.BlockSpec((NF, SLOTS, width), lambda s: (s, 0, 0))
+
+    quad_spec = pl.BlockSpec((2, 2 * NF, QP, D), lambda s: (s // along, s % along, 0, 0))
     shape = jax.ShapeDtypeStruct
     return pl.pallas_call(
         kernel,
@@ -490,7 +491,7 @@
             win_spec(D),
             win_spec(D),
             whole((4, 8, D)),
-            pl.BlockSpec((2 * NW, QC, D), lambda s: (jnp.minimum(s, along - 1), 0, 0)),
+            pl.BlockSpec((2 * NF, QC, D), lambda s: (jnp.minimum(s, along - 1), 0, 0)),
             pl.BlockSpec((2, QC, D), lambda s: (s // along, 0, 0)),
             whole((1, QC, D)),
         ],
@@ -510,16 +511,17 @@
         ],
         scratch_shapes=[pltpu.VMEM(WEIGHT_SHAPES[n], BF16) for n in ["qkv", "out", "fin", "fout"]]
         + [
-            pltpu.VMEM((NW * SLOTS, D), F32),
+            pltpu.VMEM((NF * SLOTS, D), F32),
             pltpu.VMEM((D, D), BF16),
             pltpu.VMEM((4, 8, D), F32),
         ],
         compiler_params=params_for(),
+        cost_estimate=cost_of(pillars.size * 12000),
         name="first_layer",
     )(pillars, par)
 
 
-def second_layer(flags, field, halos, tags, tag_halos, cot, cot_halos, par, scale, grad_rows):
+def second_layer(flags, field, halos, tags, cot, early_halos, par, scale, grad_rows):
     quads_x, quads_y = field.shape[:2]
     across = quads_x // 2
     along = quads_y // (2 * NW)
@@ -528,9 +530,9 @@
     anames = list(ACC_SHAPES)
 
     def kernel(flag, *refs):
-        ins, refs = refs[:13], refs[13:]
+        ins, refs = refs[:10], refs[10:]
         outs, scratch = refs[:5], refs[5:]
-        fields, tagss, cots, par_ref = ins[:4], ins[4:8], ins[8:12], ins[12]
+        fields, (tag_ref, cot_ref), early, par_ref = ins[:4], ins[4:6], ins[6:9], ins[9]
         grads, weights, row_out, col_out, cor_out = outs
         w = dict(zip(wnames, scratch))
         scratch = scratch[len(wnames) :]
@@ -550,8 +552,9 @@
             def moved(v, region):
                 return pltpu.roll(v, 3 * region, axis=1)
 
-            def fill(ext, srcs, turn_row, turn_col, turn_cor):
+            def fill(ext, srcs, first, turn_row, turn_col, turn_cor):
                 main, row, col, cor = srcs
+                rows = slice(first, first + QC)
 
                 def one(i, _):
                     ext[i // quads_y, i % quads_y, :QC, :] = main[
@@ -562,13 +565,13 @@
                 lax.fori_loop(0, quads_x * quads_y, one, 0, unroll=4)
 
                 def one_row(i, _):
-                    ext[quads_x, i, :QC, :] = turn_row(row[i].astype(F32))
+                    ext[quads_x, i, :QC, :] = turn_row(row[i, rows, :].astype(F32))
                     return 0
 
                 lax.fori_loop(1, quads_y, one_row, 0)
                 for i in range(1, quads_x):
-                    ext[i, quads_y, :QC, :] = turn_col(col[i].astype(F32))
-                ext[quads_x, quads_y, :QC, :] = turn_cor(cor[0].astype(F32))
+                    ext[i, quads_y, :QC, :] = turn_col(col[i, rows, :].astype(F32))
+                ext[quads_x, quads_y, :QC, :] = turn_cor(cor[0, rows, :].astype(F32))
 
             def same(v):
                 return v
@@ -582,9 +585,9 @@
             def tag_col(v):
                 return jnp.where(last_y, moved(v, 1), v)
 
-            fill(ext_x, fields, same, same, same)
-            fill(ext_t, tagss, tag_row, tag_col, lambda v: tag_row(tag_col(v)))
-            fill(ext_g, cots, same, same, same)
+            fill(ext_x, fields, 0, same, same, same)
+            fill(ext_g, [cot_ref, *early], 0, same, same, same)
+            fill(ext_t, [tag_ref, *early], QP, tag_row, tag_col, lambda v: tag_row(tag_col(v)))
 
         def picker(ext):
             return lambda r, c: ext[2 * a + 1 + r, 2 * NW * b + 1 + c, :QC, :]
@@ -619,7 +622,7 @@
     shape = jax.ShapeDtypeStruct
     quad_spec = pl.BlockSpec((2, 2 * NW, QP, D), lambda s: (s // along, s % along, 0, 0))
     ext = pltpu.VMEM((quads_x + 1, quads_y + 1, QP, D), F32)
-    arrays = [field, *halos, tags, *tag_halos, cot, *cot_halos, par]
+    arrays = [field, *halos, tags, cot, *early_halos, par]
     return pl.pallas_call(
         kernel,
         grid=(across * along,),
@@ -901,15 +904,17 @@
     lax.fori_loop(0, (count + 1) // 2, pair, 0)
 
 
-def encode_points(recv, held, par, base_rows, quads):
+def encode_points(recv, held, par, base_rows, quads_x, quads_y):
     sources, _, capacity = recv.shape
     chunk = min(CHUNK, capacity)
+    quads = quads_x * quads_y
     groups = -(-quads * QP // LO)
     pairs = -(-groups // 2)
 
     most = capacity // chunk
 
-    def kernel(held_ref, recv_ref, par_ref, base_ref, out_ref, tag_ref, win, acc, todo, *buffers):
+    def kernel(held_ref, recv_ref, par_ref, base_ref, out_ref, tag_ref, col_ref, *refs):
+        win, acc, todo, *buffers = refs
         bias = unpack_point_in(par_ref, win)
         acc[...] = jnp.zeros(acc.shape, F32)
         lanes = lane_iota()
@@ -953,13 +958,19 @@
             return 0
 
         lax.fori_loop(0, quads, finish, 0, unroll=4)
+        for i in range(quads_x):
+            col_ref[i] = tag_ref[i * quads_y]
 
     shape = jax.ShapeDtypeStruct
     return pl.pallas_call(
         kernel,
         in_specs=[pl.BlockSpec(memory_space=pltpu.SMEM)]
         + [pl.BlockSpec(memory_space=pltpu.VMEM)] * 3,
-        out_shape=[shape((quads * QP, D), F32), shape((quads, QC, D), BF16)],
+        out_shape=[
+            shape((quads * QP, D), F32),
+            shape((quads, QC, D), BF16),
+            shape((quads_x, QC, D), BF16),
+        ],
         scratch_shapes=[pltpu.VMEM((16, 3 * D), BF16), pltpu.VMEM((LO, (pairs + 1) * D), F32)]
         + [pltpu.SMEM((sources * most + 1,), jnp.int32)]
         + [pltpu.VMEM((LO, chunk), BF16), pltpu.VMEM((chunk, (pairs + 1) * D), BF16)] * 2,
@@ -1164,7 +1175,6 @@
     par = params.reshape(-1, D)
 
     cot = by_quads(cotangent, quads_x, quads_y)
-    cot_halos = exchange(cot[0], cot[:, 0], cot[0, :1], -1)
 
     shape = (points // BLOCK, BLOCK)
     send = bin_points(
@@ -1184,14 +1194,22 @@
     frames = jnp.pad(frames, ((0, 0), (0, 0), (0, QP - QC)), constant_values=-1).reshape(-1)
     lanes = jnp.arange(D, dtype=jnp.int32)
     base_rows = (frames[:, None] == lanes[None] - (H1 + 1)).astype(F32)
-    pillars, tags = encode_points(recv, held, par, base_rows, quads)
+    pillars, tags, tag_col = encode_points(recv, held, par[:72], base_rows, quads_x, quads_y)
     pillars = pillars.reshape(quads_x, quads_y, QP, D)
     tags = tags.reshape(quads_x, quads_y, QC, D)
-    tag_halos = exchange(tags[0], tags[:, 0], tags[0, :1], -1)
+
+    def edges(cells, groups):
+        gap = jnp.zeros(cells.shape[:-2] + (QP - QC, D), BF16)
+        return jnp.concatenate([cells, gap, groups], axis=1)
+
+    early_halos = exchange(
+        edges(cot[0], tags[0]), edges(cot[:, 0], tag_col), edges(cot[0, :1], tags[0, :1]), -1
+    )
 
     first = first_layer(pillars, par, quads_x, quads_y)
     field, saved, sums_one = first[0], first[1:8], first[8]
-    halos = exchange(*first[9:], -1)
+    early_halos, sides = lax.optimization_barrier((early_halos, first[9:]))
+    halos = exchange(*sides, -1)
     flags = jnp.stack(
         [
             (lax.axis_index("tile") == tile_count - 1).astype(jnp.int32),
@@ -1205,9 +1223,8 @@
         field,
         halos,
         tags,
-        tag_halos,
         cot,
-        cot_halos,
+        early_halos,
         par,
         1.0 / (cell_count * device_count),
         grad_rows,
@@ -1219,7 +1236,7 @@
     )
     grad_one, sum_two = lax.optimization_barrier((grad_one, sum_two))
     sum_one = scatter_sum(grad_one, device_count)
-    grad_pin = points_back(recv, held, par, cell_grads.reshape(quads * QP, D))
+    grad_pin = points_back(recv, held, par[:72], cell_grads.reshape(quads * QP, D))
     share = jnp.concatenate([sum_two, sum_one, grad_pin, jnp.zeros((8, D), F32)], axis=0)
     share = share.astype(BF16)
     total = all_to_all(jnp.broadcast_to(share[None], (device_count,) + share.shape))

time: 273 us -> 269 us (0.985); the launches traced: 276 us -> 268 us
  starting transfers between devices: 46.9 us -> 33.2 us
  Pallas kernels: 158 us -> 168 us
  blocking collectives: 35.8 us -> 31.6 us
    ppermute x8 -> x6, starting transfers between devices: 18.5 us -> 6.44 us  [shifted(): lax.ppermute(x, axes[0], [(i, (i + by) % count) for i in range(count)])]
    all_to_all x1, blocking collectives: 35.8 us -> 31.6 us  [all_to_all(): lax.all_to_all(x, ('tile', 'row'), split_axis=0, concat_axis=0, tiled=True)]
    ppermute x4 -> x3, waiting for transfers between devices: 12.7 us -> 8.7 us  [shifted(): return lax.ppermute(x, axes, pairs)]
    all_to_all x1, waiting for transfers between devices: 3.43 us -> 7.18 us  [local(): recv = lax.all_to_all(send, 'tile', split_axis=0, concat_axis=0, tiled=True)]
    pallas_call x1, Pallas kernels: 15.8 us -> 19.4 us  [points_back(): pl.pallas_call(kernel, in_specs=[pl.BlockSpec(memory_space=pltpu.SMEM)] +...]
    ppermute x4 -> x3, starting transfers between devices: 12.5 us -> 8.94 us  [shifted(): return lax.ppermute(x, axes, pairs)]
    pallas_call x1, Pallas kernels: 23.8 us -> 27 us  [first_layer(): pl.pallas_call(kernel, grid=(across * along,), in_specs=[quad_spec, whole...]
    unnamed x54 -> x50, local copies, waits for them, and re-layouts: 5.82 us -> 6.07 us
  transfers between devices with their start and end apart: 15 -> 12, of which waited for: 6 -> 2; matrix products, arithmetic and copies ran while one was open for 3% -> 4% of each run, Pallas kernels for 35% -> 30%
where the time goes in v5:
time: 269 us; the launch traced here: 268 us
  Pallas kernels  168 us (62%)
  starting transfers between devices  33.2 us (12%)
  blocking collectives  31.6 us (12%)
  waiting for transfers between devices  15.9 us (6%)
  local copies, waits for them, and re-layouts  13.4 us (5%)
  other arithmetic  5.46 us (2%)
    pallas_call x1, Pallas kernels, second_layer(): pl.pallas_call(kernel, grid=(across * along,), in_specs=[pl.BlockSpec(mem...  50.2 us
    pallas_call x1, Pallas kernels, first_layer_back(): pl.pallas_call(kernel, grid=(across * along,), in_specs=[whole(grads.shap...  34.7 us
    all_to_all x1, blocking collectives, all_to_all(): lax.all_to_all(x, ('tile', 'row'), split_axis=0, concat_axis=0, tiled=True)  31.6 us
    pallas_call x1, Pallas kernels, first_layer(): pl.pallas_call(kernel, grid=(across * along,), in_specs=[quad_spec, whole...  27 us
    pallas_call x1, Pallas kernels, encode_points(): pl.pallas_call(kernel, in_specs=[pl.BlockSpec(memory_space=pltpu.SMEM)] +...  23.8 us
    pallas_call x1, Pallas kernels, points_back(): pl.pallas_call(kernel, in_specs=[pl.BlockSpec(memory_space=pltpu.SMEM)] +...  19.4 us
    all_to_all x2, starting transfers between devices, all_to_all(): lax.all_to_all(x, ('tile', 'row'), split_axis=0, concat_axis=0, tiled=True)  10.6 us
    ppermute x3, starting transfers between devices, shifted(): return lax.ppermute(x, axes, pairs)  8.94 us
  transfers between devices with their start and end apart: 12, of which 2 were waited for; matrix products, arithmetic and copies ran while one was open for 4% of the time, Pallas kernels for 30%

profile of v5, /device:TPU:0, one launch (start us, length us, event | category | flops | bytes accessed | tf_op | source)
XLA Modules:
  0.0 268.3 jit_solution(10255913837067065178)
XLA Ops:
  0.6 0.9 copy-done.5
  1.6 0.8 copy-done.7
  2.3 0.8 copy-done.8
  3.1 0.8 copy-done.9
  3.9 8.9 %bin_points.1 = bf16[8,16,2048]{2,1,0:T(8,128)(2,1)} custom-call(bf16[11,8192]{1,0:T(8,128)(2,1)S(1)} %copy-done.5, s32[64,128]{1,0:T(8,128)S(1)} %bitcast.38, s32[64,128]{1,0:T(8,128)S(1)} %bitcast.39, s32[64,128]{1,0:T(8,128)S(1)} %bitcast.40), custom_call_target="tpu_custom_call" | custom-call | tf_op jit(solution)/shard_map/bin_points/pallas_call | solution.py:848
  12.7 7.3 %all-to-all-start = ((bf16[8,16,2048]{2,1,0:T(8,128)(2,1)}), bf16[8,16,2048]{2,1,0:T(8,128)(2,1)S(1)}, u32[]{:S(2)}, u32[]{:S(2)}) async-start(bf16[8,16,2048]{2,1,0:T(8,128)(2,1)} %bin_points.1), calls=%async_computation | async-start | bytes 1048576 | tf_op jit(solution)/shard_map/all_to_all | solution.py:1190
  21.3 1.4 slice_bitcast_fusion.par_ref
  23.9 3.4 %compare_convert_fusion.base_ref = f32[5120,128]{1,0:T(8,128)} fusion(s32[128]{0:T(128)S(1)} %iota_add_fusion, s32[5120]{0:T(1024)S(1)} %eq.23), kind=kLoop, calls=%fused_computation | loop fusion | flops 1310720 | bytes 2642432 | tf_op jit(solution)/shard_map/convert_element_type | solution.py:1196
  27.3 7.2 %all-to-all-done.recv_ref = bf16[8,16,2048]{2,1,0:T(8,128)(2,1)S(1)} async-done(((bf16[8,16,2048]{2,1,0:T(8,128)(2,1)}), bf16[8,16,2048]{2,1,0:T(8,128)(2,1)S(1)}, u32[]{:S(2)}, u32[]{:S(2)}) %all-to-all-start) | async-done | bytes 524320 | tf_op jit(solution)/shard_map/all_to_all | solution.py:1190
  34.5 0.8 fusion.held_ref
  35.3 23.8 %encode_points.1 = (f32[5120,128]{1,0:T(8,128)}, bf16[128,36,128]{2,1,0:T(8,128)(2,1)}, bf16[4,36,128]{2,1,0:T(8,128)(2,1)}) custom-call(s32[8]{0:T(128)} %fusion.held_ref, bf16[8,16,2048]{2,1,0:T(8,128)(2,1)} %copy-done.1, f32[72,128]{1,0:T(8,128)} %slice_bitcast_fusion.par_ref, f32[5120,128]{1,0:T(8,128)} %compare_convert_fusion.base_ref), custom_call_target="tpu_custom_call" | custom-call | tf_op jit(solution)/shard_map/encode_points/pallas_call | solution.py:965
  59.1 1.0 slice.42
  60.1 0.7 slice_bitcast_fusion.1
  61.7 1.2 collective-permute-start.1
  62.9 27.0 %first_layer.1 = (f32[4,32,40,128]{3,2,1,0:T(8,128)}, bf16[32,144,1152]{2,1,0:T(8,128)(2,1)}, bf16[32,144,384]{2,1,0:T(8,128)(2,1)}, bf16[32,144,128]{2,1,0:T(8,...) custom-call(f32[4,32,40,128]{3,2,1,0:T(8,128)} %bitcast.46, ...), custom_call_target="tpu_custom_call" | custom-call | flops 7864320000 | bytes 16777216 | tf_op jit(solution)/shard_map/first_layer/pallas_call | solution.py:480
  90.2 1.8 collective-permute-start.4
  92.0 7.3 %collective-permute-start.5 = (bf16[1,36,128]{2,1,0:T(8,128)(2,1)}, bf16[1,36,128]{2,1,0:T(8,128)(2,1)S(1)}, u32[]{:S(2)}, u32[]{:S(2)}) collective-permute-start(bf16[1,36,128]{2,1,0:T(8,128)(2,1)} %get-tuple-element.55), channel_id=1, source_target_pairs={{0,31},{1,28},{2,29},{3,30},{4,3},{5,0},{6,1},{7,2},{8,7},{9,4},{1... | collective-permute-start | bytes 27656 | tf_op jit(solution)/shard_map/ppermute | solution.py:1130
  99.3 0.7 add_convert_fusion.flag
  100.0 1.1 copy.40.refs_6_
  101.8 50.2 %second_layer.1 = (f32[4,32,40,128]{3,2,1,0:T(8,128)}, f32[1280,128]{1,0:T(8,128)}, bf16[32,36,128]{2,1,0:T(8,128)(2,1)}, bf16[4,36,128]{2,1,0:T(8,128)(2,1)}, bf16[1,36,128]{2,1,0:T(8,128)(2,1)}) custom-call(s32[2]{0:T(128)} %add_convert_fusion.flag, f32[4,32,40,128]{3,2,1,0:T(8,128)} %get-tuple-element.47.refs_0_, bf16[32,36,128]{2,1,0:T(8,128)(2,1)} %copy-done.15, ...), custom_call_target="tpu_custom_call" | custom-call | tf_op jit(solution)/shard_map/second_layer/pallas_call | solution.py:626
  152.0 1.7 collective-permute-start.6
  153.7 1.3 collective-permute-start.7
  155.0 1.6 collective-permute-start.8
  156.7 8.7 %collective-permute-done.8.refs_3_ = bf16[1,36,128]{2,1,0:T(8,128)(2,1)S(1)} collective-permute-done((bf16[1,36,128]{2,1,0:T(8,128)(2,1)}, bf16[1,36,128]{2,1,0:T(8,128)(2,1)S(1)}, u32[]{:S(2)}, u32[]{:S(2)}) %collective-permute-start.8) | collective-permute-done | bytes 9248 | tf_op jit(solution)/shard_map/ppermute | solution.py:1130
  165.4 4.9 %all-to-all-start.1 = ((f32[32,40,128]{2,1,0:T(8,128)}), f32[32,40,128]{2,1,0:T(8,128)S(1)}, u32[]{:S(2)}, u32[]{:S(2)}) async-start(f32[32,40,128]{2,1,0:T(8,128)} %bitcast.52), calls=%async_computation.1 | async-start | bytes 1310720 | tf_op jit(solution)/shard_map/all_to_all | solution.py:1148
  170.4 34.7 %first_layer_back.1 = (f32[4,32,40,128]{3,2,1,0:T(8,128)}, f32[1280,128]{1,0:T(8,128)}) custom-call(f32[4,32,40,128]{3,2,1,0:T(8,128)} %get-tuple-element.59.refs_0_, bf16[32,36,128]{2,1,0:T(8,128)(2,1)} %copy-done.14, bf16[4,36,128]{2,1,0:T(8,128)(2,1)} %copy-done.17, bf16[1,36,128]{2,1,0:T(8,128)(2,1)} %copy-done.23, f32[4,32,40,128]{3,2,1,0:T(8,128)} %bitcast.47, ...), custom_call_target="tpu_custom_call" | custom-call | flops 7864320000 | bytes 16777216 | tf_op jit(solution)/shard_map/first_layer_back/pallas_call | solution.py:752
  205.2 5.6 %all-to-all-start.2 = ((f32[32,40,128]{2,1,0:T(8,128)}), f32[32,40,128]{2,1,0:T(8,128)S(1)}, u32[]{:S(2)}, u32[]{:S(2)}) async-start(f32[32,40,128]{2,1,0:T(8,128)} %bitcast.53), calls=%async_computation.2 | async-start | bytes 1310720 | tf_op jit(solution)/shard_map/all_to_all | solution.py:1148
  210.9 1.7 copy-done.11
  212.6 19.4 %points_back.1 = f32[8,128]{1,0:T(8,128)S(1)} custom-call(s32[8]{0:T(128)S(1)} %copy-done.10, bf16[8,16,2048]{2,1,0:T(8,128)(2,1)S(1)} %copy-done.2, f32[72,128]{1,0:T(8,128)S(1)} %copy-done.6, f32[5120,128]{1,0:T(8,128)S(1)} %bitcast.41), custom_call_target="tpu_custom_call" | custom-call | flops 26214400000 | bytes 16777216 | tf_op jit(solution)/shard_map/points_back/pallas_call | solution.py:1040
  232.4 31.6 %all_to_all.20.got = bf16[32,96,128]{2,1,0:T(8,128)(2,1)S(1)} all-to-all(bf16[32,96,128]{2,1,0:T(8,128)(2,1)S(1)} %broadcast_in_dim.23), channel_id=1, replica_groups=mesh['tile'=8,'row'=4] {'tile','row'}, dimensions={0} | all-to-all | bytes 1572864 | tf_op jit(solution)/shard_map/all_to_all | solution.py:1148
  263.9 3.7 %update.1 = (f32[1,1]{1,0:T(1,128)}, f32[2139,128]{1,0:T(8,128)}, f32[2139,128]{1,0:T(8,128)}, f32[2139,128]{1,0:T(8,128)}, bf16[2139,128]{1,0:T(8,128)(2,1)}, /*index=5*/f32[8,128]{1,0:T(8,128)S(1)}) custom-call(bf16[32,96,128]{2,1,0:T(8,128)(2,1)S(1)} %all_to_all.20.got, f32[2139,128]{1,0:T(8,128)S(1)} %bitcast.35, f32[2139,128]{1,0:T(8,128)S(1)} %bitcast.36, ...), custom_call_target="tpu_custom_call" | custom-call | tf_op jit(solution)/shard_map/update/pallas_call | solution.py:1109
  267.6 0.6 slice_reduce_fusion
  (84 shorter events, 4.7 us)
Async XLA Ops:
  0.6 1.0 copy-start.5
  1.6 0.8 copy-start.7
  2.3 0.8 copy-start.8
  3.9 16.2 %copy-start.13 = (bf16[24,192,128]{2,1,0:T(8,128)(2,1)S(1)}, bf16[24,192,128]{2,1,0:T(8,128)(2,1)}, u32[]{:S(2)}) copy-start(bf16[24,192,128]{2,1,0:T(8,128)(2,1)} %param.14) | copy-start | bytes 3538948
  12.7 21.8 %all-to-all-start = ((bf16[8,16,2048]{2,1,0:T(8,128)(2,1)}), bf16[8,16,2048]{2,1,0:T(8,128)(2,1)S(1)}, u32[]{:S(2)}, u32[]{:S(2)}) async-start(bf16[8,16,2048]{2,1,0:T(8,128)(2,1)} %bin_points.1), calls=%async_computation | async-start | bytes 1048576 | tf_op jit(solution)/shard_map/all_to_all | solution.py:1190
  20.8 2.0 copy-start.20
  21.3 2.5 copy-start.12
  34.5 0.8 copy-start.1
  60.8 0.8 copy-start.18
  60.9 28.9 %collective-permute-start.2 = (bf16[1,76,128]{2,1,0:T(8,128)(2,1)S(1)}, bf16[1,76,128]{2,1,0:T(8,128)(2,1)S(1)}, u32[]{:S(2)}, u32[]{:S(2)}) collective-permute-start(bf16[1,76,128]{2,1,0:T(8,128)(2,1)S(1)} %pad_maximum_fusion.2), channel_id=1, source_target_pairs={{0,31},{1,28},{2,29},{3,30},{4,3},{5,0},{6,1},{7,2},{8,7},{9,4},{1... | collective-permute-start | bytes 58376 | tf_op jit(solution)/shard_map/ppermute | solution.py:1130
  61.3 28.6 %collective-permute-start = (bf16[32,76,128]{2,0,1:T(8,128)(2,1)S(1)}, bf16[32,76,128]{2,0,1:T(8,128)(2,1)S(1)}, u32[]{:S(2)}, u32[]{:S(2)}) collective-permute-start(bf16[32,76,128]{2,0,1:T(8,128)(2,1)S(1)} %copy.35), channel_id=1, source_target_pairs={{0,28},{4,0},{8,4},{12,8},{16,12},{20,16},{24,20},{28,24},{1,29},{... | collective-permute-start | bytes 1867784 | tf_op jit(solution)/shard_map/ppermute | solution.py:1123
  61.7 28.2 %collective-permute-start.1 = (bf16[4,76,128]{2,1,0:T(8,128)(2,1)S(1)}, bf16[4,76,128]{2,1,0:T(8,128)(2,1)S(1)}, u32[]{:S(2)}, u32[]{:S(2)}) collective-permute-start(bf16[4,76,128]{2,1,0:T(8,128)(2,1)S(1)} %pad_maximum_fusion.1), channel_id=1, source_target_pairs={{0,3},{1,0},{2,1},{3,2},{4,7},{5,4},{6,5},{7,6},{8,11},{9,8},{10,9... | collective-permute-start | bytes 233480 | tf_op jit(solution)/shard_map/ppermute | solution.py:1123
  89.8 11.3 %copy-start.21 = (bf16[1,76,128]{2,1,0:T(8,128)(2,1)}, bf16[1,76,128]{2,1,0:T(8,128)(2,1)S(1)}, u32[]{:S(2)}) copy-start(bf16[1,76,128]{2,1,0:T(8,128)(2,1)S(1)} %collective-permute-done.2.refs_8_) | copy-start | bytes 58372
  89.9 11.3 %copy-start.16 = (bf16[4,76,128]{2,1,0:T(8,128)(2,1)}, bf16[4,76,128]{2,1,0:T(8,128)(2,1)S(1)}, u32[]{:S(2)}) copy-start(bf16[4,76,128]{2,1,0:T(8,128)(2,1)S(1)} %collective-permute-done.1.refs_7_) | copy-start | bytes 233476
  89.9 11.2 %collective-permute-start.3 = (bf16[32,36,128]{2,1,0:T(8,128)(2,1)}, bf16[32,36,128]{2,1,0:T(8,128)(2,1)S(1)}, u32[]{:S(2)}, u32[]{:S(2)}) collective-permute-start(bf16[32,36,128]{2,1,0:T(8,128)(2,1)} %get-tuple-element.53), channel_id=1, source_target_pairs={{0,28},{4,0},{8,4},{12,8},{16,12},{20,16},{24,20},{28,24},{1,29},{... | collective-permute-start | bytes 884744 | tf_op jit(solution)/shard_map/ppermute | solution.py:1123
  90.2 10.9 %collective-permute-start.4 = (bf16[4,36,128]{2,1,0:T(8,128)(2,1)}, bf16[4,36,128]{2,1,0:T(8,128)(2,1)S(1)}, u32[]{:S(2)}, u32[]{:S(2)}) collective-permute-start(bf16[4,36,128]{2,1,0:T(8,128)(2,1)} %get-tuple-element.54), channel_id=1, source_target_pairs={{0,3},{1,0},{2,1},{3,2},{4,7},{5,4},{6,5},{7,6},{8,11},{9,8},{10,9... | collective-permute-start | bytes 110600 | tf_op jit(solution)/shard_map/ppermute | solution.py:1123
  92.0 9.0 %collective-permute-start.5 = (bf16[1,36,128]{2,1,0:T(8,128)(2,1)}, bf16[1,36,128]{2,1,0:T(8,128)(2,1)S(1)}, u32[]{:S(2)}, u32[]{:S(2)}) collective-permute-start(bf16[1,36,128]{2,1,0:T(8,128)(2,1)} %get-tuple-element.55), channel_id=1, source_target_pairs={{0,31},{1,28},{2,29},{3,30},{4,3},{5,0},{6,1},{7,2},{8,7},{9,4},{1... | collective-permute-start | bytes 27656 | tf_op jit(solution)/shard_map/ppermute | solution.py:1130
  152.0 13.4 %collective-permute-start.6 = (bf16[32,36,128]{2,1,0:T(8,128)(2,1)}, bf16[32,36,128]{2,1,0:T(8,128)(2,1)S(1)}, u32[]{:S(2)}, u32[]{:S(2)}) collective-permute-start(bf16[32,36,128]{2,1,0:T(8,128)(2,1)} %get-tuple-element.61), channel_id=1, source_target_pairs={{0,4},{4,8},{8,12},{12,16},{16,20},{20,24},{24,28},{28,0},{1,5},{5... | collective-permute-start | bytes 884744 | tf_op jit(solution)/shard_map/ppermute | solution.py:1123
  153.7 11.7 %collective-permute-start.7 = (bf16[4,36,128]{2,1,0:T(8,128)(2,1)}, bf16[4,36,128]{2,1,0:T(8,128)(2,1)S(1)}, u32[]{:S(2)}, u32[]{:S(2)}) collective-permute-start(bf16[4,36,128]{2,1,0:T(8,128)(2,1)} %get-tuple-element.62), channel_id=1, source_target_pairs={{0,1},{1,2},{2,3},{3,0},{4,5},{5,6},{6,7},{7,4},{8,9},{9,10},{10,1... | collective-permute-start | bytes 110600 | tf_op jit(solution)/shard_map/ppermute | solution.py:1123
  155.0 10.3 %collective-permute-start.8 = (bf16[1,36,128]{2,1,0:T(8,128)(2,1)}, bf16[1,36,128]{2,1,0:T(8,128)(2,1)S(1)}, u32[]{:S(2)}, u32[]{:S(2)}) collective-permute-start(bf16[1,36,128]{2,1,0:T(8,128)(2,1)} %get-tuple-element.63), channel_id=1, source_target_pairs={{0,5},{1,6},{2,7},{3,4},{4,9},{5,10},{6,11},{7,8},{8,13},{9,14},{1... | collective-permute-start | bytes 27656 | tf_op jit(solution)/shard_map/ppermute | solution.py:1130
  165.4 5.1 %copy-start.23 = (bf16[1,36,128]{2,1,0:T(8,128)(2,1)}, bf16[1,36,128]{2,1,0:T(8,128)(2,1)S(1)}, u32[]{:S(2)}) copy-start(bf16[1,36,128]{2,1,0:T(8,128)(2,1)S(1)} %collective-permute-done.8.refs_3_) | copy-start | bytes 27652
  165.4 5.1 %copy-start.17 = (bf16[4,36,128]{2,1,0:T(8,128)(2,1)}, bf16[4,36,128]{2,1,0:T(8,128)(2,1)S(1)}, u32[]{:S(2)}) copy-start(bf16[4,36,128]{2,1,0:T(8,128)(2,1)S(1)} %collective-permute-done.7.refs_2_) | copy-start | bytes 110596
  165.4 5.1 %copy-start.14 = (bf16[32,36,128]{2,1,0:T(8,128)(2,1)}, bf16[32,36,128]{2,1,0:T(8,128)(2,1)S(1)}, u32[]{:S(2)}) copy-start(bf16[32,36,128]{2,1,0:T(8,128)(2,1)S(1)} %collective-permute-done.6.refs_1_) | copy-start | bytes 884740
  165.4 39.8 %all-to-all-start.1 = ((f32[32,40,128]{2,1,0:T(8,128)}), f32[32,40,128]{2,1,0:T(8,128)S(1)}, u32[]{:S(2)}, u32[]{:S(2)}) async-start(f32[32,40,128]{2,1,0:T(8,128)} %bitcast.52), calls=%async_computation.1 | async-start | bytes 1310720 | tf_op jit(solution)/shard_map/all_to_all | solution.py:1148
  205.1 5.7 %copy-start.2 = (bf16[8,16,2048]{2,1,0:T(8,128)(2,1)S(1)}, bf16[8,16,2048]{2,1,0:T(8,128)(2,1)}, u32[]{:S(2)}) copy-start(bf16[8,16,2048]{2,1,0:T(8,128)(2,1)} %copy-done.1) | copy-start | bytes 1572868
  205.1 5.7 %copy-start.6 = (f32[72,128]{1,0:T(8,128)S(1)}, f32[72,128]{1,0:T(8,128)}, u32[]{:S(2)}) copy-start(f32[72,128]{1,0:T(8,128)} %slice_bitcast_fusion.par_ref) | copy-start | bytes 110596
  205.2 5.7 %copy-start.10 = (s32[8]{0:T(128)S(1)}, s32[8]{0:T(128)}, u32[]{:S(2)}) copy-start(s32[8]{0:T(128)} %fusion.held_ref) | copy-start | bytes 100
  205.2 26.8 %all-to-all-start.2 = ((f32[32,40,128]{2,1,0:T(8,128)}), f32[32,40,128]{2,1,0:T(8,128)S(1)}, u32[]{:S(2)}, u32[]{:S(2)}) async-start(f32[32,40,128]{2,1,0:T(8,128)} %bitcast.53), calls=%async_computation.2 | async-start | bytes 1310720 | tf_op jit(solution)/shard_map/all_to_all | solution.py:1148
  210.9 1.7 copy-start.11
  212.6 51.3 %copy-start.4 = (f32[273792]{0:T(1024)S(1)}, f32[273792]{0:T(1024)}, u32[]{:S(2)}) copy-start(f32[273792]{0:T(1024)} %param.17) | copy-start | bytes 3285508
  232.1 31.8 %copy-start = (f32[273792]{0:T(1024)S(1)}, f32[273792]{0:T(1024)}, u32[]{:S(2)}) copy-start(f32[273792]{0:T(1024)} %param.15) | copy-start | bytes 3285508
  232.1 31.8 %copy-start.3 = (f32[273792]{0:T(1024)S(1)}, f32[273792]{0:T(1024)}, u32[]{:S(2)}) copy-start(f32[273792]{0:T(1024)} %param.16) | copy-start | bytes 3285508
  (4 other events, 2.7 us)
